TPU v7x, 256 devices: a whole 4x4x8 slice. The times are simulated.
256 devices in a mesh: dp: 2 (over z_lo), expert: 128 (over y, x, z_hi, core).
Axes of the slice: x: 4, y: 4, z: 8 (z_hi: 4, z_lo: 2; z = z_hi * 2 + z_lo), core: 2. Of those that a mesh axis runs over, the one named last changes fastest.
Arguments:
- tokens: bfloat16 [32768, 4096], P(('dp', 'expert')), may hold values from -6 to 6
- routes: int32 [256, 16, 4], P(('dp', 'expert')), may hold values from 0 to 127, as said below
- gate_values: float32 [256, 16, 4], P(('dp', 'expert')), may hold values from 0.1 to 1
- gate_weight: bfloat16 [128, 4096, 256], P('expert', 'dp'), may hold values from -0.09375 to 0.09375
- up_weight: bfloat16 [128, 4096, 256], P('expert', 'dp'), may hold values from -0.09375 to 0.09375
- down_weight: bfloat16 [128, 4096, 256], P('expert', 'dp'), may hold values from -0.125 to 0.125
- cotangent: bfloat16 [32768, 4096], P(('dp', 'expert')), may hold values from -6 to 6
Outputs:
- layer_out: bfloat16 [32768, 4096], P(('dp', 'expert'))
- token_grad: bfloat16 [32768, 4096], P(('dp', 'expert'))
- gate_grad: bfloat16 [128, 4096, 256], P('expert', 'dp')
- up_grad: bfloat16 [128, 4096, 256], P('expert', 'dp')
- down_grad: bfloat16 [128, 4096, 256], P('expert', 'dp')
Inputs may be any that keep to these rules, and one draw needn't show every extreme that they name: `routes`: for each home block and each expert, 4 distinct positions within that block.
All inputs are finite; a program needn't handle non-finite values.
Results may differ from a plain program's by a relative error of at most 0.025.
Values may be sent and summed in bfloat16 or wider, within the bound.
A program may use at most 128 MiB of HBM per device.

v0:
```python
import jax
import jax.numpy as jnp
from jax import lax
from jax.sharding import PartitionSpec as P

SPLIT = 8


def send_out(payload):
    expert_count, slot_count, width = payload.shape
    widened = jnp.repeat(payload, SPLIT, axis=0)
    received = lax.all_to_all(widened, "expert", split_axis=0, concat_axis=0, tiled=True)
    return received.reshape(-1, width)


def bring_back(partial_value, expert_count):
    total_rows, width = partial_value.shape
    home_count = lax.axis_size("expert")
    returned = lax.all_to_all(
        partial_value.reshape(home_count, -1, width),
        "expert",
        split_axis=0,
        concat_axis=0,
        tiled=True,
    )
    slot_count = returned.shape[1]
    returned = returned.reshape(expert_count, SPLIT, slot_count, width)
    return jnp.sum(returned.astype(jnp.float32), axis=1)


def shards(tokens, routes, gate_values, gate_weight, up_weight, down_weight, cotangent):
    width = tokens.shape[1]
    expert_count = routes.shape[1]
    chosen = routes[0]
    scales = gate_values[0][:, :, None]
    contract_last = (((1,), (1,)), ((), ()))
    contract_first = (((0,), (0,)), ((), ()))
    full_gate, full_up, full_down = (
        lax.all_gather(gate_weight, "dp", axis=1, tiled=True),
        lax.all_gather(up_weight, "dp", axis=1, tiled=True),
        lax.all_gather(down_weight, "dp", axis=1, tiled=True),
    )
    full_gate = full_gate[0]
    full_up = full_up[0]
    full_down = full_down[0]
    token_rows = send_out(tokens[chosen])
    gate_pre = jnp.dot(token_rows, full_gate, preferred_element_type=jnp.float32)
    up_pre = jnp.dot(token_rows, full_up, preferred_element_type=jnp.float32)
    gate_sigma = jax.nn.sigmoid(gate_pre)
    hidden = (gate_pre * gate_sigma * up_pre).astype(jnp.bfloat16)
    partial_value = lax.dot_general(
        hidden, full_down, contract_last, preferred_element_type=jnp.float32
    ).astype(jnp.bfloat16)
    combined = bring_back(partial_value, expert_count)
    layer_out = jnp.zeros((tokens.shape[0], width), jnp.float32).at[chosen].add(scales * combined)
    scaled_cot = (scales * cotangent[chosen].astype(jnp.float32)).astype(jnp.bfloat16)
    cot_rows = send_out(scaled_cot)
    hidden_grad = jnp.dot(cot_rows, full_down, preferred_element_type=jnp.float32)
    gate_rows = (hidden_grad * up_pre * gate_sigma * (1.0 + gate_pre * (1.0 - gate_sigma))).astype(
        jnp.bfloat16
    )
    up_rows = (hidden_grad * gate_pre * gate_sigma).astype(jnp.bfloat16)
    partial_grad = (
        lax.dot_general(gate_rows, full_gate, contract_last, preferred_element_type=jnp.float32)
        + lax.dot_general(up_rows, full_up, contract_last, preferred_element_type=jnp.float32)
    ).astype(jnp.bfloat16)
    token_grad = (
        jnp.zeros((tokens.shape[0], width), jnp.float32)
        .at[chosen]
        .add(bring_back(partial_grad, expert_count))
    )
    grad_sums = lax.psum_scatter(
        jnp.concatenate(
            [
                lax.dot_general(
                    token_rows, gate_rows, contract_first, preferred_element_type=jnp.float32
                ),
                lax.dot_general(
                    token_rows, up_rows, contract_first, preferred_element_type=jnp.float32
                ),
                lax.dot_general(
                    cot_rows, hidden, contract_first, preferred_element_type=jnp.float32
                ),
            ],
            axis=1,
        ).astype(jnp.bfloat16),
        "dp",
        scatter_dimension=0,
        tiled=True,
    ).astype(jnp.float32)
    hidden_width = hidden.shape[1]
    gate_grad = grad_sums[:, :hidden_width].astype(jnp.bfloat16)[None]
    up_grad = grad_sums[:, hidden_width : 2 * hidden_width].astype(jnp.bfloat16)[None]
    down_grad = grad_sums[:, 2 * hidden_width :].astype(jnp.bfloat16)[None]
    return (
        layer_out.astype(jnp.bfloat16),
        token_grad.astype(jnp.bfloat16),
        gate_grad,
        up_grad,
        down_grad,
    )


def solution(mesh):
    placed = (
        P(("dp", "expert"), None),
        P(("dp", "expert"), None, None),
        P(("dp", "expert"), None, None),
        P("expert", "dp", None),
        P("expert", "dp", None),
        P("expert", "dp", None),
        P(("dp", "expert"), None),
    )
    return jax.shard_map(
        shards,
        mesh=mesh,
        in_specs=placed,
        out_specs=(
            P(("dp", "expert"), None),
            P(("dp", "expert"), None),
            P("expert", "dp", None),
            P("expert", "dp", None),
            P("expert", "dp", None),
        ),
        check_vma=False,
    )
```

profile of v0, /device:TPU:32, one launch (start us, length us, event | category | flops | bytes accessed | tf_op | source)
XLA Modules:
  0.0 628.8 jit_solution(435772273276211079)
XLA Ops:
  7.2 0.0 copy-start
  7.2 0.8 compare_select_fusion
  8.0 0.1 copy.17
  8.0 0.1 reshape.89
  8.1 0.8 copy.18
  8.9 0.0 copy-done
  8.9 0.9 gather_fusion.1
  9.8 0.3 reshape.107
  10.1 0.3 multiply_convert_fusion
  10.4 4.0 broadcast_in_dim.20
  14.4 15.6 %all-to-all-start.2 = ((bf16[128,4,4096]{2,1,0:T(4,128)(2,1)}), bf16[128,4,4096]{2,1,0:T(4,128)(2,1)}, u32[]{:S(2)}, u32[]{:S(2)}) async-start(bf16[128,4,4096]{2,1,0:T(4,128)(2,1)} %bitcast.49), calls=%async_computation.2 | async-start | bytes 8388608 | tf_op jit(solution)/shard_map/all_to_all | solution.py:12
  30.0 0.0 copy-done.2
  30.0 0.9 gather_fusion
  30.9 0.2 reshape.72
  31.1 97.3 %all-to-all-done.2 = bf16[128,4,4096]{2,1,0:T(4,128)(2,1)} async-done(((bf16[128,4,4096]{2,1,0:T(4,128)(2,1)}), bf16[128,4,4096]{2,1,0:T(4,128)(2,1)}, u32[]{:S(2)}, u32[]{:S(2)}) %all-to-all-start.2) | async-done | bytes 4194336 | tf_op jit(solution)/shard_map/all_to_all | solution.py:12
  128.4 4.0 broadcast_in_dim.19
  132.4 7.4 %all-to-all-start = ((bf16[128,4,4096]{2,1,0:T(4,128)(2,1)}), bf16[128,4,4096]{2,1,0:T(4,128)(2,1)}, u32[]{:S(2)}, u32[]{:S(2)}) async-start(bf16[128,4,4096]{2,1,0:T(4,128)(2,1)} %bitcast.48), calls=%async_computation | async-start | bytes 8388608 | tf_op jit(solution)/shard_map/all_to_all | solution.py:12
  139.8 0.0 all-gather.6.cloned.1.call-start
  139.9 0.7 all-gather.6.cloned.1.call-update
  140.6 0.0 all-gather.4.cloned.1.call-start
  140.6 0.7 all-gather.4.cloned.1.call-update
  141.3 0.5 all-gather.8.cloned.1.call-start
  141.8 0.2 all-gather.8.cloned.1.call-update
  142.1 6.9 %reshape.67 = bf16[512,4096]{1,0:T(8,128)(2,1)} reshape(bf16[128,4,4096]{2,1,0:T(4,128)(2,1)} %all-to-all-done.2) | data formatting | bytes 8388608 | tf_op jit(solution)/shard_map/reshape | solution.py:13
  149.0 112.8 %all-to-all-done = bf16[128,4,4096]{2,1,0:T(4,128)(2,1)} async-done(((bf16[128,4,4096]{2,1,0:T(4,128)(2,1)}), bf16[128,4,4096]{2,1,0:T(4,128)(2,1)}, u32[]{:S(2)}, u32[]{:S(2)}) %all-to-all-start) | async-done | bytes 4194336 | tf_op jit(solution)/shard_map/all_to_all | solution.py:12
  261.7 6.9 %reshape.64 = bf16[512,4096]{1,0:T(8,128)(2,1)} reshape(bf16[128,4,4096]{2,1,0:T(4,128)(2,1)} %all-to-all-done) | data formatting | bytes 8388608 | tf_op jit(solution)/shard_map/reshape | solution.py:13
  268.7 4.1 fusion.4
  272.8 4.9 all-gather.4.cloned.1.call-done
  277.7 4.1 fusion.8
  281.8 36.0 %all-gather.8.cloned.1.call-done = bf16[1,4096,256]{2,1,0:T(8,128)(2,1)} async-done(((bf16[1,2048,256]{2,1,0:T(8,128)(2,1)}), bf16[1,4096,256]{2,1,0:T(8,128)(2,1)}) %all-gather.8.cloned.1.call-update) | async-done | bytes 2097168 | tf_op jit(solution)/shard_map/all_gather | solution.py:41
  317.8 4.4 multiply_convert_fusion.1
  322.2 0.0 copy-done.6
  322.2 3.3 convolution_convert_fusion
  325.4 7.2 %reshape.65 = bf16[128,4,4096]{2,1,0:T(4,128)(2,1)} reshape(bf16[512,4096]{1,0:T(8,128)(2,1)} %convolution_convert_fusion) | data formatting | bytes 8388608 | tf_op jit(solution)/shard_map/reshape | solution.py:20
  332.6 14.9 %all-to-all-start.1 = ((bf16[128,4,4096]{2,1,0:T(4,128)(2,1)}), bf16[128,4,4096]{2,1,0:T(4,128)(2,1)}, u32[]{:S(2)}, u32[]{:S(2)}) async-start(bf16[128,4,4096]{2,1,0:T(4,128)(2,1)} %reshape.65), calls=%async_computation.1 | async-start | bytes 8388608 | tf_op jit(solution)/shard_map/all_to_all | solution.py:19
  347.5 0.2 reduce-scatter.2.cloned.1.call-start
  347.7 0.0 copy-start.3
  347.7 3.6 convolution_convert_fusion.1
  351.4 1.4 convolution_convert_fusion.2
  352.7 1.4 convolution_convert_fusion.3
  354.1 9.4 %pad_maximum_fusion = bf16[4096,768]{0,1:T(8,128)(2,1)} fusion(bf16[4096,256]{0,1:T(8,128)(2,1)S(1)} %convolution_convert_fusion.1, bf16[4096,256]{0,1:T(8,128)(2,1)S(1)} %convolution_convert_fusion.2, bf16[4096,256]{0,1:T(8,128)(2,1)S(1)} %convolution_convert_fusion.3), kind=kLoop, calls=%fused_computation.7 | loop fusion | flops 18874368 | bytes 12582912 | tf_op jit(solution)/shard_map/concatenate | solution.py:73
  363.5 0.0 reduce-scatter.2.cloned.1.call-update
  363.5 1.6 copy-done.5
  365.1 1.3 fusion.6
  366.4 0.3 copy-done.4
  366.7 3.3 add_convert_fusion
  370.0 7.3 %reshape.68 = bf16[128,4,4096]{2,1,0:T(4,128)(2,1)} reshape(bf16[512,4096]{1,0:T(8,128)(2,1)} %add_convert_fusion) | data formatting | bytes 8388608 | tf_op jit(solution)/shard_map/reshape | solution.py:20
  377.3 102.2 %all-to-all-done.1 = bf16[128,4,4096]{2,1,0:T(4,128)(2,1)} async-done(((bf16[128,4,4096]{2,1,0:T(4,128)(2,1)}), bf16[128,4,4096]{2,1,0:T(4,128)(2,1)}, u32[]{:S(2)}, u32[]{:S(2)}) %all-to-all-start.1) | async-done | bytes 4194336 | tf_op jit(solution)/shard_map/all_to_all | solution.py:19
  479.5 7.6 %all-to-all-start.3 = ((bf16[128,4,4096]{2,1,0:T(4,128)(2,1)}), bf16[128,4,4096]{2,1,0:T(4,128)(2,1)}, u32[]{:S(2)}, u32[]{:S(2)}) async-start(bf16[128,4,4096]{2,1,0:T(4,128)(2,1)} %reshape.68), calls=%async_computation.3 | async-start | bytes 8388608 | tf_op jit(solution)/shard_map/all_to_all | solution.py:19
  487.1 4.7 convert_reduce_fusion.1
  491.8 0.3 broadcast_multiply_fusion
  492.1 0.4 reshape.91
  492.4 2.4 scatter_custom_fusion
  494.9 1.1 convert_element_type.48
  496.0 107.8 %all-to-all-done.3 = bf16[128,4,4096]{2,1,0:T(4,128)(2,1)} async-done(((bf16[128,4,4096]{2,1,0:T(4,128)(2,1)}), bf16[128,4,4096]{2,1,0:T(4,128)(2,1)}, u32[]{:S(2)}, u32[]{:S(2)}) %all-to-all-start.3) | async-done | bytes 4194336 | tf_op jit(solution)/shard_map/all_to_all | solution.py:19
  603.7 4.7 convert_reduce_fusion
  608.4 1.3 reshape.99
  609.7 3.1 scatter_custom_fusion.1
  612.8 1.1 convert_element_type.56
  614.0 3.2 slice_bitcast_fusion
  617.2 2.3 copy.21
  619.4 1.3 copy.20
  620.7 1.3 copy.19
  622.0 0.0 copy-done.1
  (9 shorter events, 0.0 us)
Async XLA Ops:
  7.2 1.7 copy-start
  14.4 15.6 %copy-start.2 = (bf16[128,4096]{1,0:T(8,128)(2,1)S(1)}, bf16[128,4096]{1,0:T(8,128)(2,1)}, u32[]{:S(2)}) copy-start(bf16[128,4096]{1,0:T(8,128)(2,1)} %param.7) | copy-start | bytes 3145732
  14.4 114.0 %all-to-all-start.2 = ((bf16[128,4,4096]{2,1,0:T(4,128)(2,1)}), bf16[128,4,4096]{2,1,0:T(4,128)(2,1)}, u32[]{:S(2)}, u32[]{:S(2)}) async-start(bf16[128,4,4096]{2,1,0:T(4,128)(2,1)} %bitcast.49), calls=%async_computation.2 | async-start | bytes 8388608 | tf_op jit(solution)/shard_map/all_to_all | solution.py:12
  132.4 129.3 %all-to-all-start = ((bf16[128,4,4096]{2,1,0:T(4,128)(2,1)}), bf16[128,4,4096]{2,1,0:T(4,128)(2,1)}, u32[]{:S(2)}, u32[]{:S(2)}) async-start(bf16[128,4,4096]{2,1,0:T(4,128)(2,1)} %bitcast.48), calls=%async_computation | async-start | bytes 8388608 | tf_op jit(solution)/shard_map/all_to_all | solution.py:12
  139.8 128.8 %all-gather.6.cloned.1.call-start = ((), (), s32[]{:S(2)}) async-start(), calls=%async_computation.6 | async-start | bytes 3145728 | tf_op jit(solution)/shard_map/all_gather | solution.py:40
  140.6 137.1 %all-gather.4.cloned.1.call-start = ((), (), s32[]{:S(2)}) async-start(), calls=%async_computation.5 | async-start | bytes 3145728 | tf_op jit(solution)/shard_map/all_gather | solution.py:39
  141.3 176.4 %all-gather.8.cloned.1.call-start = ((), (), s32[]{:S(2)}) async-start(), calls=%async_computation.7 | async-start | bytes 3145728 | tf_op jit(solution)/shard_map/all_gather | solution.py:41
  317.8 4.4 copy-start.6
  332.6 146.9 %all-to-all-start.1 = ((bf16[128,4,4096]{2,1,0:T(4,128)(2,1)}), bf16[128,4,4096]{2,1,0:T(4,128)(2,1)}, u32[]{:S(2)}, u32[]{:S(2)}) async-start(bf16[128,4,4096]{2,1,0:T(4,128)(2,1)} %reshape.65), calls=%async_computation.1 | async-start | bytes 8388608 | tf_op jit(solution)/shard_map/all_to_all | solution.py:19
  347.5 266.4 %reduce-scatter.2.cloned.1.call-start = ((), (), s32[]{:S(2)}) async-start(), calls=%async_computation.8 | async-start | bytes 9437184 | tf_op jit(solution)/shard_map/reduce_scatter | solution.py:72
  347.7 3.7 copy-start.3
  363.5 1.6 copy-start.5
  365.1 1.6 copy-start.4
  479.5 124.2 %all-to-all-start.3 = ((bf16[128,4,4096]{2,1,0:T(4,128)(2,1)}), bf16[128,4,4096]{2,1,0:T(4,128)(2,1)}, u32[]{:S(2)}, u32[]{:S(2)}) async-start(bf16[128,4,4096]{2,1,0:T(4,128)(2,1)} %reshape.68), calls=%async_computation.3 | async-start | bytes 8388608 | tf_op jit(solution)/shard_map/all_to_all | solution.py:19
  614.0 8.1 %copy-start.1 = (bf16[128,4096]{1,0:T(8,128)(2,1)S(1)}, bf16[128,4096]{1,0:T(8,128)(2,1)}, u32[]{:S(2)}) copy-start(bf16[128,4096]{1,0:T(8,128)(2,1)} %param.13) | copy-start | bytes 3145732
Sparse Core Ops, SparseCore 0:
  142.5 93.1 all-gather.5
  237.5 40.1 all-gather.3
  279.5 38.2 all-gather.7
  363.7 199.7 reduce-scatter.1
where the time goes:
time: 637 us; the launch traced here: 629 us
  waiting for transfers between devices  462 us (73%)
  local copies, waits for them, and re-layouts  51.2 us (8%)
  starting transfers between devices  46.2 us (7%)
  other arithmetic  27.8 us (4%)
  matrix products  26.8 us (4%)
  between operations  14.2 us (2%)
    all_to_all x2, waiting for transfers between devices, send_out(): lax.all_to_all(widened, 'expert', split_axis=0, concat_axis=0, tiled=True)  210 us
    all_to_all x2, waiting for transfers between devices, bring_back(): lax.all_to_all(partial_value.reshape(home_count, -1, width), 'expert', sp...  210 us
    all_gather x1, waiting for transfers between devices, shards(): lax.all_gather(down_weight, 'dp', axis=1, tiled=True)  36 us
    all_to_all x2, starting transfers between devices, send_out(): lax.all_to_all(widened, 'expert', split_axis=0, concat_axis=0, tiled=True)  22.9 us
    all_to_all x2, starting transfers between devices, bring_back(): lax.all_to_all(partial_value.reshape(home_count, -1, width), 'expert', sp...  22.5 us
    reshape x2, local copies, waits for them, and re-layouts, bring_back(): partial_value.reshape(home_count, -1, width)  14.5 us
    reshape x2, local copies, waits for them, and re-layouts, send_out(): return received.reshape(-1, width)  13.8 us
  transfers between devices with their start and end apart: 8, of which 6 were waited for; matrix products, arithmetic and copies ran while one was open for 11% of the time, Pallas kernels for 0%

commit v1 on v0

--- a/solution.py
+++ b/solution.py
@@ -1,31 +1,25 @@
 import jax
 import jax.numpy as jnp
 from jax import lax
+from jax.sharding import Mesh
 from jax.sharding import PartitionSpec as P
 
 SPLIT = 8
+ROWS = ("dp", "yx", "col")
 
 
 def send_out(payload):
-    expert_count, slot_count, width = payload.shape
-    widened = jnp.repeat(payload, SPLIT, axis=0)
-    received = lax.all_to_all(widened, "expert", split_axis=0, concat_axis=0, tiled=True)
-    return received.reshape(-1, width)
+    arrived = lax.all_to_all(payload, "yx", split_axis=0, concat_axis=0, tiled=True)
+    shared = lax.all_gather(arrived, "col", axis=0, tiled=True)
+    return shared.reshape(-1, payload.shape[-1])
 
 
 def bring_back(partial_value, expert_count):
     total_rows, width = partial_value.shape
-    home_count = lax.axis_size("expert")
-    returned = lax.all_to_all(
-        partial_value.reshape(home_count, -1, width),
-        "expert",
-        split_axis=0,
-        concat_axis=0,
-        tiled=True,
-    )
-    slot_count = returned.shape[1]
-    returned = returned.reshape(expert_count, SPLIT, slot_count, width)
-    return jnp.sum(returned.astype(jnp.float32), axis=1)
+    summed = lax.psum_scatter(partial_value, "col", scatter_dimension=0, tiled=True)
+    summed = summed.reshape(expert_count, -1, width)
+    returned = lax.all_to_all(summed, "yx", split_axis=0, concat_axis=0, tiled=True)
+    return returned.astype(jnp.float32)
 
 
 def shards(tokens, routes, gate_values, gate_weight, up_weight, down_weight, cotangent):
@@ -44,6 +38,8 @@
     full_up = full_up[0]
     full_down = full_down[0]
     token_rows = send_out(tokens[chosen])
+    scaled_cot = (scales * cotangent[chosen].astype(jnp.float32)).astype(jnp.bfloat16)
+    cot_rows = send_out(scaled_cot)
     gate_pre = jnp.dot(token_rows, full_gate, preferred_element_type=jnp.float32)
     up_pre = jnp.dot(token_rows, full_up, preferred_element_type=jnp.float32)
     gate_sigma = jax.nn.sigmoid(gate_pre)
@@ -53,8 +49,6 @@
     ).astype(jnp.bfloat16)
     combined = bring_back(partial_value, expert_count)
     layer_out = jnp.zeros((tokens.shape[0], width), jnp.float32).at[chosen].add(scales * combined)
-    scaled_cot = (scales * cotangent[chosen].astype(jnp.float32)).astype(jnp.bfloat16)
-    cot_rows = send_out(scaled_cot)
     hidden_grad = jnp.dot(cot_rows, full_down, preferred_element_type=jnp.float32)
     gate_rows = (hidden_grad * up_pre * gate_sigma * (1.0 + gate_pre * (1.0 - gate_sigma))).astype(
         jnp.bfloat16
@@ -102,25 +96,27 @@
 
 
 def solution(mesh):
+    n_dp, n_expert = mesh.devices.shape
+    fine = Mesh(mesh.devices.reshape(n_dp, n_expert // SPLIT, SPLIT), ROWS)
     placed = (
-        P(("dp", "expert"), None),
-        P(("dp", "expert"), None, None),
-        P(("dp", "expert"), None, None),
-        P("expert", "dp", None),
-        P("expert", "dp", None),
-        P("expert", "dp", None),
-        P(("dp", "expert"), None),
+        P(ROWS, None),
+        P(ROWS, None, None),
+        P(ROWS, None, None),
+        P(("yx", "col"), "dp", None),
+        P(("yx", "col"), "dp", None),
+        P(("yx", "col"), "dp", None),
+        P(ROWS, None),
     )
     return jax.shard_map(
         shards,
-        mesh=mesh,
+        mesh=fine,
         in_specs=placed,
         out_specs=(
-            P(("dp", "expert"), None),
-            P(("dp", "expert"), None),
-            P("expert", "dp", None),
-            P("expert", "dp", None),
-            P("expert", "dp", None),
+            P(ROWS, None),
+            P(ROWS, None),
+            P(("yx", "col"), "dp", None),
+            P(("yx", "col"), "dp", None),
+            P(("yx", "col"), "dp", None),
         ),
         check_vma=False,
     )

time: 637 us -> 487 us (0.76)
  waiting for transfers between devices: 462 us -> 345 us
  starting transfers between devices: 46.2 us -> 13.2 us
  blocking collectives: 0 us -> 32.3 us
  local copies, waits for them, and re-layouts: 51.2 us -> 32.9 us
  other arithmetic: 27.8 us -> 18.5 us
    all_to_all x4 -> x2, waiting for transfers between devices: 420 us -> 4.35 us  [bring_back(): lax.all_to_all(summed, 'yx', split_axis=0, concat_axis=0, tiled=True)]
    reduce_scatter x0 -> x2, waiting for transfers between devices: none -> 92.3 us  [bring_back(): lax.psum_scatter(partial_value, 'col', scatter_dimension=0, tiled=True)]
    all_gather x0 -> x2, waiting for transfers between devices: none -> 79.7 us  [send_out(): shared = lax.all_gather(arrived, 'col', axis=0, tiled=True)]
    reduce_scatter x1, waiting for transfers between devices: 0.01 us -> 63.4 us  [shards(): lax.psum_scatter(jnp.concatenate([lax.dot_general(token_rows, gate_rows,...]
    all_to_all x4 -> x2, starting transfers between devices: 45.4 us -> 12.7 us  [bring_back(): lax.all_to_all(summed, 'yx', split_axis=0, concat_axis=0, tiled=True)]
    all_to_all x0 -> x2, blocking collectives: none -> 32.3 us  [send_out(): lax.all_to_all(payload, 'yx', split_axis=0, concat_axis=0, tiled=True)]
    all_gather x1, waiting for transfers between devices: 4.87 us -> 36.2 us  [shards(): lax.all_gather(gate_weight, 'dp', axis=1, tiled=True)]
    all_gather x1, waiting for transfers between devices: 0.01 us -> 31 us  [shards(): lax.all_gather(up_weight, 'dp', axis=1, tiled=True)]
  transfers between devices with their start and end apart: 8 -> 10, of which waited for: 6 -> 9; matrix products, arithmetic and copies ran while one was open for 11% -> 12% of each run, Pallas kernels for 0% -> 0%
where the time goes in v1:
time: 487 us; the launch traced here: 483 us
  waiting for transfers between devices  345 us (71%)
  local copies, waits for them, and re-layouts  32.9 us (7%)
  blocking collectives  32.3 us (7%)
  matrix products  26.9 us (6%)
  other arithmetic  18.5 us (4%)
  between operations  14.3 us (3%)
  starting transfers between devices  13.2 us (3%)
    reduce_scatter x2, waiting for transfers between devices, bring_back(): lax.psum_scatter(partial_value, 'col', scatter_dimension=0, tiled=True)  92.3 us
    all_gather x2, waiting for transfers between devices, send_out(): shared = lax.all_gather(arrived, 'col', axis=0, tiled=True)  79.7 us
    reduce_scatter x1, waiting for transfers between devices, shards(): lax.psum_scatter(jnp.concatenate([lax.dot_general(token_rows, gate_rows,...  63.4 us
    all_gather x1, waiting for transfers between devices, shards(): lax.all_gather(gate_weight, 'dp', axis=1, tiled=True)  36.2 us
    all_gather x1, waiting for transfers between devices, shards(): lax.all_gather(down_weight, 'dp', axis=1, tiled=True)  36.2 us
    all_to_all x2, blocking collectives, send_out(): lax.all_to_all(payload, 'yx', split_axis=0, concat_axis=0, tiled=True)  32.3 us
    all_gather x1, waiting for transfers between devices, shards(): lax.all_gather(up_weight, 'dp', axis=1, tiled=True)  31 us
    reshape x2, local copies, waits for them, and re-layouts, send_out(): return shared.reshape(-1, payload.shape[-1])  13.8 us
  transfers between devices with their start and end apart: 10, of which 9 were waited for; matrix products, arithmetic and copies ran while one was open for 12% of the time, Pallas kernels for 0%

profile of v1, /device:TPU:32, one launch (start us, length us, event | category | flops | bytes accessed | tf_op | source)
XLA Modules:
  0.0 483.2 jit_solution(14935874238161383922)
XLA Ops:
  7.2 0.0 all-gather.6.cloned.1.call-start
  7.2 0.8 compare_select_fusion
  8.1 0.1 copy.22
  8.2 0.1 reshape.73
  8.3 0.2 copy-done
  8.4 0.9 gather_fusion
  9.3 0.2 reshape.56
  9.5 18.5 %all_to_all.20 = bf16[16,4,4096]{2,1,0:T(4,128)(2,1)} all-to-all(bf16[16,4,4096]{2,1,0:T(4,128)(2,1)S(1)} %reshape.56), channel_id=1, replica_groups=mesh['dp'=2,'yx'=16,'col'=8] {'yx'}, dimensions={0} | all-to-all | bytes 1048576 | tf_op jit(solution)/shard_map/all_to_all | solution.py:12
  28.0 0.0 all-gather.6.cloned.1.call-update
  28.0 0.0 all-gather.14.cloned.1.call-start
  28.0 0.1 copy.23
  28.1 0.9 gather_fusion.1
  29.0 0.3 reshape.91
  29.3 0.3 multiply_convert_fusion
  29.6 13.8 %all_to_all.21 = bf16[16,4,4096]{2,1,0:T(4,128)(2,1)} all-to-all(bf16[16,4,4096]{2,1,0:T(4,128)(2,1)S(1)} %multiply_convert_fusion), channel_id=1, replica_groups=mesh['dp'=2,'yx'=16,'col'=8] {'yx'}, dimensions={0} | all-to-all | bytes 1048576 | tf_op jit(solution)/shard_map/all_to_all | solution.py:12
  43.5 0.0 all-gather.14.cloned.1.call-update
  43.5 0.0 all-gather.10.cloned.1.call-start
  43.5 0.7 all-gather.10.cloned.1.call-update
  44.2 0.0 all-gather.8.cloned.1.call-start
  44.3 0.5 all-gather.8.cloned.1.call-update
  44.8 0.0 all-gather.12.cloned.1.call-start
  44.8 0.5 all-gather.12.cloned.1.call-update
  45.4 0.0 reduce-scatter.4.cloned.1.call-start
  45.4 33.5 %all-gather.6.cloned.1.call-done = bf16[128,4,4096]{2,1,0:T(4,128)(2,1)} async-done(((bf16[16,4,4096]{2,1,0:T(4,128)(2,1)}), bf16[128,4,4096]{2,1,0:T(4,128)(2,1)}) %all-gather.6.cloned.1.call-update) | async-done | bytes 4194320 | tf_op jit(solution)/shard_map/all_gather | solution.py:13
  78.9 6.9 %reshape.51 = bf16[512,4096]{1,0:T(8,128)(2,1)} reshape(bf16[128,4,4096]{2,1,0:T(4,128)(2,1)} %all-gather.6.cloned.1.call-done) | data formatting | bytes 8388608 | tf_op jit(solution)/shard_map/reshape | solution.py:14
  85.8 46.2 %all-gather.14.cloned.1.call-done = bf16[128,4,4096]{2,1,0:T(4,128)(2,1)} async-done(((bf16[16,4,4096]{2,1,0:T(4,128)(2,1)}), bf16[128,4,4096]{2,1,0:T(4,128)(2,1)}) %all-gather.14.cloned.1.call-update) | async-done | bytes 4194320 | tf_op jit(solution)/shard_map/all_gather | solution.py:13
  132.0 7.0 %reshape.53 = bf16[512,4096]{1,0:T(8,128)(2,1)} reshape(bf16[128,4,4096]{2,1,0:T(4,128)(2,1)} %all-gather.14.cloned.1.call-done) | data formatting | bytes 8388608 | tf_op jit(solution)/shard_map/reshape | solution.py:14
  138.9 31.0 %all-gather.10.cloned.1.call-done = bf16[1,4096,256]{2,1,0:T(8,128)(2,1)} async-done(((bf16[1,2048,256]{2,1,0:T(8,128)(2,1)}), bf16[1,4096,256]{2,1,0:T(8,128)(2,1)}) %all-gather.10.cloned.1.call-update) | async-done | bytes 2097168 | tf_op jit(solution)/shard_map/all_gather | solution.py:34
  169.9 4.1 fusion.4
  174.0 36.2 %all-gather.8.cloned.1.call-done = bf16[1,4096,256]{2,1,0:T(8,128)(2,1)} async-done(((bf16[1,2048,256]{2,1,0:T(8,128)(2,1)}), bf16[1,4096,256]{2,1,0:T(8,128)(2,1)}) %all-gather.8.cloned.1.call-update) | async-done | bytes 2097168 | tf_op jit(solution)/shard_map/all_gather | solution.py:33
  210.3 4.1 fusion.8
  214.4 36.2 %all-gather.12.cloned.1.call-done = bf16[1,4096,256]{2,1,0:T(8,128)(2,1)} async-done(((bf16[1,2048,256]{2,1,0:T(8,128)(2,1)}), bf16[1,4096,256]{2,1,0:T(8,128)(2,1)}) %all-gather.12.cloned.1.call-update) | async-done | bytes 2097168 | tf_op jit(solution)/shard_map/all_gather | solution.py:35
  250.6 4.4 multiply_convert_fusion.1
  255.0 3.4 convolution_convert_fusion
  258.4 0.0 reduce-scatter.4.cloned.1.call-update
  258.4 0.0 reduce-scatter.6.cloned.1.call-start
  258.4 1.5 copy-done.5
  260.0 1.3 fusion.6
  261.3 0.3 copy-done.4
  261.6 3.3 add_convert_fusion
  264.9 0.2 reduce-scatter.8.cloned.1.call-start
  265.1 3.6 convolution_convert_fusion.1
  268.7 1.4 convolution_convert_fusion.2
  270.1 1.4 convolution_convert_fusion.3
  271.5 9.4 %pad_maximum_fusion = bf16[4096,768]{0,1:T(8,128)(2,1)} fusion(bf16[4096,256]{0,1:T(8,128)(2,1)S(1)} %convolution_convert_fusion.1, bf16[4096,256]{0,1:T(8,128)(2,1)S(1)} %convolution_convert_fusion.2, bf16[4096,256]{0,1:T(8,128)(2,1)S(1)} %convolution_convert_fusion.3), kind=kLoop, calls=%fused_computation.5 | loop fusion | flops 18874368 | bytes 12582912 | tf_op jit(solution)/shard_map/concatenate | solution.py:67
  280.9 36.9 %reduce-scatter.4.cloned.1.call-done = bf16[64,4096]{1,0:T(8,128)(2,1)} async-done(((bf16[512,4096]{1,0:T(8,128)(2,1)}), bf16[64,4096]{1,0:T(8,128)(2,1)}) %reduce-scatter.4.cloned.1.call-update) | async-done | bytes 524304 | tf_op jit(solution)/shard_map/reduce_scatter | solution.py:19
  317.8 2.0 reshape.52
  319.8 6.6 %all-to-all-start.1 = ((bf16[16,4,4096]{2,1,0:T(4,128)(2,1)}), bf16[16,4,4096]{2,1,0:T(4,128)(2,1)S(1)}, u32[]{:S(2)}, u32[]{:S(2)}) async-start(bf16[16,4,4096]{2,1,0:T(4,128)(2,1)} %reshape.52), calls=%async_computation.2 | async-start | bytes 1048576 | tf_op jit(solution)/shard_map/all_to_all | solution.py:21
  326.4 55.5 %reduce-scatter.6.cloned.1.call-done = bf16[64,4096]{1,0:T(8,128)(2,1)} async-done(((bf16[512,4096]{1,0:T(8,128)(2,1)}), bf16[64,4096]{1,0:T(8,128)(2,1)}) %reduce-scatter.6.cloned.1.call-update) | async-done | bytes 524304 | tf_op jit(solution)/shard_map/reduce_scatter | solution.py:19
  381.9 2.0 reshape.54
  383.9 6.1 %all-to-all-start.3 = ((bf16[16,4,4096]{2,1,0:T(4,128)(2,1)}), bf16[16,4,4096]{2,1,0:T(4,128)(2,1)}, u32[]{:S(2)}, u32[]{:S(2)}) async-start(bf16[16,4,4096]{2,1,0:T(4,128)(2,1)} %reshape.54), calls=%async_computation.5 | async-start | bytes 1048576 | tf_op jit(solution)/shard_map/all_to_all | solution.py:21
  390.0 0.3 convert_multiply_fusion
  390.3 1.3 reshape.75
  391.6 3.1 scatter_custom_fusion
  394.8 1.1 convert_element_type.41
  395.9 4.3 all-to-all-done.3
  400.2 1.1 reshape.83
  401.3 2.4 scatter_custom_fusion.1
  403.7 1.1 convert_element_type.48
  404.8 63.4 %reduce-scatter.8.cloned.1.call-done = bf16[2048,768]{0,1:T(8,128)(2,1)} async-done(((bf16[4096,768]{0,1:T(8,128)(2,1)}), bf16[2048,768]{0,1:T(8,128)(2,1)}) %reduce-scatter.8.cloned.1.call-update) | async-done | bytes 3145744 | tf_op jit(solution)/shard_map/reduce_scatter | solution.py:66
  468.3 3.2 slice_bitcast_fusion
  471.5 2.3 copy.26
  473.7 1.3 copy.25
  475.0 1.3 copy.24
  (17 shorter events, 0.1 us)
Async XLA Ops:
  7.2 1.2 copy-start
  7.2 20.9 %copy-start.7 = (f32[1,16,4]{1,2,0:T(4,128)S(1)}, f32[1,16,4]{1,2,0:T(4,128)}, u32[]{:S(2)}) copy-start(f32[1,16,4]{1,2,0:T(4,128)} %param.9) | copy-start | bytes 772
  7.2 20.9 %copy-start.2 = (bf16[128,4096]{1,0:T(8,128)(2,1)S(1)}, bf16[128,4096]{1,0:T(8,128)(2,1)}, u32[]{:S(2)}) copy-start(bf16[128,4096]{1,0:T(8,128)(2,1)} %param.13) | copy-start | bytes 3145732
  7.2 71.7 %all-gather.6.cloned.1.call-start = ((), (), s32[]{:S(2)}) async-start(), calls=%async_computation.7 | async-start | bytes 4718592 | tf_op jit(solution)/shard_map/all_gather | solution.py:13
  28.0 104.0 %all-gather.14.cloned.1.call-start = ((), (), s32[]{:S(2)}) async-start(), calls=%async_computation.12 | async-start | bytes 4718592 | tf_op jit(solution)/shard_map/all_gather | solution.py:13
  43.5 126.4 %all-gather.10.cloned.1.call-start = ((), (), s32[]{:S(2)}) async-start(), calls=%async_computation.9 | async-start | bytes 3145728 | tf_op jit(solution)/shard_map/all_gather | solution.py:34
  44.2 166.0 %all-gather.8.cloned.1.call-start = ((), (), s32[]{:S(2)}) async-start(), calls=%async_computation.8 | async-start | bytes 3145728 | tf_op jit(solution)/shard_map/all_gather | solution.py:33
  44.8 205.8 %all-gather.12.cloned.1.call-start = ((), (), s32[]{:S(2)}) async-start(), calls=%async_computation.10 | async-start | bytes 3145728 | tf_op jit(solution)/shard_map/all_gather | solution.py:35
  45.4 272.4 %reduce-scatter.4.cloned.1.call-start = ((), (), s32[]{:S(2)}) async-start(), calls=%async_computation.11 | async-start | bytes 4718592 | tf_op jit(solution)/shard_map/reduce_scatter | solution.py:19
  250.6 4.4 copy-start.6
  258.4 1.6 copy-start.5
  258.4 123.5 %reduce-scatter.6.cloned.1.call-start = ((), (), s32[]{:S(2)}) async-start(), calls=%async_computation.13 | async-start | bytes 4718592 | tf_op jit(solution)/shard_map/reduce_scatter | solution.py:19
  260.0 1.6 copy-start.4
  264.9 203.4 %reduce-scatter.8.cloned.1.call-start = ((), (), s32[]{:S(2)}) async-start(), calls=%async_computation.14 | async-start | bytes 9437184 | tf_op jit(solution)/shard_map/reduce_scatter | solution.py:66
  265.1 3.7 copy-start.3
  319.8 64.1 %all-to-all-start.1 = ((bf16[16,4,4096]{2,1,0:T(4,128)(2,1)}), bf16[16,4,4096]{2,1,0:T(4,128)(2,1)S(1)}, u32[]{:S(2)}, u32[]{:S(2)}) async-start(bf16[16,4,4096]{2,1,0:T(4,128)(2,1)} %reshape.52), calls=%async_computation.2 | async-start | bytes 1048576 | tf_op jit(solution)/shard_map/all_to_all | solution.py:21
  383.9 16.3 %all-to-all-start.3 = ((bf16[16,4,4096]{2,1,0:T(4,128)(2,1)}), bf16[16,4,4096]{2,1,0:T(4,128)(2,1)}, u32[]{:S(2)}, u32[]{:S(2)}) async-start(bf16[16,4,4096]{2,1,0:T(4,128)(2,1)} %reshape.54), calls=%async_computation.5 | async-start | bytes 1048576 | tf_op jit(solution)/shard_map/all_to_all | solution.py:21
  468.3 8.1 %copy-start.1 = (bf16[128,4096]{1,0:T(8,128)(2,1)S(1)}, bf16[128,4096]{1,0:T(8,128)(2,1)}, u32[]{:S(2)}) copy-start(bf16[128,4096]{1,0:T(8,128)(2,1)} %param.7) | copy-start | bytes 3145732
Sparse Core Ops, SparseCore 0:
  28.1 50.7 all-gather.5
  80.7 51.1 all-gather.13
  133.8 36.0 all-gather.9
  171.6 38.6 all-gather.7
  211.9 38.6 all-gather.11
  258.5 59.1 reduce-scatter.3
  320.3 61.5 reduce-scatter.5
  384.4 83.7 reduce-scatter.7

commit v2 on v1

--- a/solution.py
+++ b/solution.py
@@ -9,16 +9,16 @@
 
 
 def send_out(payload):
-    arrived = lax.all_to_all(payload, "yx", split_axis=0, concat_axis=0, tiled=True)
-    shared = lax.all_gather(arrived, "col", axis=0, tiled=True)
-    return shared.reshape(-1, payload.shape[-1])
+    arrived = lax.all_to_all(payload, "yx", split_axis=1, concat_axis=1, tiled=True)
+    shared = lax.all_gather(arrived, "col", axis=1, tiled=True)
+    return shared.reshape(payload.shape[0], -1, payload.shape[-1])
 
 
 def bring_back(partial_value, expert_count):
-    total_rows, width = partial_value.shape
-    summed = lax.psum_scatter(partial_value, "col", scatter_dimension=0, tiled=True)
-    summed = summed.reshape(expert_count, -1, width)
-    returned = lax.all_to_all(summed, "yx", split_axis=0, concat_axis=0, tiled=True)
+    streams, total_rows, width = partial_value.shape
+    summed = lax.psum_scatter(partial_value, "col", scatter_dimension=1, tiled=True)
+    summed = summed.reshape(streams, expert_count, -1, width)
+    returned = lax.all_to_all(summed, "yx", split_axis=1, concat_axis=1, tiled=True)
     return returned.astype(jnp.float32)
 
 
@@ -29,17 +29,12 @@
     scales = gate_values[0][:, :, None]
     contract_last = (((1,), (1,)), ((), ()))
     contract_first = (((0,), (0,)), ((), ()))
-    full_gate, full_up, full_down = (
-        lax.all_gather(gate_weight, "dp", axis=1, tiled=True),
-        lax.all_gather(up_weight, "dp", axis=1, tiled=True),
-        lax.all_gather(down_weight, "dp", axis=1, tiled=True),
-    )
-    full_gate = full_gate[0]
-    full_up = full_up[0]
-    full_down = full_down[0]
-    token_rows = send_out(tokens[chosen])
+    weights = jnp.concatenate([gate_weight, up_weight, down_weight], axis=0)
+    full = lax.all_gather(weights, "dp", axis=1, tiled=True)
+    full_gate, full_up, full_down = full[0], full[1], full[2]
     scaled_cot = (scales * cotangent[chosen].astype(jnp.float32)).astype(jnp.bfloat16)
-    cot_rows = send_out(scaled_cot)
+    both_rows = send_out(jnp.stack([tokens[chosen], scaled_cot]))
+    token_rows, cot_rows = both_rows[0], both_rows[1]
     gate_pre = jnp.dot(token_rows, full_gate, preferred_element_type=jnp.float32)
     up_pre = jnp.dot(token_rows, full_up, preferred_element_type=jnp.float32)
     gate_sigma = jax.nn.sigmoid(gate_pre)
@@ -47,8 +42,6 @@
     partial_value = lax.dot_general(
         hidden, full_down, contract_last, preferred_element_type=jnp.float32
     ).astype(jnp.bfloat16)
-    combined = bring_back(partial_value, expert_count)
-    layer_out = jnp.zeros((tokens.shape[0], width), jnp.float32).at[chosen].add(scales * combined)
     hidden_grad = jnp.dot(cot_rows, full_down, preferred_element_type=jnp.float32)
     gate_rows = (hidden_grad * up_pre * gate_sigma * (1.0 + gate_pre * (1.0 - gate_sigma))).astype(
         jnp.bfloat16
@@ -58,11 +51,9 @@
         lax.dot_general(gate_rows, full_gate, contract_last, preferred_element_type=jnp.float32)
         + lax.dot_general(up_rows, full_up, contract_last, preferred_element_type=jnp.float32)
     ).astype(jnp.bfloat16)
-    token_grad = (
-        jnp.zeros((tokens.shape[0], width), jnp.float32)
-        .at[chosen]
-        .add(bring_back(partial_grad, expert_count))
-    )
+    back = bring_back(jnp.stack([partial_value, partial_grad]), expert_count)
+    layer_out = jnp.zeros((tokens.shape[0], width), jnp.float32).at[chosen].add(scales * back[0])
+    token_grad = jnp.zeros((tokens.shape[0], width), jnp.float32).at[chosen].add(back[1])
     grad_sums = lax.psum_scatter(
         jnp.concatenate(
             [

time: 487 us -> 442 us (0.908)
  waiting for transfers between devices: 345 us -> 296 us
  other arithmetic: 18.5 us -> 31.9 us
  local copies, waits for them, and re-layouts: 32.9 us -> 41.1 us
  blocking collectives: 32.3 us -> 24.1 us
  matrix products: 26.9 us -> 21.5 us
    all_gather x5 -> x2, waiting for transfers between devices: 183 us -> 142 us  [the longest x1 82 us: send_out(): shared = lax.all_gather(arrived, 'col', axis=1, tiled=True)]
    squeeze x0 -> x3, local copies, waits for them, and re-layouts: none -> 15.6 us  [the longest x2 14.2 us: shards(): token_rows, cot_rows = (both_rows[0], both_rows[1])]
    reshape x4 -> x2, local copies, waits for them, and re-layouts: 17.9 us -> 3.06 us  [bring_back(): summed = summed.reshape(streams, expert_count, -1, width)]
    reduce_scatter x2 -> x1, waiting for transfers between devices: 92.3 us -> 80.6 us  [bring_back(): lax.psum_scatter(partial_value, 'col', scatter_dimension=1, tiled=True)]
    slice x0 -> x2, local copies, waits for them, and re-layouts: none -> 10.2 us  [the longest x1 10.1 us: shards(): token_rows, cot_rows = (both_rows[0], both_rows[1])]
    reduce_scatter x1, waiting for transfers between devices: 63.4 us -> 72.6 us  [shards(): lax.psum_scatter(jnp.concatenate([lax.dot_general(token_rows, gate_rows,...]
    all_to_all x2 -> x1, blocking collectives: 32.3 us -> 24.1 us  [send_out(): lax.all_to_all(payload, 'yx', split_axis=1, concat_axis=1, tiled=True)]
    another operation x0 -> x2, other arithmetic: none -> 6.86 us  [the longest x1 6.18 us: shards(): back = bring_back(jnp.stack([partial_value, partial_grad]), expert_count)]
  transfers between devices with their start and end apart: 10 -> 5, of which waited for: 9 -> 4; matrix products, arithmetic and copies ran while one was open for 12% -> 13% of each run, Pallas kernels for 0% -> 0%
where the time goes in v2:
time: 442 us; the launch traced here: 439 us
  waiting for transfers between devices  296 us (67%)
  local copies, waits for them, and re-layouts  41.1 us (9%)
  other arithmetic  31.9 us (7%)
  blocking collectives  24.1 us (5%)
  matrix products  21.5 us (5%)
  between operations  14 us (3%)
  starting transfers between devices  10.8 us (2%)
    all_gather x1, waiting for transfers between devices, send_out(): shared = lax.all_gather(arrived, 'col', axis=1, tiled=True)  82 us
    reduce_scatter x1, waiting for transfers between devices, bring_back(): lax.psum_scatter(partial_value, 'col', scatter_dimension=1, tiled=True)  80.6 us
    reduce_scatter x1, waiting for transfers between devices, shards(): lax.psum_scatter(jnp.concatenate([lax.dot_general(token_rows, gate_rows,...  72.6 us
    all_gather x1, waiting for transfers between devices, shards(): full = lax.all_gather(weights, 'dp', axis=1, tiled=True)  60.4 us
    all_to_all x1, blocking collectives, send_out(): lax.all_to_all(payload, 'yx', split_axis=1, concat_axis=1, tiled=True)  24.1 us
    squeeze x2, local copies, waits for them, and re-layouts, shards(): token_rows, cot_rows = (both_rows[0], both_rows[1])  14.2 us
    all_to_all x1, starting transfers between devices, bring_back(): lax.all_to_all(summed, 'yx', split_axis=1, concat_axis=1, tiled=True)  10.2 us
    slice x1, local copies, waits for them, and re-layouts, shards(): token_rows, cot_rows = (both_rows[0], both_rows[1])  10.1 us
  transfers between devices with their start and end apart: 5, of which 4 were waited for; matrix products, arithmetic and copies ran while one was open for 13% of the time, Pallas kernels for 0%

profile of v2, /device:TPU:32, one launch (start us, length us, event | category | flops | bytes accessed | tf_op | source)
XLA Modules:
  0.0 439.1 jit_solution(145172162650093640)
XLA Ops:
  7.2 0.0 copy-start
  7.2 0.0 copy-start.8
  7.2 0.0 copy-start.2
  7.2 0.0 all-gather.3.cloned.1.call-start
  7.2 0.8 compare_select_fusion
  8.1 0.1 copy.33
  8.2 0.1 reshape.82
  8.3 0.2 copy-done
  8.4 0.9 gather_fusion.1
  9.3 0.3 reshape.63
  9.6 0.0 copy-done.8
  9.6 0.1 copy.34
  9.7 0.9 gather_fusion
  10.6 0.2 stack.16
  10.8 0.0 copy-start.7
  10.8 0.3 fusion.7
  11.1 0.7 pad_maximum_fusion.3
  11.8 24.1 %all_to_all.10 = bf16[2,16,4,4096]{3,2,0,1:T(4,128)(2,1)} all-to-all(bf16[2,16,4,4096]{3,2,0,1:T(4,128)(2,1)S(1)} %pad_maximum_fusion.3), channel_id=1, replica_groups=mesh['dp'=2,'yx'=16,'col'=8] {'yx'}, dimensions={1} | all-to-all | bytes 2097152 | tf_op jit(solution)/shard_map/all_to_all | solution.py:12
  35.9 0.0 all-gather.3.cloned.1.call-update
  35.9 0.0 all-gather.5.cloned.1.call-start
  35.9 0.0 copy-done.7
  36.0 3.7 pad_maximum_fusion.2
  39.6 0.0 all-gather.5.cloned.1.call-update
  39.6 0.2 reduce-scatter.3.cloned.1.call-start
  39.9 82.0 %all-gather.3.cloned.1.call-done = bf16[2,128,4,4096]{3,2,0,1:T(4,128)(2,1)} async-done(((bf16[2,16,4,4096]{3,2,0,1:T(4,128)(2,1)}), bf16[2,128,4,4096]{3,2,0,1:T(4,128)(2,1)}) %all-gather.3.cloned.1.call-update) | async-done | bytes 8388624 | tf_op jit(solution)/shard_map/all_gather | solution.py:13
  121.9 10.1 %fusion.12 = (bf16[1,128,4,4096]{3,2,0,1:T(4,128)(2,1)}, bf16[1,128,4,4096]{3,2,0,1:T(4,128)(2,1)}) fusion(bf16[2,128,4,4096]{3,2,0,1:T(4,128)(2,1)} %all-gather.3.cloned.1.call-done), kind=kLoop, calls=%fused_computation.39 | loop fusion | bytes 16777216 | tf_op jit(solution)/shard_map/slice | solution.py:37
  132.0 7.2 %squeeze.25 = bf16[512,4096]{1,0:T(8,128)(2,1)} reshape(bf16[1,128,4,4096]{3,2,0,1:T(4,128)(2,1)} %get-tuple-element.26) | data formatting | bytes 8388608 | tf_op jit(solution)/shard_map/squeeze | solution.py:37
  139.2 7.0 %squeeze.29 = bf16[512,4096]{1,0:T(8,128)(2,1)} reshape(bf16[1,128,4,4096]{3,2,0,1:T(4,128)(2,1)} %get-tuple-element.25) | data formatting | bytes 8388608 | tf_op jit(solution)/shard_map/squeeze | solution.py:37
  146.2 60.4 %all-gather.5.cloned.1.call-done = bf16[3,4096,256]{2,1,0:T(8,128)(2,1)} async-done(((bf16[3,2048,256]{2,1,0:T(8,128)(2,1)}), bf16[3,4096,256]{2,1,0:T(8,128)(2,1)}) %all-gather.5.cloned.1.call-update) | async-done | bytes 6291472 | tf_op jit(solution)/shard_map/all_gather | solution.py:33
  206.7 4.2 fusion.3
  210.9 0.4 copy-done.3
  211.3 3.6 fusion.5
  215.0 1.4 multiply_convert_fusion.2
  216.4 1.3 fusion.2
  217.7 3.3 fusion
  220.9 1.3 fusion.1
  222.3 6.2 %pad_maximum_fusion = bf16[2,512,4096]{2,1,0:T(8,128)(2,1)} fusion(bf16[1,512,4096]{2,1,0:T(8,128)(2,1)S(1)} %fusion.1, bf16[1,512,4096]{2,1,0:T(8,128)(2,1)} %fusion), kind=kLoop, calls=%fused_computation.4 | loop fusion | flops 4194304 | bytes 16777216 | tf_op jit(solution)/shard_map/stack | solution.py:54
  228.4 0.0 reduce-scatter.3.cloned.1.call-update
  228.5 0.3 reduce-scatter.5.cloned.1.call-start
  228.7 3.6 convolution_convert_fusion.2
  232.4 1.4 convolution_convert_fusion.3
  233.8 0.8 copy-done.6
  234.6 1.3 convolution_convert_fusion.1
  235.9 9.5 %pad_maximum_fusion.1 = bf16[4096,768]{0,1:T(8,128)(2,1)} fusion(bf16[4096,256]{0,1:T(8,128)(2,1)S(1)} %convolution_convert_fusion.1, bf16[4096,256]{0,1:T(8,128)(2,1)S(1)} %convolution_convert_fusion.2, bf16[4096,256]{0,1:T(8,128)(2,1)S(1)} %convolution_convert_fusion.3), kind=kLoop, calls=%fused_computation.6 | loop fusion | flops 18874368 | bytes 12582912 | tf_op jit(solution)/shard_map/concatenate | solution.py:58
  245.5 0.0 reduce-scatter.5.cloned.1.call-update
  245.5 80.6 %reduce-scatter.3.cloned.1.call-done = bf16[2,64,4096]{2,1,0:T(8,128)(2,1)} async-done(((bf16[2,512,4096]{2,1,0:T(8,128)(2,1)}), bf16[2,64,4096]{2,1,0:T(8,128)(2,1)}) %reduce-scatter.3.cloned.1.call-update) | async-done | bytes 1048592 | tf_op jit(solution)/shard_map/reduce_scatter | solution.py:19
  326.1 1.5 reshape.62
  327.5 1.6 copy.38
  329.1 10.2 %all-to-all-start.1 = ((bf16[2,16,4,4096]{3,2,0,1:T(4,128)(2,1)}), bf16[2,16,4,4096]{3,2,0,1:T(4,128)(2,1)S(1)}, u32[]{:S(2)}, u32[]{:S(2)}) async-start(bf16[2,16,4,4096]{3,2,0,1:T(4,128)(2,1)} %copy.38), calls=%async_computation.2 | async-start | bytes 2097152 | tf_op jit(solution)/shard_map/all_to_all | solution.py:21
  339.3 72.6 %reduce-scatter.5.cloned.1.call-done = bf16[2048,768]{0,1:T(8,128)(2,1)} async-done(((bf16[4096,768]{0,1:T(8,128)(2,1)}), bf16[2048,768]{0,1:T(8,128)(2,1)}) %reduce-scatter.5.cloned.1.call-update) | async-done | bytes 3145744 | tf_op jit(solution)/shard_map/reduce_scatter | solution.py:57
  412.0 3.2 slice_bitcast_fusion.9
  415.1 2.3 copy.39
  417.4 1.3 copy.40
  418.7 1.3 copy.41
  420.0 0.0 all-to-all-done.1
  420.0 0.2 convert_element_type.60
  420.2 0.3 fusion.6
  420.5 0.4 reshape.84
  420.9 3.3 scatter_custom_fusion
  424.2 2.7 convert_element_type.61
  426.9 0.1 slice.55
  427.0 1.3 reshape.92
  428.4 3.1 scatter_custom_fusion.1
  431.5 1.1 convert_element_type.62
  (10 shorter events, 0.0 us)
Async XLA Ops:
  7.2 1.2 copy-start
  7.2 2.4 copy-start.8
  7.2 2.5 copy-start.2
  7.2 114.7 %all-gather.3.cloned.1.call-start = ((), (), s32[]{:S(2)}) async-start(), calls=%async_computation.4 | async-start | bytes 9437184 | tf_op jit(solution)/shard_map/all_gather | solution.py:13
  10.8 25.2 %copy-start.7 = (bf16[1,2048,256]{2,1,0:T(8,128)(2,1)S(1)}, bf16[1,2048,256]{2,1,0:T(8,128)(2,1)}, u32[]{:S(2)}) copy-start(bf16[1,2048,256]{2,1,0:T(8,128)(2,1)} %param.12) | copy-start | bytes 3145732
  35.9 170.8 %all-gather.5.cloned.1.call-start = ((), (), s32[]{:S(2)}) async-start(), calls=%async_computation.5 | async-start | bytes 9437184 | tf_op jit(solution)/shard_map/all_gather | solution.py:33
  39.6 286.4 %reduce-scatter.3.cloned.1.call-start = ((), (), s32[]{:S(2)}) async-start(), calls=%async_computation.6 | async-start | bytes 9437184 | tf_op jit(solution)/shard_map/reduce_scatter | solution.py:19
  206.7 4.7 %copy-start.3 = (bf16[3,4096,256]{2,1,0:T(8,128)(2,1)S(1)}, bf16[3,4096,256]{2,1,0:T(8,128)(2,1)}, u32[]{:S(2)}) copy-start(bf16[3,4096,256]{2,1,0:T(8,128)(2,1)} %all-gather.5.cloned.1.call-done) | copy-start | bytes 18874372
  211.3 3.6 copy-start.4
  228.5 183.5 %reduce-scatter.5.cloned.1.call-start = ((), (), s32[]{:S(2)}) async-start(), calls=%async_computation.7 | async-start | bytes 9437184 | tf_op jit(solution)/shard_map/reduce_scatter | solution.py:57
  228.7 3.7 copy-start.5
  232.4 2.2 copy-start.6
  329.1 90.9 %all-to-all-start.1 = ((bf16[2,16,4,4096]{3,2,0,1:T(4,128)(2,1)}), bf16[2,16,4,4096]{3,2,0,1:T(4,128)(2,1)S(1)}, u32[]{:S(2)}, u32[]{:S(2)}) async-start(bf16[2,16,4,4096]{3,2,0,1:T(4,128)(2,1)} %copy.38), calls=%async_computation.2 | async-start | bytes 2097152 | tf_op jit(solution)/shard_map/all_to_all | solution.py:21
  426.9 5.7 %copy-start.1 = (bf16[128,4096]{1,0:T(8,128)(2,1)S(1)}, bf16[128,4096]{1,0:T(8,128)(2,1)}, u32[]{:S(2)}) copy-start(bf16[128,4096]{1,0:T(8,128)(2,1)} %param.13) | copy-start | bytes 3145732
Sparse Core Ops, SparseCore 0:
  36.0 85.8 all-gather.2
  123.7 82.9 all-gather.4
  228.6 97.4 reduce-scatter.2
  328.5 83.4 reduce-scatter.4

commit v3 on v2

--- a/solution.py
+++ b/solution.py
@@ -1,11 +1,44 @@
 import jax
 import jax.numpy as jnp
 from jax import lax
+from jax.experimental import pallas as pl
+from jax.experimental.pallas import tpu as pltpu
 from jax.sharding import Mesh
 from jax.sharding import PartitionSpec as P
 
 SPLIT = 8
 ROWS = ("dp", "yx", "col")
+MESH_ID = pl.DeviceIdType.MESH
+
+
+def swap_kernel(src_ref, dst_ref, sems):
+    other = 1 - lax.axis_index("dp")
+    barrier = pltpu.get_barrier_semaphore()
+    pl.semaphore_signal(barrier, 1, device_id={"dp": other}, device_id_type=MESH_ID)
+    pl.semaphore_wait(barrier, 1)
+    copy = pltpu.make_async_remote_copy(
+        src_ref=src_ref,
+        dst_ref=dst_ref,
+        send_sem=sems.at[0],
+        recv_sem=sems.at[1],
+        device_id={"dp": other},
+        device_id_type=MESH_ID,
+    )
+    copy.start()
+    copy.wait()
+
+
+def swap_with_partner(x, collective_id):
+    size = x.size * x.dtype.itemsize
+    return pl.pallas_call(
+        swap_kernel,
+        out_shape=jax.ShapeDtypeStruct(x.shape, x.dtype),
+        in_specs=[pl.BlockSpec(memory_space=pl.ANY)],
+        out_specs=pl.BlockSpec(memory_space=pl.ANY),
+        scratch_shapes=[pltpu.SemaphoreType.DMA((2,))],
+        compiler_params=pltpu.CompilerParams(collective_id=collective_id, has_side_effects=True),
+        cost_estimate=pl.CostEstimate(flops=0, bytes_accessed=2 * size, transcendentals=0),
+    )(x)
 
 
 def send_out(payload):
@@ -18,22 +51,25 @@
     streams, total_rows, width = partial_value.shape
     summed = lax.psum_scatter(partial_value, "col", scatter_dimension=1, tiled=True)
     summed = summed.reshape(streams, expert_count, -1, width)
-    returned = lax.all_to_all(summed, "yx", split_axis=1, concat_axis=1, tiled=True)
-    return returned.astype(jnp.float32)
+    return lax.all_to_all(summed, "yx", split_axis=1, concat_axis=1, tiled=True)
 
 
 def shards(tokens, routes, gate_values, gate_weight, up_weight, down_weight, cotangent):
     width = tokens.shape[1]
+    half = gate_weight.shape[1]
     expert_count = routes.shape[1]
     chosen = routes[0]
     scales = gate_values[0][:, :, None]
     contract_last = (((1,), (1,)), ((), ()))
     contract_first = (((0,), (0,)), ((), ()))
-    weights = jnp.concatenate([gate_weight, up_weight, down_weight], axis=0)
-    full = lax.all_gather(weights, "dp", axis=1, tiled=True)
+    shift = lax.axis_index("dp") * half
+    own = jnp.concatenate([gate_weight, up_weight, down_weight], axis=0)
+    other = swap_with_partner(own, 0)
+    full = jnp.concatenate([own, other], axis=1)
     full_gate, full_up, full_down = full[0], full[1], full[2]
     scaled_cot = (scales * cotangent[chosen].astype(jnp.float32)).astype(jnp.bfloat16)
-    both_rows = send_out(jnp.stack([tokens[chosen], scaled_cot]))
+    home_rows = jnp.roll(jnp.stack([tokens[chosen], scaled_cot]), -shift, axis=-1)
+    both_rows = send_out(home_rows)
     token_rows, cot_rows = both_rows[0], both_rows[1]
     gate_pre = jnp.dot(token_rows, full_gate, preferred_element_type=jnp.float32)
     up_pre = jnp.dot(token_rows, full_up, preferred_element_type=jnp.float32)
@@ -52,37 +88,24 @@
         + lax.dot_general(up_rows, full_up, contract_last, preferred_element_type=jnp.float32)
     ).astype(jnp.bfloat16)
     back = bring_back(jnp.stack([partial_value, partial_grad]), expert_count)
+    back = jnp.roll(back, shift, axis=-1).astype(jnp.float32)
     layer_out = jnp.zeros((tokens.shape[0], width), jnp.float32).at[chosen].add(scales * back[0])
     token_grad = jnp.zeros((tokens.shape[0], width), jnp.float32).at[chosen].add(back[1])
-    grad_sums = lax.psum_scatter(
-        jnp.concatenate(
-            [
-                lax.dot_general(
-                    token_rows, gate_rows, contract_first, preferred_element_type=jnp.float32
-                ),
-                lax.dot_general(
-                    token_rows, up_rows, contract_first, preferred_element_type=jnp.float32
-                ),
-                lax.dot_general(
-                    cot_rows, hidden, contract_first, preferred_element_type=jnp.float32
-                ),
-            ],
-            axis=1,
-        ).astype(jnp.bfloat16),
-        "dp",
-        scatter_dimension=0,
-        tiled=True,
-    ).astype(jnp.float32)
-    hidden_width = hidden.shape[1]
-    gate_grad = grad_sums[:, :hidden_width].astype(jnp.bfloat16)[None]
-    up_grad = grad_sums[:, hidden_width : 2 * hidden_width].astype(jnp.bfloat16)[None]
-    down_grad = grad_sums[:, 2 * hidden_width :].astype(jnp.bfloat16)[None]
+    grad_terms = jnp.stack(
+        [
+            lax.dot_general(token_rows, gate_rows, contract_first, preferred_element_type=jnp.float32),
+            lax.dot_general(token_rows, up_rows, contract_first, preferred_element_type=jnp.float32),
+            lax.dot_general(cot_rows, hidden, contract_first, preferred_element_type=jnp.float32),
+        ]
+    )
+    arrived = swap_with_partner(grad_terms[:, half:].astype(jnp.bfloat16), 1)
+    grad_sums = (grad_terms[:, :half] + arrived.astype(jnp.float32)).astype(jnp.bfloat16)
     return (
         layer_out.astype(jnp.bfloat16),
         token_grad.astype(jnp.bfloat16),
-        gate_grad,
-        up_grad,
-        down_grad,
+        grad_sums[0][None],
+        grad_sums[1][None],
+        grad_sums[2][None],
     )
 
 

time: 442 us -> 441 us (level)
  waiting for transfers between devices: 296 us -> 12.8 us
  Pallas kernels: 0 us -> 277 us
  local copies, waits for them, and re-layouts: 41.1 us -> 50.3 us
    pallas_call x0 -> x2, Pallas kernels: none -> 277 us  [swap_with_partner(): pl.pallas_call(swap_kernel, out_shape=jax.ShapeDtypeStruct(x.shape, x.dty...]
    all_gather x1, waiting for transfers between devices: 82 us -> 0.02 us  [send_out(): shared = lax.all_gather(arrived, 'col', axis=1, tiled=True)]
    reduce_scatter x1, waiting for transfers between devices: 80.6 us -> 0.94 us  [bring_back(): lax.psum_scatter(partial_value, 'col', scatter_dimension=1, tiled=True)]
    reduce_scatter x1 -> x0, waiting for transfers between devices: 72.6 us -> none  [shards(): lax.psum_scatter(jnp.concatenate([lax.dot_general(token_rows, gate_rows,...]
    all_gather x1 -> x0, waiting for transfers between devices: 60.4 us -> none  [shards(): full = lax.all_gather(weights, 'dp', axis=1, tiled=True)]
    concatenate x2 -> x1, other arithmetic: 13.2 us -> 1.25 us  [shards(): jnp.roll(jnp.stack([tokens[chosen], scaled_cot]), -shift, axis=-1)]
    all_to_all x1, waiting for transfers between devices: 0.01 us -> 11.8 us  [bring_back(): return lax.all_to_all(summed, 'yx', split_axis=1, concat_axis=1, tiled=True)]
    slice x0 -> x2, local copies, waits for them, and re-layouts: none -> 6.55 us  [the longest x1 4.82 us: shards(): arrived = swap_with_partner(grad_terms[:, half:].astype(jnp.bfloat16), 1)]
  transfers between devices with their start and end apart: 5 -> 3, of which waited for: 4 -> 2; matrix products, arithmetic and copies ran while one was open for 13% -> 6% of each run, Pallas kernels for 0% -> 63%
where the time goes in v3:
time: 441 us; the launch traced here: 438 us
  Pallas kernels  277 us (63%)
  local copies, waits for them, and re-layouts  50.3 us (11%)
  other arithmetic  29.4 us (7%)
  blocking collectives  24.1 us (5%)
  matrix products  23.1 us (5%)
  between operations  14.4 us (3%)
  waiting for transfers between devices  12.8 us (3%)
  starting transfers between devices  7.04 us (2%)
    pallas_call x2, Pallas kernels, swap_with_partner(): pl.pallas_call(swap_kernel, out_shape=jax.ShapeDtypeStruct(x.shape, x.dty...  277 us
    all_to_all x1, blocking collectives, send_out(): lax.all_to_all(payload, 'yx', split_axis=1, concat_axis=1, tiled=True)  24.1 us
    squeeze x2, local copies, waits for them, and re-layouts, shards(): token_rows, cot_rows = (both_rows[0], both_rows[1])  14 us
    all_to_all x1, waiting for transfers between devices, bring_back(): return lax.all_to_all(summed, 'yx', split_axis=1, concat_axis=1, tiled=True)  11.8 us
    slice x1, local copies, waits for them, and re-layouts, shards(): token_rows, cot_rows = (both_rows[0], both_rows[1])  10 us
  transfers between devices with their start and end apart: 3, of which 2 were waited for; matrix products, arithmetic and copies ran while one was open for 6% of the time, Pallas kernels for 63%

profile of v3, /device:TPU:32, one launch (start us, length us, event | category | flops | bytes accessed | tf_op | source)
XLA Modules:
  0.0 437.6 jit_solution(8622479408946111880)
XLA Ops:
  7.2 0.0 copy-start
  7.2 0.0 copy-start.8
  7.2 0.0 all-gather.2.cloned.1.call-start
  7.3 0.8 compare_select_fusion
  8.1 0.1 copy.24
  8.2 0.1 reshape.82
  8.3 0.1 copy-done
  8.4 0.9 gather_fusion
  9.3 0.2 stack.28
  9.5 0.0 copy-start.15
  9.5 0.9 gather_fusion.1
  10.4 0.3 reshape.63
  10.7 0.0 copy-done.15
  10.7 0.1 copy.25
  10.8 0.3 fusion.14
  11.1 1.3 fusion.11
  12.4 24.1 %all_to_all.10 = bf16[2,16,4,4096]{3,2,0,1:T(4,128)(2,1)} all-to-all(bf16[2,16,4,4096]{3,2,0,1:T(4,128)(2,1)S(1)} %fusion.11), channel_id=1, replica_groups=mesh['dp'=2,'yx'=16,'col'=8] {'yx'}, dimensions={1} | all-to-all | bytes 2097152 | tf_op jit(solution)/shard_map/all_to_all | solution.py:45
  36.4 0.0 all-gather.2.cloned.1.call-update
  36.5 0.2 reduce-scatter.2.cloned.1.call-start
  36.7 1.3 constant_dynamic-update-slice_fusion.2
  38.0 1.3 constant_dynamic-update-slice_fusion.1
  39.3 1.3 constant_dynamic-update-slice_fusion.src_ref
  40.6 1.6 copy-done.2
  42.3 136.3 %shard_map.110 = bf16[3,2048,256]{2,1,0:T(8,128)(2,1)} custom-call(bf16[3,2048,256]{2,1,0:T(8,128)(2,1)} %copy-done.2), custom_call_target="tpu_custom_call" | custom-call | bytes 6291456 | tf_op jit(solution)/shard_map/pallas_call | solution.py:33
  178.5 0.0 all-gather.2.cloned.1.call-done
  178.6 10.0 %fusion.29 = (bf16[1,128,4,4096]{3,2,0,1:T(4,128)(2,1)}, bf16[1,128,4,4096]{3,2,0,1:T(4,128)(2,1)}) fusion(bf16[2,128,4,4096]{3,2,0,1:T(4,128)(2,1)} %all-gather.2.cloned.1.call-done), kind=kLoop, calls=%fused_computation.58 | loop fusion | bytes 16777216 | tf_op jit(solution)/shard_map/slice | solution.py:73
  188.6 6.9 %squeeze.25 = bf16[512,4096]{1,0:T(8,128)(2,1)} reshape(bf16[1,128,4,4096]{3,2,0,1:T(4,128)(2,1)} %get-tuple-element.7) | data formatting | bytes 8388608 | tf_op jit(solution)/shard_map/squeeze | solution.py:73
  195.5 7.1 %squeeze.29 = bf16[512,4096]{1,0:T(8,128)(2,1)} reshape(bf16[1,128,4,4096]{3,2,0,1:T(4,128)(2,1)} %get-tuple-element.6) | data formatting | bytes 8388608 | tf_op jit(solution)/shard_map/squeeze | solution.py:73
  202.6 3.9 fusion.24
  206.5 0.8 copy-done.7
  207.3 1.3 fusion.19
  208.6 0.9 copy-done.5
  209.5 1.4 multiply_convert_fusion.2
  210.9 0.0 copy-start.13
  210.9 0.0 copy-start.11
  210.9 1.3 fusion.22
  212.2 0.0 copy-done.13
  212.2 3.3 fusion.1
  215.5 5.7 %fusion.2 = bf16[1,512,4096]{2,1,0:T(8,128)(2,1)} fusion(f32[512,4096]{1,0:T(8,128)S(1)} %fusion.22, bf16[512,256]{1,0:T(8,128)(2,1)S(1)} %get-tuple-element.13, bf16[3,2048,256]{2,1,0:T(8,128)(2,1)S(1)} %copy-done.3, bf16[3,2048,256]{2,1,0:T(8,128)(2,1)S(1)} %copy-done.4), kind=kOutput, calls=%fused_computation.16 | convolution fusion | flops 1082130432 | bytes 19136512 | tf_op jit(solution)/shard_map/dot_general | solution.py:88
  221.2 7.4 %pad_maximum_fusion.1 = bf16[2,512,4096]{2,1,0:T(8,128)(2,1)} fusion(bf16[1,512,4096]{2,1,0:T(8,128)(2,1)} %fusion.2, bf16[1,512,4096]{2,1,0:T(8,128)(2,1)} %fusion.1), kind=kLoop, calls=%fused_computation.5 | loop fusion | flops 4194304 | bytes 16777216 | tf_op jit(solution)/shard_map/stack | solution.py:90
  228.7 0.0 reduce-scatter.2.cloned.1.call-update
  228.7 0.9 copy-done.14
  229.6 3.6 convolution_bitcast_fusion
  233.3 1.3 convolution_bitcast_fusion.1
  234.6 1.3 convolution_bitcast_fusion.2
  235.9 5.2 %pad_maximum_fusion = f32[3,4096,256]{2,1,0:T(8,128)} fusion(f32[1,4096,256]{2,1,0:T(8,128)S(1)} %convolution_bitcast_fusion, f32[1,4096,256]{2,1,0:T(8,128)S(1)} %convolution_bitcast_fusion.1, f32[1,4096,256]{2,1,0:T(8,128)S(1)} %convolution_bitcast_fusion.2), kind=kLoop, calls=%fused_computation.4 | loop fusion | flops 6291456 | bytes 25165824 | tf_op jit(solution)/shard_map/stack | solution.py:94
  241.0 4.8 %slice.99.src_ref = bf16[3,2048,256]{2,1,0:T(8,128)(2,1)} slice(f32[3,4096,256]{2,1,0:T(8,128)} %pad_maximum_fusion), slice={[0:3], [2048:4096], [0:256]} | slice | bytes 6291456 | tf_op jit(solution)/shard_map/slice | solution.py:101
  245.9 140.2 %shard_map.111 = bf16[3,2048,256]{2,1,0:T(8,128)(2,1)} custom-call(bf16[3,2048,256]{2,1,0:T(8,128)(2,1)} %slice.99.src_ref), custom_call_target="tpu_custom_call" | custom-call | bytes 6291456 | tf_op jit(solution)/shard_map/pallas_call | solution.py:33
  386.1 0.9 reduce-scatter.2.cloned.1.call-done
  387.0 2.3 reshape.62
  389.4 2.8 copy.29
  392.2 6.8 %all-to-all-start.1 = ((bf16[2,16,4,4096]{3,2,0,1:T(4,128)(2,1)}), bf16[2,16,4,4096]{3,2,0,1:T(4,128)(2,1)}, u32[]{:S(2)}, u32[]{:S(2)}) async-start(bf16[2,16,4,4096]{3,2,0,1:T(4,128)(2,1)} %copy.29), calls=%async_computation.2 | async-start | bytes 2097152 | tf_op jit(solution)/shard_map/all_to_all | solution.py:54
  399.0 3.5 fusion
  402.5 1.7 fusion.30
  404.2 11.8 %all-to-all-done.1 = bf16[2,16,4,4096]{3,2,0,1:T(4,128)(2,1)} async-done(((bf16[2,16,4,4096]{3,2,0,1:T(4,128)(2,1)}), bf16[2,16,4,4096]{3,2,0,1:T(4,128)(2,1)}, u32[]{:S(2)}, u32[]{:S(2)}) %all-to-all-start.1) | async-done | bytes 1048608 | tf_op jit(solution)/shard_map/all_to_all | solution.py:54
  416.0 2.2 fusion.9
  418.3 0.3 fusion.13
  418.5 1.0 copy-done.10
  419.6 1.3 reshape.84
  420.9 3.2 scatter_custom_fusion
  424.1 1.1 convert_element_type.63
  425.2 1.3 reshape.92
  426.5 3.1 scatter_custom_fusion.1
  429.6 1.1 convert_element_type.64
  (22 shorter events, 0.0 us)
Async XLA Ops:
  7.2 1.2 copy-start
  7.2 2.3 copy-start.8
  7.2 171.4 %all-gather.2.cloned.1.call-start = ((), (), s32[]{:S(2)}) async-start(), calls=%async_computation.3 | async-start | bytes 9437184 | tf_op jit(solution)/shard_map/all_gather | solution.py:46
  9.5 1.2 copy-start.15
  36.5 350.6 %reduce-scatter.2.cloned.1.call-start = ((), (), s32[]{:S(2)}) async-start(), calls=%async_computation.4 | async-start | bytes 9437184 | tf_op jit(solution)/shard_map/reduce_scatter | solution.py:52
  40.6 1.7 copy-start.2
  195.5 7.1 %copy-start.3 = (bf16[3,2048,256]{2,1,0:T(8,128)(2,1)S(1)}, bf16[3,2048,256]{2,1,0:T(8,128)(2,1)}, u32[]{:S(2)}) copy-start(bf16[3,2048,256]{2,1,0:T(8,128)(2,1)} %copy-done.2) | copy-start | bytes 9437188
  202.6 3.9 copy-start.4
  202.6 4.7 %copy-start.7 = (bf16[512,4096]{1,0:T(8,128)(2,1)S(1)}, bf16[512,4096]{1,0:T(8,128)(2,1)}, u32[]{:S(2)}) copy-start(bf16[512,4096]{1,0:T(8,128)(2,1)} %squeeze.29) | copy-start | bytes 12582916
  207.3 2.2 copy-start.5
  210.9 1.3 copy-start.13
  210.9 4.6 %copy-start.11 = (bf16[512,256]{1,0:T(8,128)(2,1)}, bf16[512,256]{1,0:T(8,128)(2,1)S(1)}, u32[]{:S(2)}) copy-start(bf16[512,256]{1,0:T(8,128)(2,1)S(1)} %get-tuple-element.13) | copy-start | bytes 786436
  228.7 0.9 copy-start.14
  229.6 3.6 copy-start.6
  229.6 3.6 copy-start.12
  386.1 12.9 %copy-start.9 = (bf16[3,2048,256]{2,1,0:T(8,128)(2,1)S(1)}, bf16[3,2048,256]{2,1,0:T(8,128)(2,1)}, u32[]{:S(2)}) copy-start(bf16[3,2048,256]{2,1,0:T(8,128)(2,1)} %shard_map.111) | copy-start | bytes 9437188
  392.2 23.8 %all-to-all-start.1 = ((bf16[2,16,4,4096]{3,2,0,1:T(4,128)(2,1)}), bf16[2,16,4,4096]{3,2,0,1:T(4,128)(2,1)}, u32[]{:S(2)}, u32[]{:S(2)}) async-start(bf16[2,16,4,4096]{3,2,0,1:T(4,128)(2,1)} %copy.29), calls=%async_computation.2 | async-start | bytes 2097152 | tf_op jit(solution)/shard_map/all_to_all | solution.py:54
  418.3 1.3 copy-start.10
  420.9 4.3 slice-start
  425.2 5.5 %copy-start.1 = (bf16[128,4096]{1,0:T(8,128)(2,1)S(1)}, bf16[128,4096]{1,0:T(8,128)(2,1)}, u32[]{:S(2)}) copy-start(bf16[128,4096]{1,0:T(8,128)(2,1)} %param.9) | copy-start | bytes 3145732
Sparse Core Ops, SparseCore 0:
  36.6 118.7 all-gather.1
  228.8 158.1 reduce-scatter.1

commit v4 on v3

--- a/solution.py
+++ b/solution.py
@@ -68,9 +68,8 @@
     full = jnp.concatenate([own, other], axis=1)
     full_gate, full_up, full_down = full[0], full[1], full[2]
     scaled_cot = (scales * cotangent[chosen].astype(jnp.float32)).astype(jnp.bfloat16)
-    home_rows = jnp.roll(jnp.stack([tokens[chosen], scaled_cot]), -shift, axis=-1)
-    both_rows = send_out(home_rows)
-    token_rows, cot_rows = both_rows[0], both_rows[1]
+    token_rows = send_out(jnp.roll(tokens[chosen], -shift, axis=-1)[None])[0]
+    cot_rows = send_out(jnp.roll(scaled_cot, -shift, axis=-1)[None])[0]
     gate_pre = jnp.dot(token_rows, full_gate, preferred_element_type=jnp.float32)
     up_pre = jnp.dot(token_rows, full_up, preferred_element_type=jnp.float32)
     gate_sigma = jax.nn.sigmoid(gate_pre)
@@ -87,10 +86,12 @@
         lax.dot_general(gate_rows, full_gate, contract_last, preferred_element_type=jnp.float32)
         + lax.dot_general(up_rows, full_up, contract_last, preferred_element_type=jnp.float32)
     ).astype(jnp.bfloat16)
-    back = bring_back(jnp.stack([partial_value, partial_grad]), expert_count)
-    back = jnp.roll(back, shift, axis=-1).astype(jnp.float32)
-    layer_out = jnp.zeros((tokens.shape[0], width), jnp.float32).at[chosen].add(scales * back[0])
-    token_grad = jnp.zeros((tokens.shape[0], width), jnp.float32).at[chosen].add(back[1])
+    back_value = bring_back(partial_value[None], expert_count)[0]
+    back_value = jnp.roll(back_value, shift, axis=-1).astype(jnp.float32)
+    back_grad = bring_back(partial_grad[None], expert_count)[0]
+    back_grad = jnp.roll(back_grad, shift, axis=-1).astype(jnp.float32)
+    layer_out = jnp.zeros((tokens.shape[0], width), jnp.float32).at[chosen].add(scales * back_value)
+    token_grad = jnp.zeros((tokens.shape[0], width), jnp.float32).at[chosen].add(back_grad)
     grad_terms = jnp.stack(
         [
             lax.dot_general(token_rows, gate_rows, contract_first, preferred_element_type=jnp.float32),

time: 441 us -> 407 us (0.923)
  Pallas kernels: 277 us -> 250 us
  local copies, waits for them, and re-layouts: 50.3 us -> 37.2 us
  blocking collectives: 24.1 us -> 32.3 us
  other arithmetic: 29.4 us -> 22.2 us
  matrix products: 23.1 us -> 29.6 us
    pallas_call x2, Pallas kernels: 277 us -> 250 us  [swap_with_partner(): pl.pallas_call(swap_kernel, out_shape=jax.ShapeDtypeStruct(x.shape, x.dty...]
    squeeze x3 -> x0, local copies, waits for them, and re-layouts: 15.3 us -> none  [the longest x2 14 us: shards(): token_rows, cot_rows = (both_rows[0], both_rows[1])]
    another operation x1 -> x2, local copies, waits for them, and re-layouts: 0.2 us -> 13.9 us  [the longest x1 7.03 us: shards(): token_rows = send_out(jnp.roll(tokens[chosen], -shift, axis=-1)[None])[0]]
    slice x3 -> x0, local copies, waits for them, and re-layouts: 10 us -> none  [the longest x1 10 us: shards(): token_rows, cot_rows = (both_rows[0], both_rows[1])]
    all_to_all x1 -> x2, blocking collectives: 24.1 us -> 32.3 us  [send_out(): lax.all_to_all(payload, 'yx', split_axis=1, concat_axis=1, tiled=True)]
    another operation x1 -> x0, other arithmetic: 7.42 us -> none  [shards(): back = bring_back(jnp.stack([partial_value, partial_grad]), expert_count)]
    all_to_all x1 -> x2, waiting for transfers between devices: 11.8 us -> 7.73 us  [bring_back(): return lax.all_to_all(summed, 'yx', split_axis=1, concat_axis=1, tiled=True)]
    all_to_all x1 -> x2, starting transfers between devices: 6.78 us -> 10.7 us  [bring_back(): return lax.all_to_all(summed, 'yx', split_axis=1, concat_axis=1, tiled=True)]
  transfers between devices with their start and end apart: 3 -> 6, of which waited for: 2 -> 3; matrix products, arithmetic and copies ran while one was open for 6% -> 15% of each run, Pallas kernels for 63% -> 62%
where the time goes in v4:
time: 407 us; the launch traced here: 405 us
  Pallas kernels  250 us (61%)
  local copies, waits for them, and re-layouts  37.2 us (9%)
  blocking collectives  32.3 us (8%)
  matrix products  29.6 us (7%)
  other arithmetic  22.2 us (5%)
  between operations  14.1 us (3%)
  starting transfers between devices  11.1 us (3%)
  waiting for transfers between devices  9.26 us (2%)
    pallas_call x2, Pallas kernels, swap_with_partner(): pl.pallas_call(swap_kernel, out_shape=jax.ShapeDtypeStruct(x.shape, x.dty...  250 us
    all_to_all x2, blocking collectives, send_out(): lax.all_to_all(payload, 'yx', split_axis=1, concat_axis=1, tiled=True)  32.3 us
    all_to_all x2, starting transfers between devices, bring_back(): return lax.all_to_all(summed, 'yx', split_axis=1, concat_axis=1, tiled=True)  10.7 us
  transfers between devices with their start and end apart: 6, of which 3 were waited for; matrix products, arithmetic and copies ran while one was open for 15% of the time, Pallas kernels for 62%

profile of v4, /device:TPU:32, one launch (start us, length us, event | category | flops | bytes accessed | tf_op | source)
XLA Modules:
  0.0 405.5 jit_solution(13662199878511570479)
XLA Ops:
  7.2 0.0 copy-start
  7.2 0.0 all-gather.3.cloned.1.call-start
  7.2 0.8 compare_select_fusion
  8.0 0.1 copy.16
  8.1 0.1 reshape.65
  8.2 0.2 copy-done
  8.4 0.9 gather_fusion
  9.3 0.2 reshape.48
  9.5 0.6 fusion.18
  10.1 18.5 %all_to_all.20 = bf16[1,16,4,4096]{3,2,0,1:T(4,128)(2,1)} all-to-all(bf16[1,16,4,4096]{3,2,0,1:T(4,128)(2,1)S(1)} %fusion.18), channel_id=1, replica_groups=mesh['dp'=2,'yx'=16,'col'=8] {'yx'}, dimensions={1} | all-to-all | bytes 1048576 | tf_op jit(solution)/shard_map/all_to_all | solution.py:45
  28.6 0.0 all-gather.3.cloned.1.call-update
  28.6 0.0 all-gather.5.cloned.1.call-start
  28.6 0.9 gather_fusion.1
  29.5 0.3 reshape.83
  29.9 0.1 copy.17
  30.0 0.3 multiply_convert_fusion
  30.2 0.6 fusion.15
  30.8 13.8 %all_to_all.21 = bf16[1,16,4,4096]{3,2,0,1:T(4,128)(2,1)} all-to-all(bf16[1,16,4,4096]{3,2,0,1:T(4,128)(2,1)S(1)} %fusion.15), channel_id=1, replica_groups=mesh['dp'=2,'yx'=16,'col'=8] {'yx'}, dimensions={1} | all-to-all | bytes 1048576 | tf_op jit(solution)/shard_map/all_to_all | solution.py:45
  44.6 0.0 all-gather.5.cloned.1.call-update
  44.7 0.0 reduce-scatter.3.cloned.1.call-start
  44.7 1.3 constant_dynamic-update-slice_fusion.2
  46.0 1.3 constant_dynamic-update-slice_fusion.1
  47.3 1.3 constant_dynamic-update-slice_fusion.src_ref
  48.6 1.6 copy-done.2
  50.3 126.2 %shard_map.110 = bf16[3,2048,256]{2,1,0:T(8,128)(2,1)} custom-call(bf16[3,2048,256]{2,1,0:T(8,128)(2,1)} %copy-done.2), custom_call_target="tpu_custom_call" | custom-call | bytes 6291456 | tf_op jit(solution)/shard_map/pallas_call | solution.py:33
  176.5 0.0 all-gather.3.cloned.1.call-done
  176.5 7.0 %squeeze_reshape.6 = bf16[512,4096]{1,0:T(8,128)(2,1)} reshape(bf16[1,128,4,4096]{3,2,0,1:T(4,128)(2,1)} %all-gather.3.cloned.1.call-done) | data formatting | bytes 8388608 | tf_op jit(solution)/shard_map/squeeze;reshape | solution.py:71
  183.6 4.7 %fusion.24 = f32[512,256]{1,0:T(8,128)} fusion(bf16[512,4096]{1,0:T(8,128)(2,1)} %squeeze_reshape.6, bf16[3,2048,256]{2,1,0:T(8,128)(2,1)S(1)} %copy-done.3, bf16[3,2048,256]{2,1,0:T(8,128)(2,1)} %shard_map.110), kind=kOutput, calls=%fused_computation.57 | convolution fusion | flops 1077936128 | bytes 11010048 | tf_op jit(solution)/shard_map/dot_general | solution.py:73
  188.2 0.0 copy-done.7
  188.3 2.1 fusion.27
  190.3 6.9 %squeeze_reshape.7 = bf16[512,4096]{1,0:T(8,128)(2,1)} reshape(bf16[1,128,4,4096]{3,2,0,1:T(4,128)(2,1)} %all-gather.5.cloned.1.call-done) | data formatting | bytes 8388608 | tf_op jit(solution)/shard_map/squeeze;reshape | solution.py:72
  197.2 5.0 %multiply_convert_fusion.1 = (bf16[512,256]{1,0:T(8,128)(2,1)}, bf16[512,256]{1,0:T(8,128)(2,1)S(1)}, bf16[512,256]{1,0:T(8,128)(2,1)S(1)}) fusion(f32[512,256]{1,0:T(8,128)} %fusion.24, f32[512,256]{1,0:T(8,128)} %fusion.27, bf16[512,4096]{1,0:T(8,128)(2,1)} %squeeze_reshape.7, bf16[3,2048,256]{2,1,0:T(8,128)(2,1)} %shard_map.110, ...), kind=kOutput, calls=%fused_computation.46 | convolution fusion | flops 1080033280 | bytes 12320768 | tf_op jit(solution)/shard_map/dot_general | solution.py:80
  202.2 0.7 copy-done.12
  202.9 3.2 fusion.1
  206.2 0.0 reduce-scatter.3.cloned.1.call-update
  206.2 0.2 reduce-scatter.5.cloned.1.call-start
  206.4 2.7 fusion.22
  209.1 5.7 %fusion.2 = bf16[1,512,4096]{2,1,0:T(8,128)(2,1)} fusion(f32[512,4096]{1,0:T(8,128)S(1)} %fusion.22, bf16[512,256]{1,0:T(8,128)(2,1)S(1)} %copy-done.10, bf16[3,2048,256]{2,1,0:T(8,128)(2,1)S(1)} %copy-done.3, bf16[3,2048,256]{2,1,0:T(8,128)(2,1)S(1)} %copy-done.6), kind=kOutput, calls=%fused_computation.15 | convolution fusion | flops 1082130432 | bytes 19136512 | tf_op jit(solution)/shard_map/dot_general | solution.py:87
  214.9 0.0 reduce-scatter.5.cloned.1.call-update
  214.9 0.9 copy-done.13
  215.8 3.6 convolution_bitcast_fusion
  219.5 1.3 convolution_bitcast_fusion.1
  220.8 1.3 convolution_bitcast_fusion.2
  222.1 5.0 %pad_maximum_fusion = f32[3,4096,256]{2,1,0:T(8,128)} fusion(f32[1,4096,256]{2,1,0:T(8,128)S(1)} %convolution_bitcast_fusion, f32[1,4096,256]{2,1,0:T(8,128)S(1)} %convolution_bitcast_fusion.1, f32[1,4096,256]{2,1,0:T(8,128)S(1)} %convolution_bitcast_fusion.2), kind=kLoop, calls=%fused_computation.4 | loop fusion | flops 6291456 | bytes 25165824 | tf_op jit(solution)/shard_map/stack | solution.py:95
  227.1 4.9 %slice.74.src_ref = bf16[3,2048,256]{2,1,0:T(8,128)(2,1)} slice(f32[3,4096,256]{2,1,0:T(8,128)} %pad_maximum_fusion), slice={[0:3], [2048:4096], [0:256]} | slice | bytes 6291456 | tf_op jit(solution)/shard_map/slice | solution.py:102
  231.9 123.6 %shard_map.111 = bf16[3,2048,256]{2,1,0:T(8,128)(2,1)} custom-call(bf16[3,2048,256]{2,1,0:T(8,128)(2,1)} %slice.74.src_ref), custom_call_target="tpu_custom_call" | custom-call | bytes 6291456 | tf_op jit(solution)/shard_map/pallas_call | solution.py:33
  355.5 4.5 %fusion = bf16[3,2048,256]{2,1,0:T(8,128)(2,1)S(1)} fusion(f32[3,4096,256]{2,1,0:T(8,128)} %pad_maximum_fusion, bf16[3,2048,256]{2,1,0:T(8,128)(2,1)} %shard_map.111), kind=kLoop, calls=%fused_computation.12 | loop fusion | flops 4718592 | bytes 12582912 | tf_op jit(solution)/shard_map/convert_element_type | solution.py:103
  360.0 0.0 reduce-scatter.3.cloned.1.call-done
  360.0 2.0 reshape.45
  362.1 6.9 %all-to-all-start.1 = ((bf16[1,16,4,4096]{3,2,0,1:T(4,128)(2,1)}), bf16[1,16,4,4096]{3,2,0,1:T(4,128)(2,1)}, u32[]{:S(2)}, u32[]{:S(2)}) async-start(bf16[1,16,4,4096]{3,2,0,1:T(4,128)(2,1)} %bitcast.54), calls=%async_computation.2 | async-start | bytes 1048576 | tf_op jit(solution)/shard_map/all_to_all | solution.py:54
  369.0 1.7 fusion.29
  370.7 1.4 reduce-scatter.5.cloned.1.call-done
  372.2 2.0 reshape.46
  374.2 5.0 %all-to-all-done.1 = bf16[1,16,4,4096]{3,2,0,1:T(4,128)(2,1)} async-done(((bf16[1,16,4,4096]{3,2,0,1:T(4,128)(2,1)}), bf16[1,16,4,4096]{3,2,0,1:T(4,128)(2,1)}, u32[]{:S(2)}, u32[]{:S(2)}) %all-to-all-start.1) | async-done | bytes 524320 | tf_op jit(solution)/shard_map/all_to_all | solution.py:54
  379.2 3.8 all-to-all-start.3
  383.0 1.6 convert_multiply_fusion
  384.6 1.3 reshape.67
  385.9 3.1 scatter_custom_fusion
  389.0 1.1 convert_element_type.43
  390.1 2.7 all-to-all-done.3
  392.9 0.5 fusion.13
  393.4 1.3 reshape.75
  394.7 3.1 scatter_custom_fusion.1
  397.9 1.1 convert_element_type.50
  (26 shorter events, 0.1 us)
Async XLA Ops:
  7.2 1.2 copy-start
  7.2 169.3 %all-gather.3.cloned.1.call-start = ((), (), s32[]{:S(2)}) async-start(), calls=%async_computation.6 | async-start | bytes 4718592 | tf_op jit(solution)/shard_map/all_gather | solution.py:46
  8.4 20.2 %copy-start.9 = (bf16[128,4096]{1,0:T(8,128)(2,1)S(1)}, bf16[128,4096]{1,0:T(8,128)(2,1)}, u32[]{:S(2)}) copy-start(bf16[128,4096]{1,0:T(8,128)(2,1)} %param.15) | copy-start | bytes 3145732
  10.1 19.8 %copy-start.14 = (f32[1,16,4]{1,2,0:T(4,128)S(1)}, f32[1,16,4]{1,2,0:T(4,128)}, u32[]{:S(2)}) copy-start(f32[1,16,4]{1,2,0:T(4,128)} %param.11) | copy-start | bytes 772
  28.6 161.8 %all-gather.5.cloned.1.call-start = ((), (), s32[]{:S(2)}) async-start(), calls=%async_computation.8 | async-start | bytes 4718592 | tf_op jit(solution)/shard_map/all_gather | solution.py:46
  44.7 315.4 %reduce-scatter.3.cloned.1.call-start = ((), (), s32[]{:S(2)}) async-start(), calls=%async_computation.7 | async-start | bytes 4718592 | tf_op jit(solution)/shard_map/reduce_scatter | solution.py:52
  48.6 1.6 copy-start.2
  176.5 7.1 %copy-start.3 = (bf16[3,2048,256]{2,1,0:T(8,128)(2,1)S(1)}, bf16[3,2048,256]{2,1,0:T(8,128)(2,1)}, u32[]{:S(2)}) copy-start(bf16[3,2048,256]{2,1,0:T(8,128)(2,1)} %copy-done.2) | copy-start | bytes 9437188
  183.6 4.7 %copy-start.4 = (bf16[3,2048,256]{2,1,0:T(8,128)(2,1)S(1)}, bf16[3,2048,256]{2,1,0:T(8,128)(2,1)}, u32[]{:S(2)}) copy-start(bf16[3,2048,256]{2,1,0:T(8,128)(2,1)} %shard_map.110) | copy-start | bytes 9437188
  183.6 4.7 %copy-start.7 = (bf16[512,4096]{1,0:T(8,128)(2,1)S(1)}, bf16[512,4096]{1,0:T(8,128)(2,1)}, u32[]{:S(2)}) copy-start(bf16[512,4096]{1,0:T(8,128)(2,1)} %squeeze_reshape.6) | copy-start | bytes 12582916
  197.2 5.7 %copy-start.5 = (bf16[3,2048,256]{2,1,0:T(8,128)(2,1)S(1)}, bf16[3,2048,256]{2,1,0:T(8,128)(2,1)}, u32[]{:S(2)}) copy-start(bf16[3,2048,256]{2,1,0:T(8,128)(2,1)} %shard_map.110) | copy-start | bytes 9437188
  202.2 0.7 copy-start.12
  206.2 166.0 %reduce-scatter.5.cloned.1.call-start = ((), (), s32[]{:S(2)}) async-start(), calls=%async_computation.9 | async-start | bytes 4718592 | tf_op jit(solution)/shard_map/reduce_scatter | solution.py:52
  206.4 2.7 copy-start.6
  206.4 2.7 copy-start.10
  214.9 0.9 copy-start.13
  215.8 3.6 copy-start.8
  215.8 3.6 copy-start.11
  362.1 17.1 %all-to-all-start.1 = ((bf16[1,16,4,4096]{3,2,0,1:T(4,128)(2,1)}), bf16[1,16,4,4096]{3,2,0,1:T(4,128)(2,1)}, u32[]{:S(2)}, u32[]{:S(2)}) async-start(bf16[1,16,4,4096]{3,2,0,1:T(4,128)(2,1)} %bitcast.54), calls=%async_computation.2 | async-start | bytes 1048576 | tf_op jit(solution)/shard_map/all_to_all | solution.py:54
  379.2 13.7 %all-to-all-start.3 = ((bf16[1,16,4,4096]{3,2,0,1:T(4,128)(2,1)}), bf16[1,16,4,4096]{3,2,0,1:T(4,128)(2,1)S(1)}, u32[]{:S(2)}, u32[]{:S(2)}) async-start(bf16[1,16,4,4096]{3,2,0,1:T(4,128)(2,1)} %bitcast.11), calls=%async_computation.5 | async-start | bytes 1048576 | tf_op jit(solution)/shard_map/all_to_all | solution.py:54
  392.9 6.1 %copy-start.1 = (bf16[128,4096]{1,0:T(8,128)(2,1)S(1)}, bf16[128,4096]{1,0:T(8,128)(2,1)}, u32[]{:S(2)}) copy-start(bf16[128,4096]{1,0:T(8,128)(2,1)} %param.9) | copy-start | bytes 3145732
Sparse Core Ops, SparseCore 0:
  28.7 61.1 all-gather.2
  91.8 70.4 all-gather.4
  206.3 79.2 reduce-scatter.2
  288.0 84.1 reduce-scatter.4

commit v5 on v4

v5 whole, which is shorter than its diff:
```python
import jax
import jax.numpy as jnp
from jax import lax
from jax.experimental import pallas as pl
from jax.experimental.pallas import tpu as pltpu
from jax.sharding import Mesh
from jax.sharding import PartitionSpec as P

SPLIT = 8
ROWS = ("dp", "yx", "col")
MESH_ID = pl.DeviceIdType.MESH
CONTRACT_LAST = (((1,), (1,)), ((), ()))
CONTRACT_FIRST = (((0,), (0,)), ((), ()))


def swap_kernel(src_ref, dst_ref, sems):
    other = 1 - lax.axis_index("dp")
    barrier = pltpu.get_barrier_semaphore()
    pl.semaphore_signal(barrier, 1, device_id={"dp": other}, device_id_type=MESH_ID)
    pl.semaphore_wait(barrier, 1)
    copy = pltpu.make_async_remote_copy(
        src_ref=src_ref,
        dst_ref=dst_ref,
        send_sem=sems.at[0],
        recv_sem=sems.at[1],
        device_id={"dp": other},
        device_id_type=MESH_ID,
    )
    copy.start()
    copy.wait()


def swap_with_partner(x, collective_id):
    size = x.size * x.dtype.itemsize
    return pl.pallas_call(
        swap_kernel,
        out_shape=jax.ShapeDtypeStruct(x.shape, x.dtype),
        in_specs=[pl.BlockSpec(memory_space=pl.ANY)],
        out_specs=pl.BlockSpec(memory_space=pl.ANY),
        scratch_shapes=[pltpu.SemaphoreType.DMA((2,))],
        compiler_params=pltpu.CompilerParams(collective_id=collective_id, has_side_effects=True),
        cost_estimate=pl.CostEstimate(flops=0, bytes_accessed=2 * size, transcendentals=0),
    )(x)


def send_out(payload, shift, half, collective_id):
    arrived = lax.all_to_all(payload[None], "yx", split_axis=1, concat_axis=1, tiled=True)[0]
    rolled = jnp.roll(arrived, -shift, axis=-1)
    traded = swap_with_partner(rolled[..., half:], collective_id)
    both = jnp.stack([rolled[..., :half], traded])
    shared = lax.all_gather(both, "col", axis=0, tiled=False)
    return shared.reshape(-1, half)


def bring_back(partial_rows, shift, collective_id):
    total_rows, half = partial_rows.shape
    summed = lax.psum_scatter(
        partial_rows.reshape(SPLIT, 2, -1, half), "col", scatter_dimension=0, tiled=True
    )[0]
    traded = swap_with_partner(summed[1], collective_id)
    rows = jnp.roll(jnp.concatenate([summed[0], traded], axis=-1), shift, axis=-1)
    rows = rows.reshape(-1, 4, 2 * half)
    back = lax.all_to_all(rows[None], "yx", split_axis=1, concat_axis=1, tiled=True)[0]
    return back.astype(jnp.float32)


def own_batch(partial, collective_id):
    rows, k = partial.shape
    split = partial.reshape(SPLIT, 2, -1, k)
    traded = swap_with_partner(split[:, 1], collective_id)
    return (split[:, 0] + traded).reshape(-1, k)


def both_batches(values, collective_id):
    traded = swap_with_partner(values, collective_id)
    lead = values.shape[:-2]
    k = values.shape[-1]
    mine = values.reshape(lead + (SPLIT, 1, -1, k))
    theirs = traded.reshape(lead + (SPLIT, 1, -1, k))
    return jnp.concatenate([mine, theirs], axis=-3).reshape(lead + (-1, k))


def shards(tokens, routes, gate_values, gate_weight, up_weight, down_weight, cotangent):
    width = tokens.shape[1]
    half = gate_weight.shape[1]
    chosen = routes[0]
    scales = gate_values[0][:, :, None]
    shift = lax.axis_index("dp") * half
    wg, wu, wd = gate_weight[0], up_weight[0], down_weight[0]
    scaled_cot = (scales * cotangent[chosen].astype(jnp.float32)).astype(jnp.bfloat16)
    token_rows = send_out(tokens[chosen], shift, half, 0)
    cot_rows = send_out(scaled_cot, shift, half, 1)
    gate_pre = own_batch(jnp.dot(token_rows, wg, preferred_element_type=jnp.float32), 2)
    up_pre = own_batch(jnp.dot(token_rows, wu, preferred_element_type=jnp.float32), 3)
    gate_sigma = jax.nn.sigmoid(gate_pre)
    hidden = (gate_pre * gate_sigma * up_pre).astype(jnp.bfloat16)
    hidden_all = both_batches(hidden, 4)
    partial_value = lax.dot_general(
        hidden_all, wd, CONTRACT_LAST, preferred_element_type=jnp.float32
    ).astype(jnp.bfloat16)
    back_value = bring_back(partial_value, shift, 5)
    hidden_grad = own_batch(jnp.dot(cot_rows, wd, preferred_element_type=jnp.float32), 6)
    gate_rows = (hidden_grad * up_pre * gate_sigma * (1.0 + gate_pre * (1.0 - gate_sigma))).astype(
        jnp.bfloat16
    )
    up_rows = (hidden_grad * gate_pre * gate_sigma).astype(jnp.bfloat16)
    rows_all = both_batches(jnp.stack([gate_rows, up_rows]), 7)
    gate_all, up_all = rows_all[0], rows_all[1]
    partial_grad = (
        lax.dot_general(gate_all, wg, CONTRACT_LAST, preferred_element_type=jnp.float32)
        + lax.dot_general(up_all, wu, CONTRACT_LAST, preferred_element_type=jnp.float32)
    ).astype(jnp.bfloat16)
    back_grad = bring_back(partial_grad, shift, 8)
    layer_out = jnp.zeros((tokens.shape[0], width), jnp.float32).at[chosen].add(scales * back_value)
    token_grad = jnp.zeros((tokens.shape[0], width), jnp.float32).at[chosen].add(back_grad)
    gate_grad = lax.dot_general(token_rows, gate_all, CONTRACT_FIRST, preferred_element_type=jnp.float32)
    up_grad = lax.dot_general(token_rows, up_all, CONTRACT_FIRST, preferred_element_type=jnp.float32)
    down_grad = lax.dot_general(cot_rows, hidden_all, CONTRACT_FIRST, preferred_element_type=jnp.float32)
    return (
        layer_out.astype(jnp.bfloat16),
        token_grad.astype(jnp.bfloat16),
        gate_grad.astype(jnp.bfloat16)[None],
        up_grad.astype(jnp.bfloat16)[None],
        down_grad.astype(jnp.bfloat16)[None],
    )


def solution(mesh):
    n_dp, n_expert = mesh.devices.shape
    fine = Mesh(mesh.devices.reshape(n_dp, n_expert // SPLIT, SPLIT), ROWS)
    placed = (
        P(ROWS, None),
        P(ROWS, None, None),
        P(ROWS, None, None),
        P(("yx", "col"), "dp", None),
        P(("yx", "col"), "dp", None),
        P(("yx", "col"), "dp", None),
        P(ROWS, None),
    )
    return jax.shard_map(
        shards,
        mesh=fine,
        in_specs=placed,
        out_specs=(
            P(ROWS, None),
            P(ROWS, None),
            P(("yx", "col"), "dp", None),
            P(("yx", "col"), "dp", None),
            P(("yx", "col"), "dp", None),
        ),
        check_vma=False,
    )
```

time: 407 us -> 400 us (0.983); the launches traced: 405 us -> 394 us
  Pallas kernels: 250 us -> 112 us
  waiting for transfers between devices: 9.26 us -> 125 us
  blocking collectives: 32.3 us -> 0 us
  local copies, waits for them, and re-layouts: 37.2 us -> 67.2 us
  starting transfers between devices: 11.1 us -> 24.3 us
    pallas_call x2 -> x9, Pallas kernels: 250 us -> 112 us  [swap_with_partner(): pl.pallas_call(swap_kernel, out_shape=jax.ShapeDtypeStruct(x.shape, x.dty...]
    reduce_scatter x2, waiting for transfers between devices: 1.43 us -> 59 us  [bring_back(): lax.psum_scatter(partial_rows.reshape(SPLIT, 2, -1, half), 'col', scatter...]
    all_gather x2, waiting for transfers between devices: 0.02 us -> 40.7 us  [send_out(): shared = lax.all_gather(both, 'col', axis=0, tiled=False)]
    all_to_all x2 -> x0, blocking collectives: 32.3 us -> none  [send_out(): lax.all_to_all(payload, 'yx', split_axis=1, concat_axis=1, tiled=True)]
    all_to_all x2 -> x4, waiting for transfers between devices: 7.73 us -> 24.8 us  [the longest x2 19.6 us: send_out(): lax.all_to_all(payload[None], 'yx', split_axis=1, concat_axis=1, tiled=True)]
    all_gather x0 -> x2, local copies, waits for them, and re-layouts: none -> 15.5 us  [send_out(): shared = lax.all_gather(both, 'col', axis=0, tiled=False)]
    dot_general x0 -> x2, local copies, waits for them, and re-layouts: none -> 14 us  [the longest x1 7.08 us: shards(): jnp.dot(token_rows, wg, preferred_element_type=jnp.float32)]
    all_to_all x2 -> x4, starting transfers between devices: 10.7 us -> 23.9 us  [the longest x2 13.3 us: bring_back(): lax.all_to_all(rows[None], 'yx', split_axis=1, concat_axis=1, tiled=True)[0]]
  transfers between devices with their start and end apart: 6 -> 8, of which waited for: 3 -> 6; matrix products, arithmetic and copies ran while one was open for 15% -> 19% of each run, Pallas kernels for 62% -> 22%
where the time goes in v5:
time: 400 us; the launch traced here: 394 us
  waiting for transfers between devices  125 us (31%)
  Pallas kernels  112 us (28%)
  local copies, waits for them, and re-layouts  67.2 us (17%)
  matrix products  27.9 us (7%)
  starting transfers between devices  24.3 us (6%)
  other arithmetic  24.2 us (6%)
  between operations  14.2 us (4%)
    pallas_call x9, Pallas kernels, swap_with_partner(): pl.pallas_call(swap_kernel, out_shape=jax.ShapeDtypeStruct(x.shape, x.dty...  112 us
    reduce_scatter x2, waiting for transfers between devices, bring_back(): lax.psum_scatter(partial_rows.reshape(SPLIT, 2, -1, half), 'col', scatter...  59 us
    all_gather x2, waiting for transfers between devices, send_out(): shared = lax.all_gather(both, 'col', axis=0, tiled=False)  40.7 us
    all_to_all x2, waiting for transfers between devices, send_out(): lax.all_to_all(payload[None], 'yx', split_axis=1, concat_axis=1, tiled=True)  19.6 us
    all_gather x2, local copies, waits for them, and re-layouts, send_out(): shared = lax.all_gather(both, 'col', axis=0, tiled=False)  15.5 us
    reshape x2, local copies, waits for them, and re-layouts, send_out(): return shared.reshape(-1, half)  13.9 us
    all_to_all x2, starting transfers between devices, bring_back(): lax.all_to_all(rows[None], 'yx', split_axis=1, concat_axis=1, tiled=True)[0]  13.3 us
    all_to_all x2, starting transfers between devices, send_out(): lax.all_to_all(payload[None], 'yx', split_axis=1, concat_axis=1, tiled=True)  10.6 us
  transfers between devices with their start and end apart: 8, of which 6 were waited for; matrix products, arithmetic and copies ran while one was open for 19% of the time, Pallas kernels for 22%

profile of v5, /device:TPU:32, one launch (start us, length us, event | category | flops | bytes accessed | tf_op | source)
XLA Modules:
  0.0 394.3 jit_solution(11746787583611644853)
XLA Ops:
  8.2 2.7 gather_fusion
  11.0 1.0 broadcast_in_dim.8
  12.0 7.0 %all-to-all-start = ((bf16[1,16,4,4096]{3,2,0,1:T(4,128)(2,1)}), bf16[1,16,4,4096]{3,2,0,1:T(4,128)(2,1)S(1)}, u32[]{:S(2)}, u32[]{:S(2)}) async-start(bf16[1,16,4,4096]{3,2,0,1:T(4,128)(2,1)} %bitcast.169), calls=%async_computation | async-start | bytes 1048576 | tf_op jit(solution)/shard_map/all_to_all | solution.py:47
  19.1 0.9 gather_fusion.1
  20.3 1.1 fusion.12
  21.4 9.2 %all-to-all-done = bf16[1,16,4,4096]{3,2,0,1:T(4,128)(2,1)S(1)} async-done(((bf16[1,16,4,4096]{3,2,0,1:T(4,128)(2,1)}), bf16[1,16,4,4096]{3,2,0,1:T(4,128)(2,1)S(1)}, u32[]{:S(2)}, u32[]{:S(2)}) %all-to-all-start) | async-done | bytes 524320 | tf_op jit(solution)/shard_map/all_to_all | solution.py:47
  30.5 3.6 all-to-all-start.2
  34.2 10.4 %all-to-all-done.2 = bf16[1,16,4,4096]{3,2,0,1:T(4,128)(2,1)S(1)} async-done(((bf16[1,16,4,4096]{3,2,0,1:T(4,128)(2,1)}), bf16[1,16,4,4096]{3,2,0,1:T(4,128)(2,1)S(1)}, u32[]{:S(2)}, u32[]{:S(2)}) %all-to-all-start.2) | async-done | bytes 524320 | tf_op jit(solution)/shard_map/all_to_all | solution.py:47
  44.6 1.1 fusion.24
  45.7 0.9 slice_bitcast_fusion.11
  46.7 6.7 %shard_map.110 = bf16[16,4,2048]{2,1,0:T(4,128)(2,1)} custom-call(bf16[16,4,2048]{2,1,0:T(4,128)(2,1)} %get-tuple-element.22.src_ref), custom_call_target="tpu_custom_call" | custom-call | bytes 524288 | tf_op jit(solution)/shard_map/pallas_call | solution.py:35
  53.4 1.3 pad_maximum_fusion.1
  54.7 1.1 copy.57
  55.9 0.9 slice_bitcast_fusion.8
  56.8 6.7 %shard_map.115 = bf16[16,4,2048]{2,1,0:T(4,128)(2,1)} custom-call(bf16[16,4,2048]{2,1,0:T(4,128)(2,1)} %get-tuple-element.24.src_ref), custom_call_target="tpu_custom_call" | custom-call | bytes 524288 | tf_op jit(solution)/shard_map/pallas_call | solution.py:35
  63.5 1.3 pad_maximum_fusion.3
  64.9 1.1 copy.66
  66.1 40.6 %all-gather.5.cloned.1.call-done = bf16[16,16,4,2048]{3,1,2,0:T(8,128)(2,1)} async-done(((bf16[2,16,4,2048]{3,1,2,0:T(8,128)(2,1)}), bf16[16,16,4,2048]{3,1,2,0:T(8,128)(2,1)}) %all-gather.5.cloned.1.call-update) | async-done | bytes 4194320 | tf_op jit(solution)/shard_map/all_gather | solution.py:51
  106.7 7.7 %copy.58 = bf16[16,16,4,2048]{3,2,1,0:T(4,128)(2,1)} copy(bf16[16,16,4,2048]{3,1,2,0:T(8,128)(2,1)} %all-gather.5.cloned.1.call-done) | data formatting | bytes 8388608 | tf_op jit(solution)/shard_map/all_gather | solution.py:51
  114.4 7.1 %dot_general.31 = bf16[8,2,64,2048]{3,2,1,0:T(8,128)(2,1)} reshape(bf16[16,16,4,2048]{3,2,1,0:T(4,128)(2,1)} %copy.58) | data formatting | bytes 8388608 | tf_op jit(solution)/shard_map/dot_general | solution.py:93
  121.5 3.6 fusion.4
  125.1 1.0 copy-done.10
  126.9 40.5 %shard_map.111 = f32[8,64,256]{2,1,0:T(8,128)} custom-call(f32[8,64,256]{2,1,0:T(8,128)} %slice_bitcast_fusion.4.src_ref), custom_call_target="tpu_custom_call" | custom-call | bytes 1048576 | tf_op jit(solution)/shard_map/pallas_call | solution.py:35
  167.4 3.5 fusion.2
  171.0 1.0 copy-done.11
  172.8 13.9 %shard_map.112 = f32[8,64,256]{2,1,0:T(8,128)} custom-call(f32[8,64,256]{2,1,0:T(8,128)} %slice_bitcast_fusion.2.src_ref), custom_call_target="tpu_custom_call" | custom-call | bytes 1048576 | tf_op jit(solution)/shard_map/pallas_call | solution.py:35
  186.7 7.8 %copy.67 = bf16[16,16,4,2048]{3,2,1,0:T(4,128)(2,1)} copy(bf16[16,16,4,2048]{3,1,2,0:T(8,128)(2,1)} %all-gather.7.cloned.1.call-done) | data formatting | bytes 8388608 | tf_op jit(solution)/shard_map/all_gather | solution.py:51
  194.5 6.9 %dot_general.35 = bf16[8,2,64,2048]{3,2,1,0:T(8,128)(2,1)} reshape(bf16[16,16,4,2048]{3,2,1,0:T(4,128)(2,1)} %copy.67) | data formatting | bytes 8388608 | tf_op jit(solution)/shard_map/dot_general | solution.py:102
  201.4 3.5 fusion
  204.9 1.0 copy-done.12
  206.7 13.0 %shard_map.116 = f32[8,64,256]{2,1,0:T(8,128)} custom-call(f32[8,64,256]{2,1,0:T(8,128)} %slice_bitcast_fusion.src_ref), custom_call_target="tpu_custom_call" | custom-call | bytes 1048576 | tf_op jit(solution)/shard_map/pallas_call | solution.py:35
  219.8 2.0 fusion.47
  222.7 6.7 %shard_map.113 = bf16[512,256]{1,0:T(8,128)(2,1)} custom-call(bf16[512,256]{1,0:T(8,128)(2,1)} %fusion.41.src_ref), custom_call_target="tpu_custom_call" | custom-call | bytes 524288 | tf_op jit(solution)/shard_map/pallas_call | solution.py:35
  229.4 0.9 fusion.46
  230.3 1.0 pad_maximum_fusion.2
  231.3 3.3 convolution_convert_fusion
  236.0 11.0 %shard_map.117 = bf16[2,512,256]{2,1,0:T(8,128)(2,1)} custom-call(bf16[2,512,256]{2,1,0:T(8,128)(2,1)} %pad_maximum_fusion.4.src_ref), custom_call_target="tpu_custom_call" | custom-call | bytes 1048576 | tf_op jit(solution)/shard_map/pallas_call | solution.py:35
  247.0 1.2 pad_maximum_fusion
  248.4 1.3 fusion.15
  249.7 3.3 add_convert_fusion
  253.1 7.0 %reshape.242 = bf16[1024,2048]{1,0:T(8,128)(2,1)} reshape(bf16[16,16,4,2048]{3,2,1,0:T(4,128)(2,1)} %copy.58) | data formatting | bytes 8388608 | tf_op jit(solution)/shard_map/reshape | solution.py:52
  260.1 6.9 %reshape.243 = bf16[1024,2048]{1,0:T(8,128)(2,1)} reshape(bf16[16,16,4,2048]{3,2,1,0:T(4,128)(2,1)} %copy.67) | data formatting | bytes 8388608 | tf_op jit(solution)/shard_map/reshape | solution.py:52
  267.0 4.7 %fusion.6 = bf16[1,2048,256]{2,1,0:T(8,128)(2,1)} fusion(bf16[1024,2048]{1,0:T(8,128)(2,1)} %reshape.242, bf16[1024,256]{1,0:T(8,128)(2,1)S(1)} %bitcast.164), kind=kOutput, calls=%fused_computation.15 | convolution fusion | flops 1074266112 | bytes 5767168 | tf_op jit(solution)/shard_map/dot_general | solution.py:116
  271.7 2.4 fusion.7
  274.1 2.4 fusion.8
  276.4 15.3 %reduce-scatter.3.cloned.1.call-done = bf16[1,2,64,2048]{3,2,1,0:T(8,128)(2,1)} async-done(((bf16[8,2,64,2048]{3,2,1,0:T(8,128)(2,1)}), bf16[1,2,64,2048]{3,2,1,0:T(8,128)(2,1)}) %reduce-scatter.3.cloned.1.call-update) | async-done | bytes 524304 | tf_op jit(solution)/shard_map/reduce_scatter | solution.py:57
  291.7 1.8 slice_bitcast_fusion.9
  293.5 6.7 %shard_map.114 = bf16[64,2048]{1,0:T(8,128)(2,1)} custom-call(bf16[64,2048]{1,0:T(8,128)(2,1)} %get-tuple-element.19.src_ref), custom_call_target="tpu_custom_call" | custom-call | bytes 524288 | tf_op jit(solution)/shard_map/pallas_call | solution.py:35
  300.2 1.3 fusion.26
  301.5 1.0 broadcast_in_dim_reshape.6
  302.5 6.2 %all-to-all-start.1 = ((bf16[1,16,4,4096]{3,2,0,1:T(4,128)(2,1)}), bf16[1,16,4,4096]{3,2,0,1:T(4,128)(2,1)S(1)}, u32[]{:S(2)}, u32[]{:S(2)}) async-start(bf16[1,16,4,4096]{3,2,0,1:T(4,128)(2,1)} %broadcast_in_dim_reshape.6), calls=%async_computation.2 | async-start | bytes 1048576 | tf_op jit(solution)/shard_map/all_to_all | solution.py:63
  308.8 43.8 %reduce-scatter.5.cloned.1.call-done = bf16[1,2,64,2048]{3,2,1,0:T(8,128)(2,1)} async-done(((bf16[8,2,64,2048]{3,2,1,0:T(8,128)(2,1)}), bf16[1,2,64,2048]{3,2,1,0:T(8,128)(2,1)}) %reduce-scatter.5.cloned.1.call-update) | async-done | bytes 524304 | tf_op jit(solution)/shard_map/reduce_scatter | solution.py:57
  352.5 1.8 slice_bitcast_fusion.6
  354.3 6.7 %shard_map.118 = bf16[64,2048]{1,0:T(8,128)(2,1)} custom-call(bf16[64,2048]{1,0:T(8,128)(2,1)} %get-tuple-element.15.src_ref), custom_call_target="tpu_custom_call" | custom-call | bytes 524288 | tf_op jit(solution)/shard_map/pallas_call | solution.py:35
  361.0 1.3 fusion.22
  362.4 1.0 broadcast_in_dim_reshape.7
  363.4 7.0 %all-to-all-start.3 = ((bf16[1,16,4,4096]{3,2,0,1:T(4,128)(2,1)}), bf16[1,16,4,4096]{3,2,0,1:T(4,128)(2,1)}, u32[]{:S(2)}, u32[]{:S(2)}) async-start(bf16[1,16,4,4096]{3,2,0,1:T(4,128)(2,1)} %broadcast_in_dim_reshape.7), calls=%async_computation.5 | async-start | bytes 1048576 | tf_op jit(solution)/shard_map/all_to_all | solution.py:63
  370.7 1.3 reshape.267
  372.0 3.1 scatter_custom_fusion
  375.1 1.1 convert_element_type.101
  376.2 5.2 %all-to-all-done.3 = bf16[1,16,4,4096]{3,2,0,1:T(4,128)(2,1)} async-done(((bf16[1,16,4,4096]{3,2,0,1:T(4,128)(2,1)}), bf16[1,16,4,4096]{3,2,0,1:T(4,128)(2,1)}, u32[]{:S(2)}, u32[]{:S(2)}) %all-to-all-start.3) | async-done | bytes 524320 | tf_op jit(solution)/shard_map/all_to_all | solution.py:63
  381.5 2.1 reshape.275
  383.6 3.1 scatter_custom_fusion.1
  386.7 1.1 convert_element_type.114
  (52 shorter events, 6.9 us)
Async XLA Ops:
  7.2 194.3 %copy-start = (bf16[1,2048,256]{2,1,0:T(8,128)(2,1)S(1)}, bf16[1,2048,256]{2,1,0:T(8,128)(2,1)}, u32[]{:S(2)}) copy-start(bf16[1,2048,256]{2,1,0:T(8,128)(2,1)} %param.16) | copy-start | bytes 3145732
  7.2 11.8 %copy-start.13 = (f32[1,16,4]{1,2,0:T(4,128)S(1)}, f32[1,16,4]{1,2,0:T(4,128)}, u32[]{:S(2)}) copy-start(f32[1,16,4]{1,2,0:T(4,128)} %param.13) | copy-start | bytes 772
  7.2 11.9 %copy-start.2 = (bf16[128,4096]{1,0:T(8,128)(2,1)S(1)}, bf16[128,4096]{1,0:T(8,128)(2,1)}, u32[]{:S(2)}) copy-start(bf16[128,4096]{1,0:T(8,128)(2,1)} %param.17) | copy-start | bytes 3145732
  12.0 18.6 %all-to-all-start = ((bf16[1,16,4,4096]{3,2,0,1:T(4,128)(2,1)}), bf16[1,16,4,4096]{3,2,0,1:T(4,128)(2,1)S(1)}, u32[]{:S(2)}, u32[]{:S(2)}) async-start(bf16[1,16,4,4096]{3,2,0,1:T(4,128)(2,1)} %bitcast.169), calls=%async_computation | async-start | bytes 1048576 | tf_op jit(solution)/shard_map/all_to_all | solution.py:47
  30.5 14.1 %all-to-all-start.2 = ((bf16[1,16,4,4096]{3,2,0,1:T(4,128)(2,1)}), bf16[1,16,4,4096]{3,2,0,1:T(4,128)(2,1)S(1)}, u32[]{:S(2)}, u32[]{:S(2)}) async-start(bf16[1,16,4,4096]{3,2,0,1:T(4,128)(2,1)} %fusion.12), calls=%async_computation.3 | async-start | bytes 1048576 | tf_op jit(solution)/shard_map/all_to_all | solution.py:47
  34.1 72.6 %all-gather.5.cloned.1.call-start = ((), (), s32[]{:S(2)}) async-start(), calls=%async_computation.8 | async-start | bytes 4718592 | tf_op jit(solution)/shard_map/all_gather | solution.py:51
  55.8 130.9 %all-gather.7.cloned.1.call-start = ((), (), s32[]{:S(2)}) async-start(), calls=%async_computation.9 | async-start | bytes 4718592 | tf_op jit(solution)/shard_map/all_gather | solution.py:51
  66.0 225.7 %reduce-scatter.3.cloned.1.call-start = ((), (), s32[]{:S(2)}) async-start(), calls=%async_computation.6 | async-start | bytes 4718592 | tf_op jit(solution)/shard_map/reduce_scatter | solution.py:57
  114.4 7.1 %copy-start.6 = (bf16[1,2048,256]{2,1,0:T(8,128)(2,1)S(1)}, bf16[1,2048,256]{2,1,0:T(8,128)(2,1)}, u32[]{:S(2)}) copy-start(bf16[1,2048,256]{2,1,0:T(8,128)(2,1)} %param.14) | copy-start | bytes 3145732
  121.5 45.9 %copy-start.8 = (bf16[1,2048,256]{2,1,0:T(8,128)(2,1)S(1)}, bf16[1,2048,256]{2,1,0:T(8,128)(2,1)}, u32[]{:S(2)}) copy-start(bf16[1,2048,256]{2,1,0:T(8,128)(2,1)} %param.15) | copy-start | bytes 3145732
  125.1 1.0 copy-start.10
  170.9 1.0 copy-start.11
  201.4 18.4 %copy-start.5 = (f32[8,64,256]{2,1,0:T(8,128)S(1)}, f32[8,64,256]{2,1,0:T(8,128)}, u32[]{:S(2)}) copy-start(f32[8,64,256]{2,1,0:T(8,128)} %shard_map.111) | copy-start | bytes 1572868
  204.9 1.0 copy-start.12
  234.6 117.9 %reduce-scatter.5.cloned.1.call-start = ((), (), s32[]{:S(2)}) async-start(), calls=%async_computation.7 | async-start | bytes 4718592 | tf_op jit(solution)/shard_map/reduce_scatter | solution.py:57
  235.2 13.2 %copy-start.7 = (bf16[1,2048,256]{2,1,0:T(8,128)(2,1)S(1)}, bf16[1,2048,256]{2,1,0:T(8,128)(2,1)}, u32[]{:S(2)}) copy-start(bf16[1,2048,256]{2,1,0:T(8,128)(2,1)} %param.14) | copy-start | bytes 3145732
  248.4 1.3 copy-start.9
  267.0 4.7 %copy-start.4 = (bf16[1024,2048]{1,0:T(8,128)(2,1)S(1)}, bf16[1024,2048]{1,0:T(8,128)(2,1)}, u32[]{:S(2)}) copy-start(bf16[1024,2048]{1,0:T(8,128)(2,1)} %reshape.242) | copy-start | bytes 12582916
  271.7 2.4 copy-start.3
  302.5 60.9 %all-to-all-start.1 = ((bf16[1,16,4,4096]{3,2,0,1:T(4,128)(2,1)}), bf16[1,16,4,4096]{3,2,0,1:T(4,128)(2,1)S(1)}, u32[]{:S(2)}, u32[]{:S(2)}) async-start(bf16[1,16,4,4096]{3,2,0,1:T(4,128)(2,1)} %broadcast_in_dim_reshape.6), calls=%async_computation.2 | async-start | bytes 1048576 | tf_op jit(solution)/shard_map/all_to_all | solution.py:63
  363.4 18.1 %all-to-all-start.3 = ((bf16[1,16,4,4096]{3,2,0,1:T(4,128)(2,1)}), bf16[1,16,4,4096]{3,2,0,1:T(4,128)(2,1)}, u32[]{:S(2)}, u32[]{:S(2)}) async-start(bf16[1,16,4,4096]{3,2,0,1:T(4,128)(2,1)} %broadcast_in_dim_reshape.7), calls=%async_computation.5 | async-start | bytes 1048576 | tf_op jit(solution)/shard_map/all_to_all | solution.py:63
  375.1 12.7 %copy-start.1 = (bf16[1,2048,256]{2,1,0:T(8,128)(2,1)S(1)}, bf16[1,2048,256]{2,1,0:T(8,128)(2,1)}, u32[]{:S(2)}) copy-start(bf16[1,2048,256]{2,1,0:T(8,128)(2,1)} %param.16) | copy-start | bytes 3145732
Sparse Core Ops, SparseCore 0:
  56.0 50.6 all-gather.4
  109.1 62.0 all-gather.6
  234.8 56.8 reduce-scatter.2
  294.1 58.3 reduce-scatter.4

commit v6 on v5

--- a/solution.py
+++ b/solution.py
@@ -44,40 +44,38 @@
 
 
 def send_out(payload, shift, half, collective_id):
-    arrived = lax.all_to_all(payload[None], "yx", split_axis=1, concat_axis=1, tiled=True)[0]
+    arrived = lax.all_to_all(payload, "yx", split_axis=1, concat_axis=1, tiled=True)
     rolled = jnp.roll(arrived, -shift, axis=-1)
     traded = swap_with_partner(rolled[..., half:], collective_id)
-    both = jnp.stack([rolled[..., :half], traded])
-    shared = lax.all_gather(both, "col", axis=0, tiled=False)
-    return shared.reshape(-1, half)
+    both = jnp.stack([rolled[..., :half], traded], axis=1)
+    shared = lax.all_gather(both, "col", axis=1, tiled=False)
+    return shared.reshape(payload.shape[0], -1, half)
 
 
 def bring_back(partial_rows, shift, collective_id):
-    total_rows, half = partial_rows.shape
+    streams, total_rows, half = partial_rows.shape
     summed = lax.psum_scatter(
-        partial_rows.reshape(SPLIT, 2, -1, half), "col", scatter_dimension=0, tiled=True
-    )[0]
-    traded = swap_with_partner(summed[1], collective_id)
-    rows = jnp.roll(jnp.concatenate([summed[0], traded], axis=-1), shift, axis=-1)
-    rows = rows.reshape(-1, 4, 2 * half)
-    back = lax.all_to_all(rows[None], "yx", split_axis=1, concat_axis=1, tiled=True)[0]
+        partial_rows.reshape(streams, SPLIT, 2, -1, half), "col", scatter_dimension=1, tiled=True
+    )[:, 0]
+    traded = swap_with_partner(summed[:, 1], collective_id)
+    rows = jnp.roll(jnp.concatenate([summed[:, 0], traded], axis=-1), shift, axis=-1)
+    back = lax.all_to_all(rows, "yx", split_axis=1, concat_axis=1, tiled=True)
     return back.astype(jnp.float32)
 
 
 def own_batch(partial, collective_id):
-    rows, k = partial.shape
-    split = partial.reshape(SPLIT, 2, -1, k)
-    traded = swap_with_partner(split[:, 1], collective_id)
-    return (split[:, 0] + traded).reshape(-1, k)
+    streams, rows, k = partial.shape
+    split = partial.reshape(streams, SPLIT, 2, -1, k)
+    traded = swap_with_partner(split[:, :, 1], collective_id)
+    return (split[:, :, 0] + traded).reshape(streams, -1, k)
 
 
 def both_batches(values, collective_id):
     traded = swap_with_partner(values, collective_id)
-    lead = values.shape[:-2]
-    k = values.shape[-1]
-    mine = values.reshape(lead + (SPLIT, 1, -1, k))
-    theirs = traded.reshape(lead + (SPLIT, 1, -1, k))
-    return jnp.concatenate([mine, theirs], axis=-3).reshape(lead + (-1, k))
+    streams, rows, k = values.shape
+    mine = values.reshape(streams, SPLIT, 1, -1, k)
+    theirs = traded.reshape(streams, SPLIT, 1, -1, k)
+    return jnp.concatenate([mine, theirs], axis=2).reshape(streams, -1, k)
 
 
 def shards(tokens, routes, gate_values, gate_weight, up_weight, down_weight, cotangent):
@@ -88,31 +86,35 @@
     shift = lax.axis_index("dp") * half
     wg, wu, wd = gate_weight[0], up_weight[0], down_weight[0]
     scaled_cot = (scales * cotangent[chosen].astype(jnp.float32)).astype(jnp.bfloat16)
-    token_rows = send_out(tokens[chosen], shift, half, 0)
-    cot_rows = send_out(scaled_cot, shift, half, 1)
-    gate_pre = own_batch(jnp.dot(token_rows, wg, preferred_element_type=jnp.float32), 2)
-    up_pre = own_batch(jnp.dot(token_rows, wu, preferred_element_type=jnp.float32), 3)
+    home_rows = jnp.stack([tokens[chosen], scaled_cot]).reshape(2, -1, width)
+    both_rows = send_out(home_rows, shift, half, 0)
+    token_rows, cot_rows = both_rows[0], both_rows[1]
+    partials = jnp.stack(
+        [
+            jnp.dot(token_rows, wg, preferred_element_type=jnp.float32),
+            jnp.dot(token_rows, wu, preferred_element_type=jnp.float32),
+            jnp.dot(cot_rows, wd, preferred_element_type=jnp.float32),
+        ]
+    )
+    gate_pre, up_pre, hidden_grad = own_batch(partials, 1)
     gate_sigma = jax.nn.sigmoid(gate_pre)
     hidden = (gate_pre * gate_sigma * up_pre).astype(jnp.bfloat16)
-    hidden_all = both_batches(hidden, 4)
-    partial_value = lax.dot_general(
-        hidden_all, wd, CONTRACT_LAST, preferred_element_type=jnp.float32
-    ).astype(jnp.bfloat16)
-    back_value = bring_back(partial_value, shift, 5)
-    hidden_grad = own_batch(jnp.dot(cot_rows, wd, preferred_element_type=jnp.float32), 6)
     gate_rows = (hidden_grad * up_pre * gate_sigma * (1.0 + gate_pre * (1.0 - gate_sigma))).astype(
         jnp.bfloat16
     )
     up_rows = (hidden_grad * gate_pre * gate_sigma).astype(jnp.bfloat16)
-    rows_all = both_batches(jnp.stack([gate_rows, up_rows]), 7)
-    gate_all, up_all = rows_all[0], rows_all[1]
+    hidden_all, gate_all, up_all = both_batches(jnp.stack([hidden, gate_rows, up_rows]), 2)
+    partial_value = lax.dot_general(
+        hidden_all, wd, CONTRACT_LAST, preferred_element_type=jnp.float32
+    ).astype(jnp.bfloat16)
     partial_grad = (
         lax.dot_general(gate_all, wg, CONTRACT_LAST, preferred_element_type=jnp.float32)
         + lax.dot_general(up_all, wu, CONTRACT_LAST, preferred_element_type=jnp.float32)
     ).astype(jnp.bfloat16)
-    back_grad = bring_back(partial_grad, shift, 8)
-    layer_out = jnp.zeros((tokens.shape[0], width), jnp.float32).at[chosen].add(scales * back_value)
-    token_grad = jnp.zeros((tokens.shape[0], width), jnp.float32).at[chosen].add(back_grad)
+    back = bring_back(jnp.stack([partial_value, partial_grad]), shift, 3)
+    back = back.reshape(2, chosen.shape[0], chosen.shape[1], width)
+    layer_out = jnp.zeros((tokens.shape[0], width), jnp.float32).at[chosen].add(scales * back[0])
+    token_grad = jnp.zeros((tokens.shape[0], width), jnp.float32).at[chosen].add(back[1])
     gate_grad = lax.dot_general(token_rows, gate_all, CONTRACT_FIRST, preferred_element_type=jnp.float32)
     up_grad = lax.dot_general(token_rows, up_all, CONTRACT_FIRST, preferred_element_type=jnp.float32)
     down_grad = lax.dot_general(cot_rows, hidden_all, CONTRACT_FIRST, preferred_element_type=jnp.float32)

time: 400 us -> 400 us (level)
  waiting for transfers between devices: 125 us -> 203 us
  local copies, waits for them, and re-layouts: 67.2 us -> 28.5 us
  Pallas kernels: 112 us -> 82.4 us
  starting transfers between devices: 24.3 us -> 12.5 us
  other arithmetic: 24.2 us -> 30.2 us
  matrix products: 27.9 us -> 23.1 us
    all_gather x2 -> x1, waiting for transfers between devices: 40.7 us -> 87.3 us  [send_out(): shared = lax.all_gather(both, 'col', axis=1, tiled=False)]
    reduce_scatter x2 -> x1, waiting for transfers between devices: 59 us -> 89.7 us  [bring_back(): lax.psum_scatter(partial_rows.reshape(streams, SPLIT, 2, -1, half), 'col'...]
    pallas_call x9 -> x4, Pallas kernels: 112 us -> 82.4 us  [swap_with_partner(): pl.pallas_call(swap_kernel, out_shape=jax.ShapeDtypeStruct(x.shape, x.dty...]
    all_gather x2 -> x0, local copies, waits for them, and re-layouts: 15.5 us -> none  [send_out(): shared = lax.all_gather(both, 'col', axis=0, tiled=False)]
    dot_general x2 -> x0, local copies, waits for them, and re-layouts: 14 us -> none  [the longest x1 7.08 us: shards(): jnp.dot(token_rows, wg, preferred_element_type=jnp.float32)]
    reshape x2 -> x0, local copies, waits for them, and re-layouts: 13.9 us -> none  [send_out(): return shared.reshape(-1, half)]
    all_to_all x4 -> x2, starting transfers between devices: 23.9 us -> 12.4 us  [the longest x1 7.03 us: send_out(): lax.all_to_all(payload, 'yx', split_axis=1, concat_axis=1, tiled=True)]
    slice x3, local copies, waits for them, and re-layouts: 0.14 us -> 9.22 us  [the longest x1 4.18 us: shards(): token_rows, cot_rows = (both_rows[0], both_rows[1])]
  transfers between devices with their start and end apart: 8 -> 4, of which waited for: 6 -> 4; matrix products, arithmetic and copies ran while one was open for 19% -> 3% of each run, Pallas kernels for 22% -> 0%
where the time goes in v6:
time: 400 us; the launch traced here: 394 us
  waiting for transfers between devices  203 us (51%)
  Pallas kernels  82.4 us (21%)
  other arithmetic  30.2 us (8%)
  local copies, waits for them, and re-layouts  28.5 us (7%)
  matrix products  23.1 us (6%)
  between operations  14.5 us (4%)
  starting transfers between devices  12.5 us (3%)
    reduce_scatter x1, waiting for transfers between devices, bring_back(): lax.psum_scatter(partial_rows.reshape(streams, SPLIT, 2, -1, half), 'col'...  89.7 us
    all_gather x1, waiting for transfers between devices, send_out(): shared = lax.all_gather(both, 'col', axis=1, tiled=False)  87.3 us
    pallas_call x4, Pallas kernels, swap_with_partner(): pl.pallas_call(swap_kernel, out_shape=jax.ShapeDtypeStruct(x.shape, x.dty...  82.4 us
    all_to_all x1, waiting for transfers between devices, send_out(): lax.all_to_all(payload, 'yx', split_axis=1, concat_axis=1, tiled=True)  17.6 us
    all_to_all x1, waiting for transfers between devices, bring_back(): back = lax.all_to_all(rows, 'yx', split_axis=1, concat_axis=1, tiled=True)  8.54 us
  transfers between devices with their start and end apart: 4, of which 4 were waited for; matrix products, arithmetic and copies ran while one was open for 3% of the time, Pallas kernels for 0%

profile of v6, /device:TPU:32, one launch (start us, length us, event | category | flops | bytes accessed | tf_op | source)
XLA Modules:
  0.0 394.2 jit_solution(541516334213793214)
XLA Ops:
  7.2 0.8 compare_select_fusion
  8.0 0.1 copy.35
  8.1 0.1 reshape.405
  8.2 0.8 copy.37
  9.0 0.1 mul.185
  9.1 2.7 gather_fusion.1
  11.8 0.9 gather_fusion
  12.7 0.2 fusion.32
  12.8 0.1 pad_maximum_fusion.3
  13.0 2.1 copy.38
  15.0 7.0 %all-to-all-start = ((bf16[2,64,4096]{2,0,1:T(2,128)(2,1)}), bf16[2,64,4096]{2,0,1:T(2,128)(2,1)S(1)}, u32[]{:S(2)}, u32[]{:S(2)}) async-start(bf16[2,64,4096]{2,0,1:T(2,128)(2,1)} %copy.38), calls=%async_computation | async-start | bytes 2097152 | tf_op jit(solution)/shard_map/all_to_all | solution.py:47
  22.1 17.6 %all-to-all-done = bf16[2,64,4096]{2,0,1:T(2,128)(2,1)S(1)} async-done(((bf16[2,64,4096]{2,0,1:T(2,128)(2,1)}), bf16[2,64,4096]{2,0,1:T(2,128)(2,1)S(1)}, u32[]{:S(2)}, u32[]{:S(2)}) %all-to-all-start) | async-done | bytes 1048608 | tf_op jit(solution)/shard_map/all_to_all | solution.py:47
  39.7 0.6 copy.39
  40.3 0.6 fusion.25
  40.9 0.9 slice_bitcast_fusion.4
  41.7 12.1 %shard_map.110 = bf16[2,64,2048]{2,1,0:T(8,128)(2,1)} custom-call(bf16[2,64,2048]{2,1,0:T(8,128)(2,1)} %get-tuple-element.26.src_ref), custom_call_target="tpu_custom_call" | custom-call | bytes 1048576 | tf_op jit(solution)/shard_map/pallas_call | solution.py:35
  53.8 2.1 pad_maximum_fusion.4
  56.0 0.0 reduce-scatter.2.cloned.1.call-start
  56.0 87.3 %all-gather.3.cloned.1.call-done = bf16[2,16,64,2048]{3,2,0,1:T(8,128)(2,1)} async-done(((bf16[2,2,64,2048]{3,2,0,1:T(8,128)(2,1)}), bf16[2,16,64,2048]{3,2,0,1:T(8,128)(2,1)}) %all-gather.3.cloned.1.call-update) | async-done | bytes 8388624 | tf_op jit(solution)/shard_map/all_gather | solution.py:51
  143.3 4.2 %fusion.63 = (bf16[1,16,64,2048]{3,2,0,1:T(8,128)(2,1)S(1)}, bf16[1,16,64,2048]{3,2,0,1:T(8,128)(2,1)S(1)}) fusion(bf16[2,16,64,2048]{3,2,0,1:T(8,128)(2,1)} %all-gather.3.cloned.1.call-done), kind=kLoop, calls=%fused_computation.103 | loop fusion | bytes 16777216 | tf_op jit(solution)/shard_map/slice | solution.py:91
  147.5 1.3 fusion.16
  148.8 0.7 copy-done.5
  149.4 0.1 copy-done.8
  149.5 1.3 fusion.13
  150.8 1.3 fusion.19
  152.1 0.3 pad_maximum_fusion.1
  152.4 1.6 copy-done.4
  154.1 1.4 slice_bitcast_fusion.src_ref
  155.4 36.9 %shard_map.111 = f32[3,8,64,256]{3,2,1,0:T(8,128)} custom-call(f32[3,8,64,256]{3,2,1,0:T(8,128)} %slice_bitcast_fusion.src_ref), custom_call_target="tpu_custom_call" | custom-call | bytes 3145728 | tf_op jit(solution)/shard_map/pallas_call | solution.py:35
  192.3 2.1 fusion.12
  194.4 1.1 fusion.55
  195.5 0.1 fusion.64
  195.6 0.3 fusion.45
  195.9 1.0 pad_maximum_fusion.5.src_ref
  196.9 19.2 %shard_map.112 = bf16[3,512,256]{2,1,0:T(8,128)(2,1)} custom-call(bf16[3,512,256]{2,1,0:T(8,128)(2,1)} %pad_maximum_fusion.5.src_ref), custom_call_target="tpu_custom_call" | custom-call | bytes 1572864 | tf_op jit(solution)/shard_map/pallas_call | solution.py:35
  216.1 1.4 pad_maximum_fusion.2
  217.5 1.3 slice_bitcast_fusion.7
  218.9 3.2 convolution_convert_fusion
  222.2 1.3 fusion.35
  223.5 3.2 add_convert_fusion
  226.7 6.2 %pad_maximum_fusion = bf16[2,8,2,64,2048]{4,3,0,2,1:T(8,128)(2,1)} fusion(bf16[1,8,2,64,2048]{4,3,0,2,1:T(8,128)(2,1)} %bitcast.188, bf16[1,8,2,64,2048]{4,3,0,2,1:T(8,128)(2,1)S(1)} %bitcast.187), kind=kLoop, calls=%fused_computation.4 | loop fusion | flops 4194304 | bytes 16777216 | tf_op jit(solution)/shard_map/stack | solution.py:114
  233.0 0.6 copy-done.13
  233.6 0.1 copy.36
  233.7 0.3 copy-done.12
  234.0 4.5 %fusion.9 = bf16[1,2048,256]{2,1,0:T(8,128)(2,1)} fusion(bf16[8,2,64,2048]{3,2,1,0:T(8,128)(2,1)} %bitcast.194, bf16[8,2,64,256]{3,2,0,1:T(8,128)(2,1)S(1)} %copy-done.12), kind=kOutput, calls=%fused_computation.20 | convolution fusion | flops 1074266112 | bytes 5767168 | tf_op jit(solution)/shard_map/dot_general | solution.py:120
  238.5 89.7 %reduce-scatter.2.cloned.1.call-done = bf16[2,1,2,64,2048]{4,3,0,2,1:T(8,128)(2,1)} async-done(((bf16[2,8,2,64,2048]{4,3,0,2,1:T(8,128)(2,1)}), bf16[2,1,2,64,2048]{4,3,0,2,1:T(8,128)(2,1)}) %reduce-scatter.2.cloned.1.call-update) | async-done | bytes 1048592 | tf_op jit(solution)/shard_map/reduce_scatter | solution.py:57
  328.2 2.1 slice_bitcast_fusion.2
  330.3 14.3 %shard_map.113 = bf16[2,64,2048]{2,1,0:T(8,128)(2,1)} custom-call(bf16[2,64,2048]{2,1,0:T(8,128)(2,1)} %get-tuple-element.20.src_ref), custom_call_target="tpu_custom_call" | custom-call | bytes 1048576 | tf_op jit(solution)/shard_map/pallas_call | solution.py:35
  344.6 2.0 fusion.23
  346.6 2.1 copy.48
  348.7 5.3 %all-to-all-start.1 = ((bf16[2,64,4096]{2,0,1:T(2,128)(2,1)}), bf16[2,64,4096]{2,0,1:T(2,128)(2,1)S(1)}, u32[]{:S(2)}, u32[]{:S(2)}) async-start(bf16[2,64,4096]{2,0,1:T(2,128)(2,1)} %copy.48), calls=%async_computation.2 | async-start | bytes 2097152 | tf_op jit(solution)/shard_map/all_to_all | solution.py:62
  354.0 4.6 %fusion.11 = bf16[1,2048,256]{2,1,0:T(8,128)(2,1)} fusion(bf16[8,2,64,2048]{3,2,1,0:T(8,128)(2,1)} %bitcast.191, bf16[8,2,64,256]{3,2,0,1:T(8,128)(2,1)S(1)} %copy-done.11), kind=kOutput, calls=%fused_computation.22 | convolution fusion | flops 1074266112 | bytes 5767168 | tf_op jit(solution)/shard_map/dot_general | solution.py:118
  358.7 2.4 fusion.10
  361.1 8.5 %all-to-all-done.1 = bf16[2,64,4096]{2,0,1:T(2,128)(2,1)S(1)} async-done(((bf16[2,64,4096]{2,0,1:T(2,128)(2,1)}), bf16[2,64,4096]{2,0,1:T(2,128)(2,1)S(1)}, u32[]{:S(2)}, u32[]{:S(2)}) %all-to-all-start.1) | async-done | bytes 1048608 | tf_op jit(solution)/shard_map/all_to_all | solution.py:62
  369.6 0.9 convert_element_type.117
  370.5 2.8 slice_reduce_fusion
  373.2 0.3 squeeze.44
  373.5 0.3 broadcast_multiply_fusion
  373.8 0.4 reshape.407
  374.2 3.3 scatter_custom_fusion
  377.5 2.7 convert_element_type.118
  380.2 2.3 slice.65
  382.5 3.7 scatter_custom_fusion.1
  386.2 1.1 convert_element_type.119
  (30 shorter events, 0.3 us)
Async XLA Ops:
  7.2 143.6 %copy-start = (bf16[1,2048,256]{2,1,0:T(8,128)(2,1)S(1)}, bf16[1,2048,256]{2,1,0:T(8,128)(2,1)}, u32[]{:S(2)}) copy-start(bf16[1,2048,256]{2,1,0:T(8,128)(2,1)} %param.14) | copy-start | bytes 3145732
  7.2 4.6 %copy-start.3 = (bf16[128,4096]{1,0:T(8,128)(2,1)S(1)}, bf16[128,4096]{1,0:T(8,128)(2,1)}, u32[]{:S(2)}) copy-start(bf16[128,4096]{1,0:T(8,128)(2,1)} %param.9) | copy-start | bytes 3145732
  15.0 24.7 %all-to-all-start = ((bf16[2,64,4096]{2,0,1:T(2,128)(2,1)}), bf16[2,64,4096]{2,0,1:T(2,128)(2,1)S(1)}, u32[]{:S(2)}, u32[]{:S(2)}) async-start(bf16[2,64,4096]{2,0,1:T(2,128)(2,1)} %copy.38), calls=%async_computation | async-start | bytes 2097152 | tf_op jit(solution)/shard_map/all_to_all | solution.py:47
  22.1 121.2 %all-gather.3.cloned.1.call-start = ((), (), s32[]{:S(2)}) async-start(), calls=%async_computation.4 | async-start | bytes 9437184 | tf_op jit(solution)/shard_map/all_gather | solution.py:51
  55.9 91.5 %copy-start.9 = (bf16[1,2048,256]{2,1,0:T(8,128)(2,1)S(1)}, bf16[1,2048,256]{2,1,0:T(8,128)(2,1)}, u32[]{:S(2)}) copy-start(bf16[1,2048,256]{2,1,0:T(8,128)(2,1)} %param.13) | copy-start | bytes 3145732
  56.0 272.2 %reduce-scatter.2.cloned.1.call-start = ((), (), s32[]{:S(2)}) async-start(), calls=%async_computation.3 | async-start | bytes 9437184 | tf_op jit(solution)/shard_map/reduce_scatter | solution.py:57
  147.5 2.0 copy-start.5
  147.5 3.3 copy-start.7
  147.5 2.0 copy-start.8
  152.4 1.6 copy-start.4
  223.5 3.3 copy-start.2
  232.9 0.7 copy-start.13
  232.9 1.1 copy-start.12
  344.5 9.5 %copy-start.11 = (bf16[8,2,64,256]{3,2,0,1:T(8,128)(2,1)S(1)}, bf16[8,2,64,256]{3,2,0,1:T(8,128)(2,1)}, u32[]{:S(2)}) copy-start(bf16[8,2,64,256]{3,2,0,1:T(8,128)(2,1)} %get-tuple-element.9) | copy-start | bytes 1572868
  348.7 20.9 %all-to-all-start.1 = ((bf16[2,64,4096]{2,0,1:T(2,128)(2,1)}), bf16[2,64,4096]{2,0,1:T(2,128)(2,1)S(1)}, u32[]{:S(2)}, u32[]{:S(2)}) async-start(bf16[2,64,4096]{2,0,1:T(2,128)(2,1)} %copy.48), calls=%async_computation.2 | async-start | bytes 2097152 | tf_op jit(solution)/shard_map/all_to_all | solution.py:62
  354.0 4.7 %copy-start.6 = (bf16[1,16,64,2048]{3,2,0,1:T(8,128)(2,1)S(1)}, bf16[1,16,64,2048]{3,2,0,1:T(8,128)(2,1)}, u32[]{:S(2)}) copy-start(bf16[1,16,64,2048]{3,2,0,1:T(8,128)(2,1)} %copy-done.5) | copy-start | bytes 12582916
  354.0 4.7 %copy-start.10 = (bf16[8,2,64,256]{3,2,0,1:T(8,128)(2,1)S(1)}, bf16[8,2,64,256]{3,2,0,1:T(8,128)(2,1)}, u32[]{:S(2)}) copy-start(bf16[8,2,64,256]{3,2,0,1:T(8,128)(2,1)} %get-tuple-element.10) | copy-start | bytes 1572868
  380.2 7.1 %copy-start.1 = (bf16[1,2048,256]{2,1,0:T(8,128)(2,1)S(1)}, bf16[1,2048,256]{2,1,0:T(8,128)(2,1)}, u32[]{:S(2)}) copy-start(bf16[1,2048,256]{2,1,0:T(8,128)(2,1)} %param.14) | copy-start | bytes 3145732
Sparse Core Ops, SparseCore 0:
  56.1 87.1 all-gather.2
  233.1 95.0 reduce-scatter.1

commit v7 on v6

v7 whole, which is shorter than its diff:
```python
import jax
import jax.numpy as jnp
from jax import lax
from jax.experimental import pallas as pl
from jax.experimental.pallas import tpu as pltpu
from jax.sharding import Mesh
from jax.sharding import PartitionSpec as P

SPLIT = 8
CHUNKS = 2
ROWS = ("dp", "yx", "col")
MESH_ID = pl.DeviceIdType.MESH
CONTRACT_LAST = (((1,), (1,)), ((), ()))
CONTRACT_FIRST = (((0,), (0,)), ((), ()))


def swap_kernel(src_ref, dst_ref, sems):
    other = 1 - lax.axis_index("dp")
    barrier = pltpu.get_barrier_semaphore()
    pl.semaphore_signal(barrier, 1, device_id={"dp": other}, device_id_type=MESH_ID)
    pl.semaphore_wait(barrier, 1)
    copy = pltpu.make_async_remote_copy(
        src_ref=src_ref,
        dst_ref=dst_ref,
        send_sem=sems.at[0],
        recv_sem=sems.at[1],
        device_id={"dp": other},
        device_id_type=MESH_ID,
    )
    copy.start()
    copy.wait()


def swap_with_partner(x, collective_id):
    size = x.size * x.dtype.itemsize
    return pl.pallas_call(
        swap_kernel,
        out_shape=jax.ShapeDtypeStruct(x.shape, x.dtype),
        in_specs=[pl.BlockSpec(memory_space=pl.ANY)],
        out_specs=pl.BlockSpec(memory_space=pl.ANY),
        scratch_shapes=[pltpu.SemaphoreType.DMA((2,))],
        compiler_params=pltpu.CompilerParams(collective_id=collective_id, has_side_effects=True),
        cost_estimate=pl.CostEstimate(flops=0, bytes_accessed=2 * size, transcendentals=0),
    )(x)


def own_batch(partial, collective_id):
    streams, rows, k = partial.shape
    split = partial.reshape(streams, SPLIT, 2, -1, k)
    traded = swap_with_partner(split[:, :, 1], collective_id)
    return (split[:, :, 0] + traded).reshape(streams, -1, k)


def both_batches(values, collective_id):
    traded = swap_with_partner(values, collective_id)
    streams, rows, k = values.shape
    mine = values.reshape(streams, SPLIT, 1, -1, k)
    theirs = traded.reshape(streams, SPLIT, 1, -1, k)
    return jnp.concatenate([mine, theirs], axis=2).reshape(streams, -1, k)


def expert_chunk(arrived, shift, wg, wu, wd, first_id):
    half = wg.shape[0]
    rolled = jnp.roll(arrived, -shift, axis=-1)
    traded = swap_with_partner(rolled[..., half:], first_id)
    both = jnp.stack([rolled[..., :half], traded], axis=1)
    shared = lax.all_gather(both, "col", axis=1, tiled=False)
    token_rows, cot_rows = shared.reshape(2, -1, half)
    partials = jnp.stack(
        [
            jnp.dot(token_rows, wg, preferred_element_type=jnp.float32),
            jnp.dot(token_rows, wu, preferred_element_type=jnp.float32),
            jnp.dot(cot_rows, wd, preferred_element_type=jnp.float32),
        ]
    )
    gate_pre, up_pre, hidden_grad = own_batch(partials, first_id + 1)
    gate_sigma = jax.nn.sigmoid(gate_pre)
    hidden = (gate_pre * gate_sigma * up_pre).astype(jnp.bfloat16)
    gate_rows = (hidden_grad * up_pre * gate_sigma * (1.0 + gate_pre * (1.0 - gate_sigma))).astype(
        jnp.bfloat16
    )
    up_rows = (hidden_grad * gate_pre * gate_sigma).astype(jnp.bfloat16)
    hidden_all, gate_all, up_all = both_batches(jnp.stack([hidden, gate_rows, up_rows]), first_id + 2)
    partial_value = lax.dot_general(
        hidden_all, wd, CONTRACT_LAST, preferred_element_type=jnp.float32
    ).astype(jnp.bfloat16)
    partial_grad = (
        lax.dot_general(gate_all, wg, CONTRACT_LAST, preferred_element_type=jnp.float32)
        + lax.dot_general(up_all, wu, CONTRACT_LAST, preferred_element_type=jnp.float32)
    ).astype(jnp.bfloat16)
    partial_rows = jnp.stack([partial_value, partial_grad])
    summed = lax.psum_scatter(
        partial_rows.reshape(2, SPLIT, 2, -1, half), "col", scatter_dimension=1, tiled=True
    )[:, 0]
    traded_back = swap_with_partner(summed[:, 1], first_id + 3)
    rows = jnp.roll(jnp.concatenate([summed[:, 0], traded_back], axis=-1), shift, axis=-1)
    grad_terms = jnp.stack(
        [
            lax.dot_general(token_rows, gate_all, CONTRACT_FIRST, preferred_element_type=jnp.float32),
            lax.dot_general(token_rows, up_all, CONTRACT_FIRST, preferred_element_type=jnp.float32),
            lax.dot_general(cot_rows, hidden_all, CONTRACT_FIRST, preferred_element_type=jnp.float32),
        ]
    )
    return rows, grad_terms


def shards(tokens, routes, gate_values, gate_weight, up_weight, down_weight, cotangent):
    width = tokens.shape[1]
    half = gate_weight.shape[1]
    chosen = routes[0]
    scales = gate_values[0][:, :, None]
    shift = lax.axis_index("dp") * half
    wg, wu, wd = gate_weight[0], up_weight[0], down_weight[0]
    scaled_cot = (scales * cotangent[chosen].astype(jnp.float32)).astype(jnp.bfloat16)
    home_rows = jnp.stack([tokens[chosen], scaled_cot]).reshape(2, -1, width)
    arrived = lax.all_to_all(home_rows, "yx", split_axis=1, concat_axis=1, tiled=True)
    cut = arrived.shape[1] // CHUNKS
    outs = [
        expert_chunk(arrived[:, k * cut : (k + 1) * cut], shift, wg, wu, wd, 4 * k)
        for k in range(CHUNKS)
    ]
    rows = jnp.concatenate([o[0] for o in outs], axis=1)
    back = lax.all_to_all(rows, "yx", split_axis=1, concat_axis=1, tiled=True).astype(jnp.float32)
    back = back.reshape(2, chosen.shape[0], chosen.shape[1], width)
    layer_out = jnp.zeros((tokens.shape[0], width), jnp.float32).at[chosen].add(scales * back[0])
    token_grad = jnp.zeros((tokens.shape[0], width), jnp.float32).at[chosen].add(back[1])
    grads = sum(o[1] for o in outs).astype(jnp.bfloat16)
    return (
        layer_out.astype(jnp.bfloat16),
        token_grad.astype(jnp.bfloat16),
        grads[0][None],
        grads[1][None],
        grads[2][None],
    )


def solution(mesh):
    n_dp, n_expert = mesh.devices.shape
    fine = Mesh(mesh.devices.reshape(n_dp, n_expert // SPLIT, SPLIT), ROWS)
    placed = (
        P(ROWS, None),
        P(ROWS, None, None),
        P(ROWS, None, None),
        P(("yx", "col"), "dp", None),
        P(("yx", "col"), "dp", None),
        P(("yx", "col"), "dp", None),
        P(ROWS, None),
    )
    return jax.shard_map(
        shards,
        mesh=fine,
        in_specs=placed,
        out_specs=(
            P(ROWS, None),
            P(ROWS, None),
            P(("yx", "col"), "dp", None),
            P(("yx", "col"), "dp", None),
            P(("yx", "col"), "dp", None),
        ),
        check_vma=False,
    )
```

time: 400 us -> 387 us (0.968)
  waiting for transfers between devices: 203 us -> 108 us
  Pallas kernels: 82.4 us -> 149 us
  local copies, waits for them, and re-layouts: 28.5 us -> 38.1 us
  starting transfers between devices: 12.5 us -> 16.9 us
    pallas_call x4 -> x8, Pallas kernels: 82.4 us -> 149 us  [swap_with_partner(): pl.pallas_call(swap_kernel, out_shape=jax.ShapeDtypeStruct(x.shape, x.dty...]
    reduce_scatter x1 -> x2, waiting for transfers between devices: 89.7 us -> 36.6 us  [expert_chunk(): lax.psum_scatter(partial_rows.reshape(2, SPLIT, 2, -1, half), 'col', scat...]
    all_gather x1 -> x2, waiting for transfers between devices: 87.3 us -> 41.7 us  [expert_chunk(): shared = lax.all_gather(both, 'col', axis=1, tiled=False)]
    another operation x6 -> x14, local copies, waits for them, and re-layouts: 2.36 us -> 9.13 us  [the longest x2 5.46 us: expert_chunk(): token_rows, cot_rows = shared.reshape(2, -1, half)]
    dot_general x9 -> x18, matrix products: 23.1 us -> 21.8 us  [the longest x2 4.58 us: expert_chunk(): lax.dot_general(cot_rows, hidden_all, CONTRACT_FIRST, preferred_element_t...]
    another operation x4 -> x8, other arithmetic: 9.62 us -> 10.2 us  [the longest x2 4.73 us: expert_chunk(): partial_rows = jnp.stack([partial_value, partial_grad])]
  transfers between devices with their start and end apart: 4 -> 6, of which waited for: 4 -> 4; matrix products, arithmetic and copies ran while one was open for 3% -> 14% of each run, Pallas kernels for 0% -> 35%
where the time goes in v7:
time: 387 us; the launch traced here: 382 us
  Pallas kernels  149 us (39%)
  waiting for transfers between devices  108 us (28%)
  local copies, waits for them, and re-layouts  38.1 us (10%)
  other arithmetic  33.5 us (9%)
  matrix products  21.8 us (6%)
  starting transfers between devices  16.9 us (4%)
  between operations  14.6 us (4%)
    pallas_call x8, Pallas kernels, swap_with_partner(): pl.pallas_call(swap_kernel, out_shape=jax.ShapeDtypeStruct(x.shape, x.dty...  149 us
    all_gather x2, waiting for transfers between devices, expert_chunk(): shared = lax.all_gather(both, 'col', axis=1, tiled=False)  41.7 us
    reduce_scatter x2, waiting for transfers between devices, expert_chunk(): lax.psum_scatter(partial_rows.reshape(2, SPLIT, 2, -1, half), 'col', scat...  36.6 us
    all_to_all x1, waiting for transfers between devices, shards(): lax.all_to_all(home_rows, 'yx', split_axis=1, concat_axis=1, tiled=True)  17.6 us
    all_to_all x1, waiting for transfers between devices, shards(): lax.all_to_all(rows, 'yx', split_axis=1, concat_axis=1, tiled=True)  11.7 us
    all_to_all x1, starting transfers between devices, shards(): lax.all_to_all(rows, 'yx', split_axis=1, concat_axis=1, tiled=True)  8.97 us
  transfers between devices with their start and end apart: 6, of which 4 were waited for; matrix products, arithmetic and copies ran while one was open for 14% of the time, Pallas kernels for 35%

profile of v7, /device:TPU:32, one launch (start us, length us, event | category | flops | bytes accessed | tf_op | source)
XLA Modules:
  0.0 381.9 jit_solution(4395935436843649192)
XLA Ops:
  7.2 0.8 compare_select_fusion
  8.1 0.8 copy.52
  9.0 2.8 gather_fusion.1
  11.8 0.9 gather_fusion
  13.0 2.1 copy.53
  15.0 7.0 %all-to-all-start = ((bf16[2,64,4096]{2,0,1:T(2,128)(2,1)}), bf16[2,64,4096]{2,0,1:T(2,128)(2,1)S(1)}, u32[]{:S(2)}, u32[]{:S(2)}) async-start(bf16[2,64,4096]{2,0,1:T(2,128)(2,1)} %copy.53), calls=%async_computation | async-start | bytes 2097152 | tf_op jit(solution)/shard_map/all_to_all | solution.py:116
  22.2 17.6 %all-to-all-done = bf16[2,64,4096]{2,0,1:T(2,128)(2,1)S(1)} async-done(((bf16[2,64,4096]{2,0,1:T(2,128)(2,1)}), bf16[2,64,4096]{2,0,1:T(2,128)(2,1)S(1)}, u32[]{:S(2)}, u32[]{:S(2)}) %all-to-all-start) | async-done | bytes 1048608 | tf_op jit(solution)/shard_map/all_to_all | solution.py:116
  39.7 0.8 fusion.111
  41.1 0.7 slice_bitcast_fusion.9
  41.9 6.7 %shard_map.110 = bf16[2,32,2048]{2,1,0:T(8,128)(2,1)} custom-call(bf16[2,32,2048]{2,1,0:T(8,128)(2,1)} %get-tuple-element.45.src_ref), custom_call_target="tpu_custom_call" | custom-call | bytes 524288 | tf_op jit(solution)/shard_map/pallas_call | solution.py:36
  48.6 1.8 pad_maximum_fusion.8
  51.1 0.7 slice_bitcast_fusion.6
  51.8 6.7 %shard_map.114 = bf16[2,32,2048]{2,1,0:T(8,128)(2,1)} custom-call(bf16[2,32,2048]{2,1,0:T(8,128)(2,1)} %get-tuple-element.52.src_ref), custom_call_target="tpu_custom_call" | custom-call | bytes 524288 | tf_op jit(solution)/shard_map/pallas_call | solution.py:36
  58.5 1.8 pad_maximum_fusion.9
  60.7 41.7 %all-gather.5.cloned.1.call-done = bf16[2,16,32,2048]{3,2,0,1:T(8,128)(2,1)} async-done(((bf16[2,2,32,2048]{3,2,0,1:T(8,128)(2,1)}), bf16[2,16,32,2048]{3,2,0,1:T(8,128)(2,1)}) %all-gather.5.cloned.1.call-update) | async-done | bytes 4194320 | tf_op jit(solution)/shard_map/all_gather | solution.py:67
  102.4 2.7 fusion.108
  108.8 0.9 slice_bitcast_fusion.2.src_ref
  109.8 48.4 %shard_map.111 = f32[3,8,32,256]{3,2,1,0:T(8,128)} custom-call(f32[3,8,32,256]{3,2,1,0:T(8,128)} %slice_bitcast_fusion.2.src_ref), custom_call_target="tpu_custom_call" | custom-call | bytes 1572864 | tf_op jit(solution)/shard_map/pallas_call | solution.py:36
  158.2 1.3 fusion.53
  159.7 0.8 pad_maximum_fusion.10.src_ref
  160.5 11.5 %shard_map.112 = bf16[3,256,256]{2,1,0:T(8,128)(2,1)} custom-call(bf16[3,256,256]{2,1,0:T(8,128)(2,1)} %pad_maximum_fusion.10.src_ref), custom_call_target="tpu_custom_call" | custom-call | bytes 786432 | tf_op jit(solution)/shard_map/pallas_call | solution.py:36
  172.1 1.1 pad_maximum_fusion.6
  173.2 1.0 slice_bitcast_fusion.14
  174.3 0.7 convolution_convert_fusion.1
  175.5 0.7 fusion.45
  176.7 0.7 add_convert_fusion.1
  177.4 2.3 pad_maximum_fusion
  180.3 2.7 fusion.109
  186.0 0.9 slice_bitcast_fusion.src_ref
  187.0 35.6 %shard_map.115 = f32[3,8,32,256]{3,2,1,0:T(8,128)} custom-call(f32[3,8,32,256]{3,2,1,0:T(8,128)} %slice_bitcast_fusion.src_ref), custom_call_target="tpu_custom_call" | custom-call | bytes 1572864 | tf_op jit(solution)/shard_map/pallas_call | solution.py:36
  222.6 1.2 fusion.52
  224.1 0.8 pad_maximum_fusion.11.src_ref
  224.9 18.9 %shard_map.116 = bf16[3,256,256]{2,1,0:T(8,128)(2,1)} custom-call(bf16[3,256,256]{2,1,0:T(8,128)(2,1)} %pad_maximum_fusion.11.src_ref), custom_call_target="tpu_custom_call" | custom-call | bytes 786432 | tf_op jit(solution)/shard_map/pallas_call | solution.py:36
  243.9 1.1 pad_maximum_fusion.7
  245.0 1.0 slice_bitcast_fusion.11
  246.1 0.7 convolution_convert_fusion
  247.3 0.7 fusion.47
  248.5 0.8 add_convert_fusion
  249.3 2.4 pad_maximum_fusion.1
  252.6 2.5 convolution_bitcast_fusion.3
  255.2 2.1 convolution_bitcast_fusion.4
  257.3 2.1 convolution_bitcast_fusion.5
  259.5 2.1 convolution_bitcast_fusion
  261.5 2.1 convolution_bitcast_fusion.1
  263.6 2.1 convolution_bitcast_fusion.2
  265.7 1.8 slice_bitcast_fusion.7
  267.5 12.2 %shard_map.113 = bf16[2,32,2048]{2,1,0:T(8,128)(2,1)} custom-call(bf16[2,32,2048]{2,1,0:T(8,128)(2,1)} %get-tuple-element.39.src_ref), custom_call_target="tpu_custom_call" | custom-call | bytes 524288 | tf_op jit(solution)/shard_map/pallas_call | solution.py:36
  279.7 36.6 %reduce-scatter.5.cloned.1.call-done = bf16[2,1,2,32,2048]{4,3,0,2,1:T(8,128)(2,1)} async-done(((bf16[2,8,2,32,2048]{4,3,0,2,1:T(8,128)(2,1)}), bf16[2,1,2,32,2048]{4,3,0,2,1:T(8,128)(2,1)}) %reduce-scatter.5.cloned.1.call-update) | async-done | bytes 524304 | tf_op jit(solution)/shard_map/reduce_scatter | solution.py:92
  316.3 1.8 slice_bitcast_fusion.4
  318.1 9.3 %shard_map.117 = bf16[2,32,2048]{2,1,0:T(8,128)(2,1)} custom-call(bf16[2,32,2048]{2,1,0:T(8,128)(2,1)} %get-tuple-element.46.src_ref), custom_call_target="tpu_custom_call" | custom-call | bytes 524288 | tf_op jit(solution)/shard_map/pallas_call | solution.py:36
  327.4 1.8 fusion.55
  329.2 2.2 copy.69
  331.4 9.0 %all-to-all-start.1 = ((bf16[2,64,4096]{2,0,1:T(2,128)(2,1)}), bf16[2,64,4096]{2,0,1:T(2,128)(2,1)S(1)}, u32[]{:S(2)}, u32[]{:S(2)}) async-start(bf16[2,64,4096]{2,0,1:T(2,128)(2,1)} %copy.69), calls=%async_computation.3 | async-start | bytes 2097152 | tf_op jit(solution)/shard_map/all_to_all | solution.py:123
  340.4 4.4 %fusion = bf16[3,2048,256]{2,1,0:T(8,128)(2,1)S(1)} fusion(f32[1,2048,256]{2,1,0:T(8,128)S(1)} %convolution_bitcast_fusion.3, f32[1,2048,256]{2,1,0:T(8,128)} %convolution_bitcast_fusion.4, f32[1,2048,256]{2,1,0:T(8,128)} %convolution_bitcast_fusion.5, f32[1,2048,256]{2,1,0:T(8,128)} %convolution_bitcast_fusion, ...), kind=kLoop, calls=%fused_computation.5 | loop fusion | flops 9437184 | bytes 15728640 | tf_op jit(solution)/shard_map/convert_element_type | solution.py:127
  344.8 1.7 fusion.110
  346.5 11.7 %all-to-all-done.1 = bf16[2,64,4096]{2,0,1:T(2,128)(2,1)S(1)} async-done(((bf16[2,64,4096]{2,0,1:T(2,128)(2,1)}), bf16[2,64,4096]{2,0,1:T(2,128)(2,1)S(1)}, u32[]{:S(2)}, u32[]{:S(2)}) %all-to-all-start.1) | async-done | bytes 1048608 | tf_op jit(solution)/shard_map/all_to_all | solution.py:123
  358.2 0.9 convert_element_type.182
  359.1 2.8 slice_reduce_fusion
  362.4 1.3 reshape.703
  363.8 3.1 scatter_custom_fusion
  366.9 1.1 convert_element_type.183
  368.0 2.3 slice.121
  370.3 3.8 scatter_custom_fusion.1
  374.1 1.1 convert_element_type.184
  (88 shorter events, 13.5 us)
Async XLA Ops:
  7.2 100.8 %copy-start = (bf16[1,2048,256]{2,1,0:T(8,128)(2,1)S(1)}, bf16[1,2048,256]{2,1,0:T(8,128)(2,1)}, u32[]{:S(2)}) copy-start(bf16[1,2048,256]{2,1,0:T(8,128)(2,1)} %param.14) | copy-start | bytes 3145732
  9.0 2.8 copy-start.2
  15.0 24.7 %all-to-all-start = ((bf16[2,64,4096]{2,0,1:T(2,128)(2,1)}), bf16[2,64,4096]{2,0,1:T(2,128)(2,1)S(1)}, u32[]{:S(2)}, u32[]{:S(2)}) async-start(bf16[2,64,4096]{2,0,1:T(2,128)(2,1)} %copy.53), calls=%async_computation | async-start | bytes 2097152 | tf_op jit(solution)/shard_map/all_to_all | solution.py:116
  22.1 80.3 %all-gather.5.cloned.1.call-start = ((), (), s32[]{:S(2)}) async-start(), calls=%async_computation.6 | async-start | bytes 4718592 | tf_op jit(solution)/shard_map/all_gather | solution.py:67
  50.4 129.9 %all-gather.7.cloned.1.call-start = ((), (), s32[]{:S(2)}) async-start(), calls=%async_computation.7 | async-start | bytes 4718592 | tf_op jit(solution)/shard_map/all_gather | solution.py:67
  60.3 44.8 %copy-start.3 = (bf16[1,2048,256]{2,1,0:T(8,128)(2,1)S(1)}, bf16[1,2048,256]{2,1,0:T(8,128)(2,1)}, u32[]{:S(2)}) copy-start(bf16[1,2048,256]{2,1,0:T(8,128)(2,1)} %param.12) | copy-start | bytes 3145732
  60.4 205.3 %reduce-scatter.3.cloned.1.call-start = ((), (), s32[]{:S(2)}) async-start(), calls=%async_computation.4 | async-start | bytes 4718592 | tf_op jit(solution)/shard_map/reduce_scatter | solution.py:92
  105.1 1.4 copy-start.9
  105.1 2.8 copy-start.11
  105.1 2.0 copy-start.6
  174.2 1.2 copy-start.4
  175.4 1.2 copy-start.7
  179.8 136.5 %reduce-scatter.5.cloned.1.call-start = ((), (), s32[]{:S(2)}) async-start(), calls=%async_computation.5 | async-start | bytes 4718592 | tf_op jit(solution)/shard_map/reduce_scatter | solution.py:92
  183.1 1.3 copy-start.12
  183.1 2.0 copy-start.14
  246.1 1.2 copy-start.5
  247.3 1.2 copy-start.8
  251.7 0.7 copy-start.21
  251.7 1.0 copy-start.18
  252.6 2.5 copy-start.10
  252.6 2.5 copy-start.17
  255.2 2.1 copy-start.16
  257.3 2.1 copy-start.15
  257.3 2.1 copy-start.20
  259.4 2.1 copy-start.13
  259.4 2.1 copy-start.19
  331.4 26.8 %all-to-all-start.1 = ((bf16[2,64,4096]{2,0,1:T(2,128)(2,1)}), bf16[2,64,4096]{2,0,1:T(2,128)(2,1)S(1)}, u32[]{:S(2)}, u32[]{:S(2)}) async-start(bf16[2,64,4096]{2,0,1:T(2,128)(2,1)} %copy.69), calls=%async_computation.3 | async-start | bytes 2097152 | tf_op jit(solution)/shard_map/all_to_all | solution.py:123
  370.3 4.9 %copy-start.1 = (bf16[1,2048,256]{2,1,0:T(8,128)(2,1)S(1)}, bf16[1,2048,256]{2,1,0:T(8,128)(2,1)}, u32[]{:S(2)}) copy-start(bf16[1,2048,256]{2,1,0:T(8,128)(2,1)} %param.14) | copy-start | bytes 3145732
Sparse Core Ops, SparseCore 0:
  50.5 51.7 all-gather.4
  104.8 62.8 all-gather.6
  179.9 74.5 reduce-scatter.2
  256.9 59.3 reduce-scatter.4

commit v8 on v7

--- a/solution.py
+++ b/solution.py
@@ -112,19 +112,22 @@
     shift = lax.axis_index("dp") * half
     wg, wu, wd = gate_weight[0], up_weight[0], down_weight[0]
     scaled_cot = (scales * cotangent[chosen].astype(jnp.float32)).astype(jnp.bfloat16)
-    home_rows = jnp.stack([tokens[chosen], scaled_cot]).reshape(2, -1, width)
-    arrived = lax.all_to_all(home_rows, "yx", split_axis=1, concat_axis=1, tiled=True)
-    cut = arrived.shape[1] // CHUNKS
-    outs = [
-        expert_chunk(arrived[:, k * cut : (k + 1) * cut], shift, wg, wu, wd, 4 * k)
-        for k in range(CHUNKS)
-    ]
-    rows = jnp.concatenate([o[0] for o in outs], axis=1)
-    back = lax.all_to_all(rows, "yx", split_axis=1, concat_axis=1, tiled=True).astype(jnp.float32)
-    back = back.reshape(2, chosen.shape[0], chosen.shape[1], width)
+    home_rows = jnp.stack([tokens[chosen], scaled_cot])
+    experts, slots = chosen.shape
+    cut = slots // CHUNKS
+    backs = []
+    grads = 0.0
+    for k in range(CHUNKS):
+        chunk = home_rows[:, :, k * cut : (k + 1) * cut].reshape(2, -1, width)
+        arrived = lax.all_to_all(chunk, "yx", split_axis=1, concat_axis=1, tiled=True)
+        rows, grad_terms = expert_chunk(arrived, shift, wg, wu, wd, 4 * k)
+        back = lax.all_to_all(rows, "yx", split_axis=1, concat_axis=1, tiled=True)
+        backs.append(back.reshape(2, experts, cut, width))
+        grads = grads + grad_terms
+    back = jnp.concatenate(backs, axis=2).astype(jnp.float32)
+    grads = grads.astype(jnp.bfloat16)
     layer_out = jnp.zeros((tokens.shape[0], width), jnp.float32).at[chosen].add(scales * back[0])
     token_grad = jnp.zeros((tokens.shape[0], width), jnp.float32).at[chosen].add(back[1])
-    grads = sum(o[1] for o in outs).astype(jnp.bfloat16)
     return (
         layer_out.astype(jnp.bfloat16),
         token_grad.astype(jnp.bfloat16),

time: 387 us -> 388 us (level)
  matrix products: 21.8 us -> 13.2 us
  starting transfers between devices: 16.9 us -> 24.9 us
  local copies, waits for them, and re-layouts: 38.1 us -> 45.2 us
  Pallas kernels: 149 us -> 142 us
    all_to_all x2 -> x4, starting transfers between devices: 16 us -> 24.3 us  [the longest x2 13.7 us: shards(): back = lax.all_to_all(rows, 'yx', split_axis=1, concat_axis=1, tiled=True)]
    pallas_call x8, Pallas kernels: 149 us -> 142 us  [swap_with_partner(): pl.pallas_call(swap_kernel, out_shape=jax.ShapeDtypeStruct(x.shape, x.dty...]
    unnamed x47 -> x42, local copies, waits for them, and re-layouts: 5.95 us -> 8.07 us
    all_to_all x2 -> x4, waiting for transfers between devices: 29.3 us -> 29.7 us  [the longest x2 20.3 us: shards(): lax.all_to_all(chunk, 'yx', split_axis=1, concat_axis=1, tiled=True)]
  transfers between devices with their start and end apart: 6 -> 8, of which waited for: 4 -> 5; matrix products, arithmetic and copies ran while one was open for 14% -> 13% of each run, Pallas kernels for 35% -> 35%
where the time goes in v8:
time: 388 us; the launch traced here: 383 us
  Pallas kernels  142 us (37%)
  waiting for transfers between devices  108 us (28%)
  local copies, waits for them, and re-layouts  45.2 us (12%)
  other arithmetic  34.7 us (9%)
  starting transfers between devices  24.9 us (6%)
  between operations  14.4 us (4%)
  matrix products  13.2 us (3%)
    pallas_call x8, Pallas kernels, swap_with_partner(): pl.pallas_call(swap_kernel, out_shape=jax.ShapeDtypeStruct(x.shape, x.dty...  142 us
    all_gather x2, waiting for transfers between devices, expert_chunk(): shared = lax.all_gather(both, 'col', axis=1, tiled=False)  41.3 us
    reduce_scatter x2, waiting for transfers between devices, expert_chunk(): lax.psum_scatter(partial_rows.reshape(2, SPLIT, 2, -1, half), 'col', scat...  37.1 us
    all_to_all x2, waiting for transfers between devices, shards(): lax.all_to_all(chunk, 'yx', split_axis=1, concat_axis=1, tiled=True)  20.3 us
    all_to_all x2, starting transfers between devices, shards(): back = lax.all_to_all(rows, 'yx', split_axis=1, concat_axis=1, tiled=True)  13.7 us
    all_to_all x2, starting transfers between devices, shards(): lax.all_to_all(chunk, 'yx', split_axis=1, concat_axis=1, tiled=True)  10.6 us
    all_to_all x2, waiting for transfers between devices, shards(): back = lax.all_to_all(rows, 'yx', split_axis=1, concat_axis=1, tiled=True)  9.39 us
    unnamed x42, local copies, waits for them, and re-layouts  8.07 us
  transfers between devices with their start and end apart: 8, of which 5 were waited for; matrix products, arithmetic and copies ran while one was open for 13% of the time, Pallas kernels for 35%

profile of v8, /device:TPU:32, one launch (start us, length us, event | category | flops | bytes accessed | tf_op | source)
XLA Modules:
  0.0 382.6 jit_solution(7099874979521975824)
XLA Ops:
  7.2 0.8 compare_select_fusion
  8.2 3.6 gather_fusion.1
  11.8 1.4 reshape.662
  13.3 1.7 gather_fusion
  14.9 2.0 stack.95
  17.2 2.4 fusion.59
  19.6 1.4 copy.53
  21.0 7.0 %all-to-all-start = ((bf16[2,32,4096]{2,0,1:T(2,128)(2,1)}), bf16[2,32,4096]{2,0,1:T(2,128)(2,1)S(1)}, u32[]{:S(2)}, u32[]{:S(2)}) async-start(bf16[2,32,4096]{2,0,1:T(2,128)(2,1)} %bitcast.2), calls=%async_computation | async-start | bytes 1048576 | tf_op jit(solution)/shard_map/all_to_all | solution.py:122
  28.0 1.4 copy.63
  29.4 10.1 %all-to-all-done = bf16[2,32,4096]{2,0,1:T(2,128)(2,1)S(1)} async-done(((bf16[2,32,4096]{2,0,1:T(2,128)(2,1)}), bf16[2,32,4096]{2,0,1:T(2,128)(2,1)S(1)}, u32[]{:S(2)}, u32[]{:S(2)}) %all-to-all-start) | async-done | bytes 524320 | tf_op jit(solution)/shard_map/all_to_all | solution.py:122
  39.6 3.6 all-to-all-start.2
  43.5 10.1 %all-to-all-done.2 = bf16[2,32,4096]{2,0,1:T(2,128)(2,1)S(1)} async-done(((bf16[2,32,4096]{2,0,1:T(2,128)(2,1)}), bf16[2,32,4096]{2,0,1:T(2,128)(2,1)S(1)}, u32[]{:S(2)}, u32[]{:S(2)}) %all-to-all-start.2) | async-done | bytes 524320 | tf_op jit(solution)/shard_map/all_to_all | solution.py:122
  54.5 0.7 slice_bitcast_fusion.9
  55.3 6.7 %shard_map.110 = bf16[2,32,2048]{2,1,0:T(8,128)(2,1)} custom-call(bf16[2,32,2048]{2,1,0:T(8,128)(2,1)} %get-tuple-element.47.src_ref), custom_call_target="tpu_custom_call" | custom-call | bytes 524288 | tf_op jit(solution)/shard_map/pallas_call | solution.py:36
  62.0 1.8 pad_maximum_fusion.7
  63.8 0.7 slice_bitcast_fusion.6
  64.6 6.7 %shard_map.114 = bf16[2,32,2048]{2,1,0:T(8,128)(2,1)} custom-call(bf16[2,32,2048]{2,1,0:T(8,128)(2,1)} %get-tuple-element.54.src_ref), custom_call_target="tpu_custom_call" | custom-call | bytes 524288 | tf_op jit(solution)/shard_map/pallas_call | solution.py:36
  71.3 1.8 pad_maximum_fusion.8
  73.4 41.3 %all-gather.5.cloned.1.call-done = bf16[2,16,32,2048]{3,2,0,1:T(8,128)(2,1)} async-done(((bf16[2,2,32,2048]{3,2,0,1:T(8,128)(2,1)}), bf16[2,16,32,2048]{3,2,0,1:T(8,128)(2,1)}) %all-gather.5.cloned.1.call-update) | async-done | bytes 4194320 | tf_op jit(solution)/shard_map/all_gather | solution.py:67
  114.6 2.7 fusion.106
  121.1 0.9 slice_bitcast_fusion.2.src_ref
  122.0 48.4 %shard_map.111 = f32[3,8,32,256]{3,2,1,0:T(8,128)} custom-call(f32[3,8,32,256]{3,2,1,0:T(8,128)} %slice_bitcast_fusion.2.src_ref), custom_call_target="tpu_custom_call" | custom-call | bytes 1572864 | tf_op jit(solution)/shard_map/pallas_call | solution.py:36
  170.4 1.2 fusion.50
  171.9 0.8 pad_maximum_fusion.9.src_ref
  172.7 11.5 %shard_map.112 = bf16[3,256,256]{2,1,0:T(8,128)(2,1)} custom-call(bf16[3,256,256]{2,1,0:T(8,128)(2,1)} %pad_maximum_fusion.9.src_ref), custom_call_target="tpu_custom_call" | custom-call | bytes 786432 | tf_op jit(solution)/shard_map/pallas_call | solution.py:36
  184.4 1.1 pad_maximum_fusion.4
  185.4 1.0 slice_bitcast_fusion.14
  188.9 0.8 add_convert_fusion.1
  189.7 2.3 pad_maximum_fusion
  192.3 2.7 fusion.107
  198.0 0.9 slice_bitcast_fusion.src_ref
  199.0 35.5 %shard_map.115 = f32[3,8,32,256]{3,2,1,0:T(8,128)} custom-call(f32[3,8,32,256]{3,2,1,0:T(8,128)} %slice_bitcast_fusion.src_ref), custom_call_target="tpu_custom_call" | custom-call | bytes 1572864 | tf_op jit(solution)/shard_map/pallas_call | solution.py:36
  234.5 1.2 fusion.49
  236.0 0.8 pad_maximum_fusion.10.src_ref
  236.7 18.8 %shard_map.116 = bf16[3,256,256]{2,1,0:T(8,128)(2,1)} custom-call(bf16[3,256,256]{2,1,0:T(8,128)(2,1)} %pad_maximum_fusion.10.src_ref), custom_call_target="tpu_custom_call" | custom-call | bytes 786432 | tf_op jit(solution)/shard_map/pallas_call | solution.py:36
  255.7 1.1 pad_maximum_fusion.5
  260.3 2.4 pad_maximum_fusion.1
  262.7 1.5 copy-done.12
  265.0 0.9 copy-done.10
  267.6 0.8 copy-done.16
  269.2 0.8 copy-done.14
  271.6 1.0 fusion
  272.6 1.8 slice_bitcast_fusion.7
  274.4 6.7 %shard_map.113 = bf16[2,32,2048]{2,1,0:T(8,128)(2,1)} custom-call(bf16[2,32,2048]{2,1,0:T(8,128)(2,1)} %get-tuple-element.41.src_ref), custom_call_target="tpu_custom_call" | custom-call | bytes 524288 | tf_op jit(solution)/shard_map/pallas_call | solution.py:36
  281.1 1.4 fusion.56
  282.4 1.3 copy.62
  283.8 7.4 %all-to-all-start.1 = ((bf16[2,32,4096]{2,0,1:T(2,128)(2,1)}), bf16[2,32,4096]{2,0,1:T(2,128)(2,1)}, u32[]{:S(2)}, u32[]{:S(2)}) async-start(bf16[2,32,4096]{2,0,1:T(2,128)(2,1)} %copy.62), calls=%async_computation.2 | async-start | bytes 1048576 | tf_op jit(solution)/shard_map/all_to_all | solution.py:124
  291.1 37.1 %reduce-scatter.5.cloned.1.call-done = bf16[2,1,2,32,2048]{4,3,0,2,1:T(8,128)(2,1)} async-done(((bf16[2,8,2,32,2048]{4,3,0,2,1:T(8,128)(2,1)}), bf16[2,1,2,32,2048]{4,3,0,2,1:T(8,128)(2,1)}) %reduce-scatter.5.cloned.1.call-update) | async-done | bytes 524304 | tf_op jit(solution)/shard_map/reduce_scatter | solution.py:92
  328.2 1.8 slice_bitcast_fusion.4
  330.0 7.6 %shard_map.117 = bf16[2,32,2048]{2,1,0:T(8,128)(2,1)} custom-call(bf16[2,32,2048]{2,1,0:T(8,128)(2,1)} %get-tuple-element.48.src_ref), custom_call_target="tpu_custom_call" | custom-call | bytes 524288 | tf_op jit(solution)/shard_map/pallas_call | solution.py:36
  337.6 1.3 fusion.52
  339.0 1.3 copy.73
  340.3 6.3 %all-to-all-start.3 = ((bf16[2,32,4096]{2,0,1:T(2,128)(2,1)}), bf16[2,32,4096]{2,0,1:T(2,128)(2,1)}, u32[]{:S(2)}, u32[]{:S(2)}) async-start(bf16[2,32,4096]{2,0,1:T(2,128)(2,1)} %copy.73), calls=%async_computation.5 | async-start | bytes 1048576 | tf_op jit(solution)/shard_map/all_to_all | solution.py:124
  346.6 1.7 fusion.108
  348.4 9.4 %all-to-all-done.3 = bf16[2,32,4096]{2,0,1:T(2,128)(2,1)} async-done(((bf16[2,32,4096]{2,0,1:T(2,128)(2,1)}), bf16[2,32,4096]{2,0,1:T(2,128)(2,1)}, u32[]{:S(2)}, u32[]{:S(2)}) %all-to-all-start.3) | async-done | bytes 524320 | tf_op jit(solution)/shard_map/all_to_all | solution.py:124
  357.8 2.3 maximum_convert_fusion
  360.0 4.0 %slice_reduce_fusion = (f32[16,4,4096]{2,1,0:T(4,128)S(1)}, f32[1,16,4,4096]{3,0,2,1:T(1,128)S(1)}) fusion(f32[2,16,4,4096]{3,0,2,1:T(2,128)S(1)} %maximum_convert_fusion), kind=kLoop, calls=%fused_computation.38 | loop fusion | bytes 4194304 | tf_op jit(solution)/shard_map/slice | solution.py:130
  364.0 0.8 bitcast_multiply_fusion
  364.9 1.3 reshape.683
  366.2 3.1 scatter_custom_fusion
  369.3 1.1 convert_element_type.181
  370.4 1.3 reshape.691
  371.8 3.2 scatter_custom_fusion.1
  374.9 1.1 convert_element_type.182
  (89 shorter events, 20.2 us)
Async XLA Ops:
  7.2 113.0 %copy-start = (bf16[1,2048,256]{2,1,0:T(8,128)(2,1)S(1)}, bf16[1,2048,256]{2,1,0:T(8,128)(2,1)}, u32[]{:S(2)}) copy-start(bf16[1,2048,256]{2,1,0:T(8,128)(2,1)} %param.14) | copy-start | bytes 3145732
  8.1 5.0 %copy-start.20 = (f32[1,16,4]{1,2,0:T(4,128)S(1)}, f32[1,16,4]{1,2,0:T(4,128)}, u32[]{:S(2)}) copy-start(f32[1,16,4]{1,2,0:T(4,128)} %param.11) | copy-start | bytes 772
  8.2 5.1 %copy-start.2 = (bf16[128,4096]{1,0:T(8,128)(2,1)S(1)}, bf16[128,4096]{1,0:T(8,128)(2,1)}, u32[]{:S(2)}) copy-start(bf16[128,4096]{1,0:T(8,128)(2,1)} %param.9) | copy-start | bytes 3145732
  21.0 18.6 %all-to-all-start = ((bf16[2,32,4096]{2,0,1:T(2,128)(2,1)}), bf16[2,32,4096]{2,0,1:T(2,128)(2,1)S(1)}, u32[]{:S(2)}, u32[]{:S(2)}) async-start(bf16[2,32,4096]{2,0,1:T(2,128)(2,1)} %bitcast.2), calls=%async_computation | async-start | bytes 1048576 | tf_op jit(solution)/shard_map/all_to_all | solution.py:122
  39.6 14.1 %all-to-all-start.2 = ((bf16[2,32,4096]{2,0,1:T(2,128)(2,1)}), bf16[2,32,4096]{2,0,1:T(2,128)(2,1)S(1)}, u32[]{:S(2)}, u32[]{:S(2)}) async-start(bf16[2,32,4096]{2,0,1:T(2,128)(2,1)} %bitcast.34), calls=%async_computation.3 | async-start | bytes 1048576 | tf_op jit(solution)/shard_map/all_to_all | solution.py:122
  43.1 71.5 %all-gather.5.cloned.1.call-start = ((), (), s32[]{:S(2)}) async-start(), calls=%async_computation.8 | async-start | bytes 4718592 | tf_op jit(solution)/shard_map/all_gather | solution.py:67
  63.8 128.5 %all-gather.7.cloned.1.call-start = ((), (), s32[]{:S(2)}) async-start(), calls=%async_computation.9 | async-start | bytes 4718592 | tf_op jit(solution)/shard_map/all_gather | solution.py:67
  73.1 44.3 %copy-start.3 = (bf16[1,2048,256]{2,1,0:T(8,128)(2,1)S(1)}, bf16[1,2048,256]{2,1,0:T(8,128)(2,1)}, u32[]{:S(2)}) copy-start(bf16[1,2048,256]{2,1,0:T(8,128)(2,1)} %param.12) | copy-start | bytes 3145732
  73.1 199.4 %reduce-scatter.3.cloned.1.call-start = ((), (), s32[]{:S(2)}) async-start(), calls=%async_computation.6 | async-start | bytes 4718592 | tf_op jit(solution)/shard_map/reduce_scatter | solution.py:92
  117.4 1.3 copy-start.9
  117.4 2.8 copy-start.11
  117.4 2.0 copy-start.6
  186.5 1.2 copy-start.4
  187.7 1.2 copy-start.7
  192.0 136.2 %reduce-scatter.5.cloned.1.call-start = ((), (), s32[]{:S(2)}) async-start(), calls=%async_computation.7 | async-start | bytes 4718592 | tf_op jit(solution)/shard_map/reduce_scatter | solution.py:92
  195.1 1.3 copy-start.13
  195.1 2.0 copy-start.15
  257.1 1.2 copy-start.5
  258.3 1.2 copy-start.8
  262.7 1.6 copy-start.12
  262.7 1.6 copy-start.19
  264.3 1.6 copy-start.10
  264.3 1.6 copy-start.18
  265.9 1.0 copy-start.17
  266.9 1.6 copy-start.16
  268.5 1.6 copy-start.14
  283.8 56.5 %all-to-all-start.1 = ((bf16[2,32,4096]{2,0,1:T(2,128)(2,1)}), bf16[2,32,4096]{2,0,1:T(2,128)(2,1)}, u32[]{:S(2)}, u32[]{:S(2)}) async-start(bf16[2,32,4096]{2,0,1:T(2,128)(2,1)} %copy.62), calls=%async_computation.2 | async-start | bytes 1048576 | tf_op jit(solution)/shard_map/all_to_all | solution.py:124
  340.3 17.5 %all-to-all-start.3 = ((bf16[2,32,4096]{2,0,1:T(2,128)(2,1)}), bf16[2,32,4096]{2,0,1:T(2,128)(2,1)}, u32[]{:S(2)}, u32[]{:S(2)}) async-start(bf16[2,32,4096]{2,0,1:T(2,128)(2,1)} %copy.73), calls=%async_computation.5 | async-start | bytes 1048576 | tf_op jit(solution)/shard_map/all_to_all | solution.py:124
  371.8 4.3 %copy-start.1 = (bf16[1,2048,256]{2,1,0:T(8,128)(2,1)S(1)}, bf16[1,2048,256]{2,1,0:T(8,128)(2,1)}, u32[]{:S(2)}) copy-start(bf16[1,2048,256]{2,1,0:T(8,128)(2,1)} %param.14) | copy-start | bytes 3145732
Sparse Core Ops, SparseCore 0:
  63.9 50.6 all-gather.4
  117.1 62.8 all-gather.6
  192.2 74.3 reduce-scatter.2
  269.0 59.1 reduce-scatter.4

commit v9 on v8

--- a/solution.py
+++ b/solution.py
@@ -47,8 +47,8 @@
 def own_batch(partial, collective_id):
     streams, rows, k = partial.shape
     split = partial.reshape(streams, SPLIT, 2, -1, k)
-    traded = swap_with_partner(split[:, :, 1], collective_id)
-    return (split[:, :, 0] + traded).reshape(streams, -1, k)
+    traded = swap_with_partner(split[:, :, 1].astype(jnp.bfloat16), collective_id)
+    return (split[:, :, 0] + traded.astype(jnp.float32)).reshape(streams, -1, k)
 
 
 def both_batches(values, collective_id):
@@ -59,12 +59,15 @@
     return jnp.concatenate([mine, theirs], axis=2).reshape(streams, -1, k)
 
 
+def trade_halves(arrived, shift, half, collective_id):
+    rolled = jnp.roll(arrived, -shift, axis=-1)
+    traded = swap_with_partner(rolled[..., half:], collective_id)
+    return jnp.stack([rolled[..., :half], traded], axis=1)
+
+
 def expert_chunk(arrived, shift, wg, wu, wd, first_id):
     half = wg.shape[0]
-    rolled = jnp.roll(arrived, -shift, axis=-1)
-    traded = swap_with_partner(rolled[..., half:], first_id)
-    both = jnp.stack([rolled[..., :half], traded], axis=1)
-    shared = lax.all_gather(both, "col", axis=1, tiled=False)
+    shared = lax.all_gather(arrived, "col", axis=1, tiled=False)
     token_rows, cot_rows = shared.reshape(2, -1, half)
     partials = jnp.stack(
         [
@@ -117,10 +120,15 @@
     cut = slots // CHUNKS
     backs = []
     grads = 0.0
+    traded = []
     for k in range(CHUNKS):
         chunk = home_rows[:, :, k * cut : (k + 1) * cut].reshape(2, -1, width)
+        if traded:
+            chunk, _ = lax.optimization_barrier((chunk, traded[-1]))
         arrived = lax.all_to_all(chunk, "yx", split_axis=1, concat_axis=1, tiled=True)
-        rows, grad_terms = expert_chunk(arrived, shift, wg, wu, wd, 4 * k)
+        traded.append(trade_halves(arrived, shift, half, 4 * k))
+    for k in range(CHUNKS):
+        rows, grad_terms = expert_chunk(traded[k], shift, wg, wu, wd, 4 * k)
         back = lax.all_to_all(rows, "yx", split_axis=1, concat_axis=1, tiled=True)
         backs.append(back.reshape(2, experts, cut, width))
         grads = grads + grad_terms

time: 388 us -> 360 us (0.928)
  waiting for transfers between devices: 108 us -> 80.1 us
  blocking collectives: 0 us -> 13.5 us
  Pallas kernels: 142 us -> 134 us
  starting transfers between devices: 24.9 us -> 20.9 us
    all_gather x2, waiting for transfers between devices: 41.3 us -> 16.3 us  [expert_chunk(): shared = lax.all_gather(arrived, 'col', axis=1, tiled=False)]
    all_to_all x0 -> x1, blocking collectives: none -> 13.5 us  [shards(): lax.all_to_all(chunk, 'yx', split_axis=1, concat_axis=1, tiled=True)]
    all_to_all x2 -> x1, waiting for transfers between devices: 20.3 us -> 11.5 us  [shards(): lax.all_to_all(chunk, 'yx', split_axis=1, concat_axis=1, tiled=True)]
    pallas_call x8, Pallas kernels: 142 us -> 134 us  [swap_with_partner(): pl.pallas_call(swap_kernel, out_shape=jax.ShapeDtypeStruct(x.shape, x.dty...]
    reduce_scatter x2, waiting for transfers between devices: 37.1 us -> 42.8 us  [expert_chunk(): lax.psum_scatter(partial_rows.reshape(2, SPLIT, 2, -1, half), 'col', scat...]
    all_to_all x2 -> x1, starting transfers between devices: 10.6 us -> 7.03 us  [shards(): lax.all_to_all(chunk, 'yx', split_axis=1, concat_axis=1, tiled=True)]
  transfers between devices with their start and end apart: 8 -> 7, of which waited for: 5 -> 5; matrix products, arithmetic and copies ran while one was open for 13% -> 14% of each run, Pallas kernels for 35% -> 36%
where the time goes in v9:
time: 360 us; the launch traced here: 355 us
  Pallas kernels  134 us (37%)
  waiting for transfers between devices  80.1 us (22%)
  local copies, waits for them, and re-layouts  44.2 us (12%)
  other arithmetic  34.5 us (10%)
  starting transfers between devices  20.9 us (6%)
  between operations  14.4 us (4%)
  blocking collectives  13.5 us (4%)
  matrix products  13.2 us (4%)
    pallas_call x8, Pallas kernels, swap_with_partner(): pl.pallas_call(swap_kernel, out_shape=jax.ShapeDtypeStruct(x.shape, x.dty...  134 us
    reduce_scatter x2, waiting for transfers between devices, expert_chunk(): lax.psum_scatter(partial_rows.reshape(2, SPLIT, 2, -1, half), 'col', scat...  42.8 us
    all_gather x2, waiting for transfers between devices, expert_chunk(): shared = lax.all_gather(arrived, 'col', axis=1, tiled=False)  16.3 us
    all_to_all x1, blocking collectives, shards(): lax.all_to_all(chunk, 'yx', split_axis=1, concat_axis=1, tiled=True)  13.5 us
    all_to_all x2, starting transfers between devices, shards(): back = lax.all_to_all(rows, 'yx', split_axis=1, concat_axis=1, tiled=True)  13.3 us
    all_to_all x1, waiting for transfers between devices, shards(): lax.all_to_all(chunk, 'yx', split_axis=1, concat_axis=1, tiled=True)  11.5 us
    all_to_all x2, waiting for transfers between devices, shards(): back = lax.all_to_all(rows, 'yx', split_axis=1, concat_axis=1, tiled=True)  9.4 us
    unnamed x42, local copies, waits for them, and re-layouts  8.2 us
  transfers between devices with their start and end apart: 7, of which 5 were waited for; matrix products, arithmetic and copies ran while one was open for 14% of the time, Pallas kernels for 36%

profile of v9, /device:TPU:32, one launch (start us, length us, event | category | flops | bytes accessed | tf_op | source)
XLA Modules:
  0.0 355.1 jit_solution(9268619510906939389)
XLA Ops:
  7.2 0.8 compare_select_fusion
  8.2 3.6 %gather_fusion.1 = bf16[64,4096]{1,0:T(8,128)(2,1)} fusion(bf16[128,4096]{1,0:T(8,128)(2,1)} %param.15, s32[1024]{0:T(1024)S(1)} %pad_clamp_fusion), kind=kCustom, calls=%fused_computation.1 | custom fusion | bytes 1048832 | tf_op jit(solution)/shard_map/gather | solution.py:117
  11.8 1.4 reshape.664
  13.3 1.7 gather_fusion
  14.9 2.0 stack.95
  17.2 2.4 fusion.59
  19.6 1.4 copy.53
  21.0 7.0 %all-to-all-start = ((bf16[2,32,4096]{2,0,1:T(2,128)(2,1)}), bf16[2,32,4096]{2,0,1:T(2,128)(2,1)S(1)}, u32[]{:S(2)}, u32[]{:S(2)}) async-start(bf16[2,32,4096]{2,0,1:T(2,128)(2,1)} %bitcast.2), calls=%async_computation | async-start | bytes 1048576 | tf_op jit(solution)/shard_map/all_to_all | solution.py:128
  28.1 11.5 %all-to-all-done = bf16[2,32,4096]{2,0,1:T(2,128)(2,1)S(1)} async-done(((bf16[2,32,4096]{2,0,1:T(2,128)(2,1)}), bf16[2,32,4096]{2,0,1:T(2,128)(2,1)S(1)}, u32[]{:S(2)}, u32[]{:S(2)}) %all-to-all-start) | async-done | bytes 524320 | tf_op jit(solution)/shard_map/all_to_all | solution.py:128
  40.2 0.7 slice_bitcast_fusion.7
  40.9 7.1 %shard_map.110 = bf16[2,32,2048]{2,1,0:T(8,128)(2,1)} custom-call(bf16[2,32,2048]{2,1,0:T(8,128)(2,1)} %get-tuple-element.56.src_ref), custom_call_target="tpu_custom_call" | custom-call | bytes 524288 | tf_op jit(solution)/shard_map/pallas_call | solution.py:36
  48.0 1.8 pad_maximum_fusion.7
  50.4 13.5 %all_to_all.20 = bf16[2,32,4096]{2,0,1:T(2,128)(2,1)S(1)} all-to-all(bf16[2,32,4096]{2,0,1:T(2,128)(2,1)S(1)} %bitcast.330), channel_id=1, replica_groups=mesh['dp'=2,'yx'=16,'col'=8] {'yx'}, dimensions={1} | all-to-all | bytes 1048576 | tf_op jit(solution)/shard_map/all_to_all | solution.py:128
  64.6 0.7 slice_bitcast_fusion.4
  65.3 24.4 %shard_map.114 = bf16[2,32,2048]{2,1,0:T(8,128)(2,1)} custom-call(bf16[2,32,2048]{2,1,0:T(8,128)(2,1)} %get-tuple-element.54.src_ref), custom_call_target="tpu_custom_call" | custom-call | bytes 524288 | tf_op jit(solution)/shard_map/pallas_call | solution.py:36
  89.8 1.8 pad_maximum_fusion.8
  91.8 16.3 %all-gather.5.cloned.1.call-done = bf16[2,16,32,2048]{3,2,0,1:T(8,128)(2,1)} async-done(((bf16[2,2,32,2048]{3,2,0,1:T(8,128)(2,1)}), bf16[2,16,32,2048]{3,2,0,1:T(8,128)(2,1)}) %all-gather.5.cloned.1.call-update) | async-done | bytes 4194320 | tf_op jit(solution)/shard_map/all_gather | solution.py:70
  108.1 2.7 fusion.108
  114.6 0.8 fusion.60.src_ref
  115.4 28.0 %shard_map.111 = bf16[3,8,32,256]{3,2,1,0:T(8,128)(2,1)} custom-call(bf16[3,8,32,256]{3,2,1,0:T(8,128)(2,1)} %fusion.60.src_ref), custom_call_target="tpu_custom_call" | custom-call | bytes 786432 | tf_op jit(solution)/shard_map/pallas_call | solution.py:36
  143.4 1.1 fusion.50
  144.8 0.8 pad_maximum_fusion.9.src_ref
  145.6 22.5 %shard_map.112 = bf16[3,256,256]{2,1,0:T(8,128)(2,1)} custom-call(bf16[3,256,256]{2,1,0:T(8,128)(2,1)} %pad_maximum_fusion.9.src_ref), custom_call_target="tpu_custom_call" | custom-call | bytes 786432 | tf_op jit(solution)/shard_map/pallas_call | solution.py:36
  168.2 1.1 pad_maximum_fusion.4
  169.3 1.0 slice_bitcast_fusion.12
  170.4 0.7 convolution_convert_fusion.1
  172.8 0.8 add_convert_fusion.1
  173.6 2.3 pad_maximum_fusion
  176.2 2.7 fusion.109
  181.9 0.8 fusion.61.src_ref
  182.7 20.1 %shard_map.115 = bf16[3,8,32,256]{3,2,1,0:T(8,128)(2,1)} custom-call(bf16[3,8,32,256]{3,2,1,0:T(8,128)(2,1)} %fusion.61.src_ref), custom_call_target="tpu_custom_call" | custom-call | bytes 786432 | tf_op jit(solution)/shard_map/pallas_call | solution.py:36
  202.9 1.1 fusion.49
  204.2 0.8 pad_maximum_fusion.10.src_ref
  205.0 18.2 %shard_map.116 = bf16[3,256,256]{2,1,0:T(8,128)(2,1)} custom-call(bf16[3,256,256]{2,1,0:T(8,128)(2,1)} %pad_maximum_fusion.10.src_ref), custom_call_target="tpu_custom_call" | custom-call | bytes 786432 | tf_op jit(solution)/shard_map/pallas_call | solution.py:36
  223.4 1.1 pad_maximum_fusion.5
  227.9 2.4 pad_maximum_fusion.1
  230.4 1.6 copy-done.12
  232.7 0.9 copy-done.10
  235.3 0.9 copy-done.16
  236.9 0.9 copy-done.14
  239.3 1.0 fusion
  240.3 2.3 reduce-scatter.3.cloned.1.call-done
  242.5 1.8 slice_bitcast_fusion.5
  244.3 6.7 %shard_map.113 = bf16[2,32,2048]{2,1,0:T(8,128)(2,1)} custom-call(bf16[2,32,2048]{2,1,0:T(8,128)(2,1)} %get-tuple-element.43.src_ref), custom_call_target="tpu_custom_call" | custom-call | bytes 524288 | tf_op jit(solution)/shard_map/pallas_call | solution.py:36
  251.0 1.3 fusion.56
  252.4 1.3 copy.62
  253.7 6.5 %all-to-all-start.1 = ((bf16[2,32,4096]{2,0,1:T(2,128)(2,1)}), bf16[2,32,4096]{2,0,1:T(2,128)(2,1)}, u32[]{:S(2)}, u32[]{:S(2)}) async-start(bf16[2,32,4096]{2,0,1:T(2,128)(2,1)} %copy.62), calls=%async_computation.2 | async-start | bytes 1048576 | tf_op jit(solution)/shard_map/all_to_all | solution.py:132
  260.2 40.6 %reduce-scatter.5.cloned.1.call-done = bf16[2,1,2,32,2048]{4,3,0,2,1:T(8,128)(2,1)} async-done(((bf16[2,8,2,32,2048]{4,3,0,2,1:T(8,128)(2,1)}), bf16[2,1,2,32,2048]{4,3,0,2,1:T(8,128)(2,1)}) %reduce-scatter.5.cloned.1.call-update) | async-done | bytes 524304 | tf_op jit(solution)/shard_map/reduce_scatter | solution.py:95
  300.8 1.8 slice_bitcast_fusion.2
  302.6 7.1 %shard_map.117 = bf16[2,32,2048]{2,1,0:T(8,128)(2,1)} custom-call(bf16[2,32,2048]{2,1,0:T(8,128)(2,1)} %get-tuple-element.48.src_ref), custom_call_target="tpu_custom_call" | custom-call | bytes 524288 | tf_op jit(solution)/shard_map/pallas_call | solution.py:36
  309.7 1.3 fusion.52
  311.0 1.3 copy.73
  312.4 6.8 %all-to-all-start.3 = ((bf16[2,32,4096]{2,0,1:T(2,128)(2,1)}), bf16[2,32,4096]{2,0,1:T(2,128)(2,1)}, u32[]{:S(2)}, u32[]{:S(2)}) async-start(bf16[2,32,4096]{2,0,1:T(2,128)(2,1)} %copy.73), calls=%async_computation.5 | async-start | bytes 1048576 | tf_op jit(solution)/shard_map/all_to_all | solution.py:132
  319.2 1.7 fusion.110
  320.9 9.4 %all-to-all-done.3 = bf16[2,32,4096]{2,0,1:T(2,128)(2,1)} async-done(((bf16[2,32,4096]{2,0,1:T(2,128)(2,1)}), bf16[2,32,4096]{2,0,1:T(2,128)(2,1)}, u32[]{:S(2)}, u32[]{:S(2)}) %all-to-all-start.3) | async-done | bytes 524320 | tf_op jit(solution)/shard_map/all_to_all | solution.py:132
  330.3 2.3 maximum_convert_fusion
  332.6 4.0 %slice_reduce_fusion = (f32[16,4,4096]{2,1,0:T(4,128)S(1)}, f32[1,16,4,4096]{3,0,2,1:T(1,128)S(1)}) fusion(f32[2,16,4,4096]{3,0,2,1:T(2,128)S(1)} %maximum_convert_fusion), kind=kLoop, calls=%fused_computation.38 | loop fusion | bytes 4194304 | tf_op jit(solution)/shard_map/slice | solution.py:138
  336.6 0.8 bitcast_multiply_fusion
  337.4 1.3 reshape.685
  338.7 3.1 scatter_custom_fusion
  341.9 1.1 convert_element_type.197
  343.0 1.3 reshape.693
  344.3 3.2 scatter_custom_fusion.1
  347.5 1.1 convert_element_type.198
  (89 shorter events, 20.0 us)
Async XLA Ops:
  7.2 106.5 %copy-start = (bf16[1,2048,256]{2,1,0:T(8,128)(2,1)S(1)}, bf16[1,2048,256]{2,1,0:T(8,128)(2,1)}, u32[]{:S(2)}) copy-start(bf16[1,2048,256]{2,1,0:T(8,128)(2,1)} %param.14) | copy-start | bytes 3145732
  8.1 5.0 %copy-start.20 = (f32[1,16,4]{1,2,0:T(4,128)S(1)}, f32[1,16,4]{1,2,0:T(4,128)}, u32[]{:S(2)}) copy-start(f32[1,16,4]{1,2,0:T(4,128)} %param.11) | copy-start | bytes 772
  8.2 5.1 %copy-start.2 = (bf16[128,4096]{1,0:T(8,128)(2,1)S(1)}, bf16[128,4096]{1,0:T(8,128)(2,1)}, u32[]{:S(2)}) copy-start(bf16[128,4096]{1,0:T(8,128)(2,1)} %param.9) | copy-start | bytes 3145732
  21.0 18.6 %all-to-all-start = ((bf16[2,32,4096]{2,0,1:T(2,128)(2,1)}), bf16[2,32,4096]{2,0,1:T(2,128)(2,1)S(1)}, u32[]{:S(2)}, u32[]{:S(2)}) async-start(bf16[2,32,4096]{2,0,1:T(2,128)(2,1)} %bitcast.2), calls=%async_computation | async-start | bytes 1048576 | tf_op jit(solution)/shard_map/all_to_all | solution.py:128
  28.0 80.1 %all-gather.5.cloned.1.call-start = ((), (), s32[]{:S(2)}) async-start(), calls=%async_computation.8 | async-start | bytes 4718592 | tf_op jit(solution)/shard_map/all_gather | solution.py:70
  49.8 126.4 %all-gather.7.cloned.1.call-start = ((), (), s32[]{:S(2)}) async-start(), calls=%async_computation.9 | async-start | bytes 4718592 | tf_op jit(solution)/shard_map/all_gather | solution.py:70
  91.6 19.3 %copy-start.3 = (bf16[1,2048,256]{2,1,0:T(8,128)(2,1)S(1)}, bf16[1,2048,256]{2,1,0:T(8,128)(2,1)}, u32[]{:S(2)}) copy-start(bf16[1,2048,256]{2,1,0:T(8,128)(2,1)} %param.12) | copy-start | bytes 3145732
  91.6 150.9 %reduce-scatter.3.cloned.1.call-start = ((), (), s32[]{:S(2)}) async-start(), calls=%async_computation.6 | async-start | bytes 4718592 | tf_op jit(solution)/shard_map/reduce_scatter | solution.py:95
  110.9 1.4 copy-start.9
  110.9 2.8 copy-start.11
  110.9 2.0 copy-start.6
  170.4 1.2 copy-start.4
  171.6 1.2 copy-start.7
  175.9 124.9 %reduce-scatter.5.cloned.1.call-start = ((), (), s32[]{:S(2)}) async-start(), calls=%async_computation.7 | async-start | bytes 4718592 | tf_op jit(solution)/shard_map/reduce_scatter | solution.py:95
  179.0 1.3 copy-start.13
  179.0 2.0 copy-start.15
  224.7 1.2 copy-start.5
  225.9 1.2 copy-start.8
  230.3 1.6 copy-start.12
  230.3 1.6 copy-start.19
  231.9 1.6 copy-start.10
  232.0 1.6 copy-start.18
  233.6 1.0 copy-start.17
  234.5 1.6 copy-start.16
  236.2 1.6 copy-start.14
  253.7 58.7 %all-to-all-start.1 = ((bf16[2,32,4096]{2,0,1:T(2,128)(2,1)}), bf16[2,32,4096]{2,0,1:T(2,128)(2,1)}, u32[]{:S(2)}, u32[]{:S(2)}) async-start(bf16[2,32,4096]{2,0,1:T(2,128)(2,1)} %copy.62), calls=%async_computation.2 | async-start | bytes 1048576 | tf_op jit(solution)/shard_map/all_to_all | solution.py:132
  312.4 17.9 %all-to-all-start.3 = ((bf16[2,32,4096]{2,0,1:T(2,128)(2,1)}), bf16[2,32,4096]{2,0,1:T(2,128)(2,1)}, u32[]{:S(2)}, u32[]{:S(2)}) async-start(bf16[2,32,4096]{2,0,1:T(2,128)(2,1)} %copy.73), calls=%async_computation.5 | async-start | bytes 1048576 | tf_op jit(solution)/shard_map/all_to_all | solution.py:132
  344.3 4.3 %copy-start.1 = (bf16[1,2048,256]{2,1,0:T(8,128)(2,1)S(1)}, bf16[1,2048,256]{2,1,0:T(8,128)(2,1)}, u32[]{:S(2)}) copy-start(bf16[1,2048,256]{2,1,0:T(8,128)(2,1)} %param.14) | copy-start | bytes 3145732
Sparse Core Ops, SparseCore 0:
  49.9 58.1 all-gather.4
  110.6 57.8 all-gather.6
  176.1 66.4 reduce-scatter.2
  244.9 55.8 reduce-scatter.4

commit v10 on v9

--- a/solution.py
+++ b/solution.py
@@ -92,11 +92,6 @@
         + lax.dot_general(up_all, wu, CONTRACT_LAST, preferred_element_type=jnp.float32)
     ).astype(jnp.bfloat16)
     partial_rows = jnp.stack([partial_value, partial_grad])
-    summed = lax.psum_scatter(
-        partial_rows.reshape(2, SPLIT, 2, -1, half), "col", scatter_dimension=1, tiled=True
-    )[:, 0]
-    traded_back = swap_with_partner(summed[:, 1], first_id + 3)
-    rows = jnp.roll(jnp.concatenate([summed[:, 0], traded_back], axis=-1), shift, axis=-1)
     grad_terms = jnp.stack(
         [
             lax.dot_general(token_rows, gate_all, CONTRACT_FIRST, preferred_element_type=jnp.float32),
@@ -104,7 +99,16 @@
             lax.dot_general(cot_rows, hidden_all, CONTRACT_FIRST, preferred_element_type=jnp.float32),
         ]
     )
-    return rows, grad_terms
+    return partial_rows, grad_terms
+
+
+def bring_back(partial_rows, shift, collective_id):
+    half = partial_rows.shape[-1]
+    summed = lax.psum_scatter(
+        partial_rows.reshape(2, SPLIT, 2, -1, half), "col", scatter_dimension=1, tiled=True
+    )[:, 0]
+    traded_back = swap_with_partner(summed[:, 1], collective_id)
+    return jnp.roll(jnp.concatenate([summed[:, 0], traded_back], axis=-1), shift, axis=-1)
 
 
 def shards(tokens, routes, gate_values, gate_weight, up_weight, down_weight, cotangent):
@@ -127,15 +131,20 @@
             chunk, _ = lax.optimization_barrier((chunk, traded[-1]))
         arrived = lax.all_to_all(chunk, "yx", split_axis=1, concat_axis=1, tiled=True)
         traded.append(trade_halves(arrived, shift, half, 4 * k))
+    computed = [expert_chunk(traded[k], shift, wg, wu, wd, 4 * k) for k in range(CHUNKS)]
+    grads = sum(c[1] for c in computed).astype(jnp.bfloat16)
+    layer_out = jnp.zeros((tokens.shape[0], width), jnp.float32)
+    token_grad = jnp.zeros((tokens.shape[0], width), jnp.float32)
     for k in range(CHUNKS):
-        rows, grad_terms = expert_chunk(traded[k], shift, wg, wu, wd, 4 * k)
+        partial_rows = computed[k][0]
+        if k == CHUNKS - 1:
+            partial_rows, grads = lax.optimization_barrier((partial_rows, grads))
+        rows = bring_back(partial_rows, shift, 4 * k + 3)
         back = lax.all_to_all(rows, "yx", split_axis=1, concat_axis=1, tiled=True)
-        backs.append(back.reshape(2, experts, cut, width))
-        grads = grads + grad_terms
-    back = jnp.concatenate(backs, axis=2).astype(jnp.float32)
-    grads = grads.astype(jnp.bfloat16)
-    layer_out = jnp.zeros((tokens.shape[0], width), jnp.float32).at[chosen].add(scales * back[0])
-    token_grad = jnp.zeros((tokens.shape[0], width), jnp.float32).at[chosen].add(back[1])
+        back = back.astype(jnp.float32).reshape(2, experts, cut, width)
+        taken = chosen[:, k * cut : (k + 1) * cut]
+        layer_out = layer_out.at[taken].add(scales[:, k * cut : (k + 1) * cut] * back[0])
+        token_grad = token_grad.at[taken].add(back[1])
     return (
         layer_out.astype(jnp.bfloat16),
         token_grad.astype(jnp.bfloat16),

time: 360 us -> 366 us (1.017)
  waiting for transfers between devices: 80.1 us -> 57 us
  Pallas kernels: 134 us -> 148 us
  matrix products: 13.2 us -> 19 us
  other arithmetic: 34.5 us -> 38.7 us
    reduce_scatter x2, waiting for transfers between devices: 42.8 us -> 27 us  [bring_back(): lax.psum_scatter(partial_rows.reshape(2, SPLIT, 2, -1, half), 'col', scat...]
    pallas_call x8, Pallas kernels: 134 us -> 148 us  [swap_with_partner(): pl.pallas_call(swap_kernel, out_shape=jax.ShapeDtypeStruct(x.shape, x.dty...]
    all_to_all x2, waiting for transfers between devices: 9.4 us -> 2.27 us  [shards(): back = lax.all_to_all(rows, 'yx', split_axis=1, concat_axis=1, tiled=True)]
    scatter-add x2 -> x4, other arithmetic: 6.28 us -> 12.4 us  [the longest x2 7.62 us: shards(): token_grad = token_grad.at[taken].add(back[1])]
    unnamed x42 -> x44, local copies, waits for them, and re-layouts: 8.2 us -> 8.7 us
  transfers between devices with their start and end apart: 7 -> 7, of which waited for: 5 -> 4; matrix products, arithmetic and copies ran while one was open for 14% -> 18% of each run, Pallas kernels for 36% -> 39%
where the time goes in v10:
time: 366 us; the launch traced here: 360 us
  Pallas kernels  148 us (40%)
  waiting for transfers between devices  57 us (16%)
  local copies, waits for them, and re-layouts  47.8 us (13%)
  other arithmetic  38.7 us (11%)
  starting transfers between devices  21.4 us (6%)
  matrix products  19 us (5%)
  between operations  14.8 us (4%)
  blocking collectives  13.5 us (4%)
    pallas_call x8, Pallas kernels, swap_with_partner(): pl.pallas_call(swap_kernel, out_shape=jax.ShapeDtypeStruct(x.shape, x.dty...  148 us
    reduce_scatter x2, waiting for transfers between devices, bring_back(): lax.psum_scatter(partial_rows.reshape(2, SPLIT, 2, -1, half), 'col', scat...  27 us
    all_gather x2, waiting for transfers between devices, expert_chunk(): shared = lax.all_gather(arrived, 'col', axis=1, tiled=False)  16.2 us
    all_to_all x1, blocking collectives, shards(): lax.all_to_all(chunk, 'yx', split_axis=1, concat_axis=1, tiled=True)  13.5 us
    all_to_all x2, starting transfers between devices, shards(): back = lax.all_to_all(rows, 'yx', split_axis=1, concat_axis=1, tiled=True)  13.4 us
    all_to_all x1, waiting for transfers between devices, shards(): lax.all_to_all(chunk, 'yx', split_axis=1, concat_axis=1, tiled=True)  11.5 us
    unnamed x44, local copies, waits for them, and re-layouts  8.7 us
    scatter-add x2, other arithmetic, shards(): token_grad = token_grad.at[taken].add(back[1])  7.62 us
  transfers between devices with their start and end apart: 7, of which 4 were waited for; matrix products, arithmetic and copies ran while one was open for 18% of the time, Pallas kernels for 39%

profile of v10, /device:TPU:32, one launch (start us, length us, event | category | flops | bytes accessed | tf_op | source)
XLA Modules:
  0.0 360.1 jit_solution(7380885114603679674)
XLA Ops:
  7.2 0.8 compare_select_fusion
  8.2 3.6 %gather_fusion.1 = bf16[64,4096]{1,0:T(8,128)(2,1)} fusion(bf16[128,4096]{1,0:T(8,128)(2,1)} %param.15, s32[1024]{0:T(1024)S(1)} %pad_clamp_fusion), kind=kCustom, calls=%fused_computation.1 | custom fusion | bytes 1048832 | tf_op jit(solution)/shard_map/gather | solution.py:121
  11.8 1.4 reshape.665
  13.3 1.7 gather_fusion
  14.9 2.0 stack.95
  17.2 2.4 pad_maximum_fusion.6
  19.6 1.4 copy.61
  21.0 7.0 %all-to-all-start = ((bf16[2,32,4096]{2,0,1:T(2,128)(2,1)}), bf16[2,32,4096]{2,0,1:T(2,128)(2,1)S(1)}, u32[]{:S(2)}, u32[]{:S(2)}) async-start(bf16[2,32,4096]{2,0,1:T(2,128)(2,1)} %bitcast.5), calls=%async_computation | async-start | bytes 1048576 | tf_op jit(solution)/shard_map/all_to_all | solution.py:132
  28.1 11.5 %all-to-all-done = bf16[2,32,4096]{2,0,1:T(2,128)(2,1)S(1)} async-done(((bf16[2,32,4096]{2,0,1:T(2,128)(2,1)}), bf16[2,32,4096]{2,0,1:T(2,128)(2,1)S(1)}, u32[]{:S(2)}, u32[]{:S(2)}) %all-to-all-start) | async-done | bytes 524320 | tf_op jit(solution)/shard_map/all_to_all | solution.py:132
  40.9 7.1 %shard_map.110 = bf16[2,32,2048]{2,1,0:T(8,128)(2,1)} custom-call(bf16[2,32,2048]{2,1,0:T(8,128)(2,1)} %get-tuple-element.58.src_ref), custom_call_target="tpu_custom_call" | custom-call | bytes 524288 | tf_op jit(solution)/shard_map/pallas_call | solution.py:36
  48.0 1.8 pad_maximum_fusion.7
  50.4 13.5 %all_to_all.20 = bf16[2,32,4096]{2,0,1:T(2,128)(2,1)S(1)} all-to-all(bf16[2,32,4096]{2,0,1:T(2,128)(2,1)S(1)} %bitcast.340), channel_id=1, replica_groups=mesh['dp'=2,'yx'=16,'col'=8] {'yx'}, dimensions={1} | all-to-all | bytes 1048576 | tf_op jit(solution)/shard_map/all_to_all | solution.py:132
  65.3 24.4 %shard_map.114 = bf16[2,32,2048]{2,1,0:T(8,128)(2,1)} custom-call(bf16[2,32,2048]{2,1,0:T(8,128)(2,1)} %get-tuple-element.51.src_ref), custom_call_target="tpu_custom_call" | custom-call | bytes 524288 | tf_op jit(solution)/shard_map/pallas_call | solution.py:36
  89.8 1.8 pad_maximum_fusion.8
  91.9 16.2 %all-gather.5.cloned.1.call-done = bf16[2,16,32,2048]{3,2,0,1:T(8,128)(2,1)} async-done(((bf16[2,2,32,2048]{3,2,0,1:T(8,128)(2,1)}), bf16[2,16,32,2048]{3,2,0,1:T(8,128)(2,1)}) %all-gather.5.cloned.1.call-update) | async-done | bytes 4194320 | tf_op jit(solution)/shard_map/all_gather | solution.py:70
  108.1 2.7 fusion.116
  114.6 0.8 fusion.67.src_ref
  115.4 27.9 %shard_map.111 = bf16[3,8,32,256]{3,2,1,0:T(8,128)(2,1)} custom-call(bf16[3,8,32,256]{3,2,1,0:T(8,128)(2,1)} %fusion.67.src_ref), custom_call_target="tpu_custom_call" | custom-call | bytes 786432 | tf_op jit(solution)/shard_map/pallas_call | solution.py:36
  143.4 1.1 fusion.52
  144.7 0.8 pad_maximum_fusion.9.src_ref
  145.5 22.5 %shard_map.112 = bf16[3,256,256]{2,1,0:T(8,128)(2,1)} custom-call(bf16[3,256,256]{2,1,0:T(8,128)(2,1)} %pad_maximum_fusion.9.src_ref), custom_call_target="tpu_custom_call" | custom-call | bytes 786432 | tf_op jit(solution)/shard_map/pallas_call | solution.py:36
  168.2 1.1 pad_maximum_fusion.4
  169.3 1.0 slice_bitcast_fusion.14
  172.8 0.8 add_convert_fusion.1
  173.5 2.3 pad_maximum_fusion
  176.5 3.9 %convolution_bitcast_fusion.3 = f32[1,2048,256]{2,1,0:T(8,128)} fusion(bf16[8,2,32,2048]{3,2,1,0:T(8,128)(2,1)} %bitcast.346, bf16[8,2,32,256]{3,2,0,1:T(8,128)(2,1)} %get-tuple-element.28), kind=kOutput, calls=%fused_computation.19 | convolution fusion | flops 536870912 | bytes 4456448 | tf_op jit(solution)/shard_map/dot_general | solution.py:99
  180.3 2.1 convolution_bitcast_fusion.4
  182.4 2.0 convolution_bitcast_fusion.5
  184.5 2.7 fusion.115
  190.3 0.8 fusion.68.src_ref
  191.1 19.6 %shard_map.115 = bf16[3,8,32,256]{3,2,1,0:T(8,128)(2,1)} custom-call(bf16[3,8,32,256]{3,2,1,0:T(8,128)(2,1)} %fusion.68.src_ref), custom_call_target="tpu_custom_call" | custom-call | bytes 786432 | tf_op jit(solution)/shard_map/pallas_call | solution.py:36
  210.7 1.1 fusion.51
  212.0 0.8 pad_maximum_fusion.10.src_ref
  212.8 22.2 %shard_map.116 = bf16[3,256,256]{2,1,0:T(8,128)(2,1)} custom-call(bf16[3,256,256]{2,1,0:T(8,128)(2,1)} %pad_maximum_fusion.10.src_ref), custom_call_target="tpu_custom_call" | custom-call | bytes 786432 | tf_op jit(solution)/shard_map/pallas_call | solution.py:36
  235.1 1.1 pad_maximum_fusion.5
  240.0 1.2 copy-done.18
  242.7 0.8 copy-done.16
  243.6 0.7 convolution_bitcast_fusion
  244.3 0.9 copy-done.9
  246.5 1.2 fusion
  247.7 2.3 copy.89
  251.2 1.7 fusion.117
  253.0 1.8 slice_bitcast_fusion.5
  254.8 13.5 %shard_map.113 = bf16[2,32,2048]{2,1,0:T(8,128)(2,1)} custom-call(bf16[2,32,2048]{2,1,0:T(8,128)(2,1)} %get-tuple-element.52.src_ref), custom_call_target="tpu_custom_call" | custom-call | bytes 524288 | tf_op jit(solution)/shard_map/pallas_call | solution.py:36
  268.2 1.3 fusion.58
  269.6 1.3 copy.70
  270.9 6.5 %all-to-all-start.1 = ((bf16[2,32,4096]{2,0,1:T(2,128)(2,1)}), bf16[2,32,4096]{2,0,1:T(2,128)(2,1)S(1)}, u32[]{:S(2)}, u32[]{:S(2)}) async-start(bf16[2,32,4096]{2,0,1:T(2,128)(2,1)} %copy.70), calls=%async_computation.2 | async-start | bytes 1048576 | tf_op jit(solution)/shard_map/all_to_all | solution.py:143
  277.4 27.0 %reduce-scatter.5.cloned.1.call-done = bf16[2,1,2,32,2048]{4,3,0,2,1:T(8,128)(2,1)} async-done(((bf16[2,8,2,32,2048]{4,3,0,2,1:T(8,128)(2,1)}), bf16[2,1,2,32,2048]{4,3,0,2,1:T(8,128)(2,1)}) %reduce-scatter.5.cloned.1.call-update) | async-done | bytes 524304 | tf_op jit(solution)/shard_map/reduce_scatter | solution.py:107
  304.4 1.8 slice_bitcast_fusion.2
  306.2 10.7 %shard_map.117 = bf16[2,32,2048]{2,1,0:T(8,128)(2,1)} custom-call(bf16[2,32,2048]{2,1,0:T(8,128)(2,1)} %get-tuple-element.45.src_ref), custom_call_target="tpu_custom_call" | custom-call | bytes 524288 | tf_op jit(solution)/shard_map/pallas_call | solution.py:36
  316.8 1.3 fusion.54
  318.2 1.3 copy.90
  319.5 6.9 %all-to-all-start.3 = ((bf16[2,32,4096]{2,0,1:T(2,128)(2,1)}), bf16[2,32,4096]{2,0,1:T(2,128)(2,1)S(1)}, u32[]{:S(2)}, u32[]{:S(2)}) async-start(bf16[2,32,4096]{2,0,1:T(2,128)(2,1)} %copy.90), calls=%async_computation.5 | async-start | bytes 1048576 | tf_op jit(solution)/shard_map/all_to_all | solution.py:143
  326.8 1.3 slice_reduce_fusion.1
  328.8 1.2 reshape.686
  330.6 3.0 scatter_custom_fusion.2
  333.6 2.3 scatter_custom_fusion
  335.9 2.3 all-to-all-done.3
  338.8 4.6 %scatter_custom_fusion.3 = f32[128,4096]{1,0:T(8,128)} fusion(f32[128,4096]{1,0:T(8,128)} %scatter_custom_fusion.2, s32[32]{0:T(128)S(1)} %reshape.692, f32[1,32,4096]{2,0,1:T(1,128)S(1)} %slice.151), kind=kCustom, calls=%fused_computation.97 | custom fusion | flops 131072 | bytes 2621440 | tf_op jit(solution)/shard_map/scatter-add | solution.py:147
  343.4 2.7 convert_element_type.203
  346.6 1.3 slice_reduce_fusion
  348.5 1.2 reshape.694
  349.7 2.5 scatter_fusion
  352.2 1.1 convert_element_type.202
  (109 shorter events, 25.7 us)
Async XLA Ops:
  7.2 106.5 %copy-start = (bf16[1,2048,256]{2,1,0:T(8,128)(2,1)S(1)}, bf16[1,2048,256]{2,1,0:T(8,128)(2,1)}, u32[]{:S(2)}) copy-start(bf16[1,2048,256]{2,1,0:T(8,128)(2,1)} %param.14) | copy-start | bytes 3145732
  8.1 5.0 %copy-start.20 = (f32[1,16,4]{1,2,0:T(4,128)S(1)}, f32[1,16,4]{1,2,0:T(4,128)}, u32[]{:S(2)}) copy-start(f32[1,16,4]{1,2,0:T(4,128)} %param.11) | copy-start | bytes 772
  8.2 5.1 %copy-start.2 = (bf16[128,4096]{1,0:T(8,128)(2,1)S(1)}, bf16[128,4096]{1,0:T(8,128)(2,1)}, u32[]{:S(2)}) copy-start(bf16[128,4096]{1,0:T(8,128)(2,1)} %param.9) | copy-start | bytes 3145732
  21.0 18.6 %all-to-all-start = ((bf16[2,32,4096]{2,0,1:T(2,128)(2,1)}), bf16[2,32,4096]{2,0,1:T(2,128)(2,1)S(1)}, u32[]{:S(2)}, u32[]{:S(2)}) async-start(bf16[2,32,4096]{2,0,1:T(2,128)(2,1)} %bitcast.5), calls=%async_computation | async-start | bytes 1048576 | tf_op jit(solution)/shard_map/all_to_all | solution.py:132
  28.0 80.1 %all-gather.5.cloned.1.call-start = ((), (), s32[]{:S(2)}) async-start(), calls=%async_computation.8 | async-start | bytes 4718592 | tf_op jit(solution)/shard_map/all_gather | solution.py:70
  49.8 134.7 %all-gather.7.cloned.1.call-start = ((), (), s32[]{:S(2)}) async-start(), calls=%async_computation.9 | async-start | bytes 4718592 | tf_op jit(solution)/shard_map/all_gather | solution.py:70
  91.6 19.3 %copy-start.3 = (bf16[1,2048,256]{2,1,0:T(8,128)(2,1)S(1)}, bf16[1,2048,256]{2,1,0:T(8,128)(2,1)}, u32[]{:S(2)}) copy-start(bf16[1,2048,256]{2,1,0:T(8,128)(2,1)} %param.12) | copy-start | bytes 3145732
  91.6 161.4 %reduce-scatter.3.cloned.1.call-start = ((), (), s32[]{:S(2)}) async-start(), calls=%async_computation.6 | async-start | bytes 4718592 | tf_op jit(solution)/shard_map/reduce_scatter | solution.py:107
  110.9 1.4 copy-start.12
  110.9 2.8 copy-start.14
  110.9 2.0 copy-start.6
  170.3 1.2 copy-start.4
  171.5 1.2 copy-start.7
  175.9 128.5 %reduce-scatter.5.cloned.1.call-start = ((), (), s32[]{:S(2)}) async-start(), calls=%async_computation.7 | async-start | bytes 4718592 | tf_op jit(solution)/shard_map/reduce_scatter | solution.py:107
  176.4 3.9 %copy-start.13 = (bf16[1,16,32,2048]{3,2,0,1:T(8,128)(2,1)S(1)}, bf16[1,16,32,2048]{3,2,0,1:T(8,128)(2,1)}, u32[]{:S(2)}) copy-start(bf16[1,16,32,2048]{3,2,0,1:T(8,128)(2,1)} %copy-done.12) | copy-start | bytes 6291460
  176.5 3.9 %copy-start.19 = (bf16[8,2,32,256]{3,2,0,1:T(8,128)(2,1)S(1)}, bf16[8,2,32,256]{3,2,0,1:T(8,128)(2,1)}, u32[]{:S(2)}) copy-start(bf16[8,2,32,256]{3,2,0,1:T(8,128)(2,1)} %get-tuple-element.29) | copy-start | bytes 786436
  187.2 1.4 copy-start.17
  187.2 2.1 copy-start.15
  236.4 1.2 copy-start.5
  237.6 1.2 copy-start.8
  239.6 1.6 copy-start.18
  242.0 1.6 copy-start.16
  243.6 1.6 copy-start.9
  243.6 2.3 copy-start.10
  243.6 2.9 copy-start.11
  250.0 0.7 copy-start.21
  270.9 48.6 %all-to-all-start.1 = ((bf16[2,32,4096]{2,0,1:T(2,128)(2,1)}), bf16[2,32,4096]{2,0,1:T(2,128)(2,1)S(1)}, u32[]{:S(2)}, u32[]{:S(2)}) async-start(bf16[2,32,4096]{2,0,1:T(2,128)(2,1)} %copy.70), calls=%async_computation.2 | async-start | bytes 1048576 | tf_op jit(solution)/shard_map/all_to_all | solution.py:143
  319.5 18.6 %all-to-all-start.3 = ((bf16[2,32,4096]{2,0,1:T(2,128)(2,1)}), bf16[2,32,4096]{2,0,1:T(2,128)(2,1)S(1)}, u32[]{:S(2)}, u32[]{:S(2)}) async-start(bf16[2,32,4096]{2,0,1:T(2,128)(2,1)} %copy.90), calls=%async_computation.5 | async-start | bytes 1048576 | tf_op jit(solution)/shard_map/all_to_all | solution.py:143
  349.7 3.6 %copy-start.1 = (bf16[1,2048,256]{2,1,0:T(8,128)(2,1)S(1)}, bf16[1,2048,256]{2,1,0:T(8,128)(2,1)}, u32[]{:S(2)}) copy-start(bf16[1,2048,256]{2,1,0:T(8,128)(2,1)} %param.14) | copy-start | bytes 3145732
Sparse Core Ops, SparseCore 0:
  49.9 58.1 all-gather.4
  110.6 57.9 all-gather.6
  176.0 69.0 reduce-scatter.2
  250.2 54.1 reduce-scatter.4

commit v11 on v9

--- a/solution.py
+++ b/solution.py
@@ -92,11 +92,6 @@
         + lax.dot_general(up_all, wu, CONTRACT_LAST, preferred_element_type=jnp.float32)
     ).astype(jnp.bfloat16)
     partial_rows = jnp.stack([partial_value, partial_grad])
-    summed = lax.psum_scatter(
-        partial_rows.reshape(2, SPLIT, 2, -1, half), "col", scatter_dimension=1, tiled=True
-    )[:, 0]
-    traded_back = swap_with_partner(summed[:, 1], first_id + 3)
-    rows = jnp.roll(jnp.concatenate([summed[:, 0], traded_back], axis=-1), shift, axis=-1)
     grad_terms = jnp.stack(
         [
             lax.dot_general(token_rows, gate_all, CONTRACT_FIRST, preferred_element_type=jnp.float32),
@@ -104,7 +99,19 @@
             lax.dot_general(cot_rows, hidden_all, CONTRACT_FIRST, preferred_element_type=jnp.float32),
         ]
     )
-    return rows, grad_terms
+    return partial_rows, grad_terms
+
+
+def bring_back(partial_rows, shift, collective_id, grads=None):
+    half = partial_rows.shape[-1]
+    summed = lax.psum_scatter(
+        partial_rows.reshape(2, SPLIT, 2, -1, half), "col", scatter_dimension=1, tiled=True
+    )[:, 0]
+    if grads is not None:
+        summed, grads = lax.optimization_barrier((summed, grads))
+    traded_back = swap_with_partner(summed[:, 1], collective_id)
+    rows = jnp.roll(jnp.concatenate([summed[:, 0], traded_back], axis=-1), shift, axis=-1)
+    return rows, grads
 
 
 def shards(tokens, routes, gate_values, gate_weight, up_weight, down_weight, cotangent):
@@ -114,24 +121,28 @@
     scales = gate_values[0][:, :, None]
     shift = lax.axis_index("dp") * half
     wg, wu, wd = gate_weight[0], up_weight[0], down_weight[0]
-    scaled_cot = (scales * cotangent[chosen].astype(jnp.float32)).astype(jnp.bfloat16)
-    home_rows = jnp.stack([tokens[chosen], scaled_cot])
     experts, slots = chosen.shape
     cut = slots // CHUNKS
-    backs = []
-    grads = 0.0
     traded = []
     for k in range(CHUNKS):
-        chunk = home_rows[:, :, k * cut : (k + 1) * cut].reshape(2, -1, width)
+        taken = chosen[:, k * cut : (k + 1) * cut]
+        gains = scales[:, k * cut : (k + 1) * cut]
+        scaled_cot = (gains * cotangent[taken].astype(jnp.float32)).astype(jnp.bfloat16)
+        chunk = jnp.stack([tokens[taken], scaled_cot]).reshape(2, -1, width)
         if traded:
             chunk, _ = lax.optimization_barrier((chunk, traded[-1]))
         arrived = lax.all_to_all(chunk, "yx", split_axis=1, concat_axis=1, tiled=True)
         traded.append(trade_halves(arrived, shift, half, 4 * k))
+    computed = [expert_chunk(traded[k], shift, wg, wu, wd, 4 * k) for k in range(CHUNKS)]
+    grads = sum(c[1] for c in computed)
+    backs = []
     for k in range(CHUNKS):
-        rows, grad_terms = expert_chunk(traded[k], shift, wg, wu, wd, 4 * k)
+        last = k == CHUNKS - 1
+        rows, finished = bring_back(computed[k][0], shift, 4 * k + 3, grads if last else None)
+        if last:
+            grads = finished
         back = lax.all_to_all(rows, "yx", split_axis=1, concat_axis=1, tiled=True)
         backs.append(back.reshape(2, experts, cut, width))
-        grads = grads + grad_terms
     back = jnp.concatenate(backs, axis=2).astype(jnp.float32)
     grads = grads.astype(jnp.bfloat16)
     layer_out = jnp.zeros((tokens.shape[0], width), jnp.float32).at[chosen].add(scales * back[0])

time: 360 us -> 355 us (0.986)
    reduce_scatter x2, waiting for transfers between devices: 42.8 us -> 47 us  [bring_back(): lax.psum_scatter(partial_rows.reshape(2, SPLIT, 2, -1, half), 'col', scat...]
    unnamed x42 -> x46, local copies, waits for them, and re-layouts: 8.2 us -> 7.95 us
  transfers between devices with their start and end apart: 7 -> 7, of which waited for: 5 -> 5; matrix products, arithmetic and copies ran while one was open for 14% -> 15% of each run, Pallas kernels for 36% -> 36%
where the time goes in v11:
time: 355 us; the launch traced here: 350 us
  Pallas kernels  134 us (38%)
  waiting for transfers between devices  81.5 us (23%)
  local copies, waits for them, and re-layouts  41.1 us (12%)
  other arithmetic  32.2 us (9%)
  starting transfers between devices  20.4 us (6%)
  between operations  14.5 us (4%)
  blocking collectives  13.5 us (4%)
  matrix products  13.2 us (4%)
    pallas_call x8, Pallas kernels, swap_with_partner(): pl.pallas_call(swap_kernel, out_shape=jax.ShapeDtypeStruct(x.shape, x.dty...  134 us
    reduce_scatter x2, waiting for transfers between devices, bring_back(): lax.psum_scatter(partial_rows.reshape(2, SPLIT, 2, -1, half), 'col', scat...  47 us
    all_gather x2, waiting for transfers between devices, expert_chunk(): shared = lax.all_gather(arrived, 'col', axis=1, tiled=False)  13.8 us
    all_to_all x1, blocking collectives, shards(): lax.all_to_all(chunk, 'yx', split_axis=1, concat_axis=1, tiled=True)  13.5 us
    all_to_all x2, starting transfers between devices, shards(): back = lax.all_to_all(rows, 'yx', split_axis=1, concat_axis=1, tiled=True)  13 us
    all_to_all x1, waiting for transfers between devices, shards(): lax.all_to_all(chunk, 'yx', split_axis=1, concat_axis=1, tiled=True)  11.5 us
    all_to_all x2, waiting for transfers between devices, shards(): back = lax.all_to_all(rows, 'yx', split_axis=1, concat_axis=1, tiled=True)  9.13 us
    unnamed x46, local copies, waits for them, and re-layouts  7.95 us
  transfers between devices with their start and end apart: 7, of which 5 were waited for; matrix products, arithmetic and copies ran while one was open for 15% of the time, Pallas kernels for 36%

profile of v11, /device:TPU:32, one launch (start us, length us, event | category | flops | bytes accessed | tf_op | source)
XLA Modules:
  0.0 350.1 jit_solution(9675620093001336136)
XLA Ops:
  7.2 0.9 compare_select_fusion.2
  8.2 0.8 fusion.114
  9.2 2.3 gather_fusion.1
  12.4 1.3 copy.60
  13.7 7.0 %all-to-all-start = ((bf16[2,32,4096]{2,0,1:T(2,128)(2,1)}), bf16[2,32,4096]{2,0,1:T(2,128)(2,1)S(1)}, u32[]{:S(2)}, u32[]{:S(2)}) async-start(bf16[2,32,4096]{2,0,1:T(2,128)(2,1)} %copy.60), calls=%async_computation | async-start | bytes 1048576 | tf_op jit(solution)/shard_map/all_to_all | solution.py:134
  20.8 11.5 %all-to-all-done = bf16[2,32,4096]{2,0,1:T(2,128)(2,1)S(1)} async-done(((bf16[2,32,4096]{2,0,1:T(2,128)(2,1)}), bf16[2,32,4096]{2,0,1:T(2,128)(2,1)S(1)}, u32[]{:S(2)}, u32[]{:S(2)}) %all-to-all-start) | async-done | bytes 524320 | tf_op jit(solution)/shard_map/all_to_all | solution.py:134
  32.9 0.7 slice_bitcast_fusion.5
  33.7 7.1 %shard_map.110 = bf16[2,32,2048]{2,1,0:T(8,128)(2,1)} custom-call(bf16[2,32,2048]{2,1,0:T(8,128)(2,1)} %get-tuple-element.58.src_ref), custom_call_target="tpu_custom_call" | custom-call | bytes 524288 | tf_op jit(solution)/shard_map/pallas_call | solution.py:36
  40.7 1.8 pad_maximum_fusion.7
  45.1 13.5 %all_to_all.20 = bf16[2,32,4096]{2,0,1:T(2,128)(2,1)S(1)} all-to-all(bf16[2,32,4096]{2,0,1:T(2,128)(2,1)S(1)} %copy.72), channel_id=1, replica_groups=mesh['dp'=2,'yx'=16,'col'=8] {'yx'}, dimensions={1} | all-to-all | bytes 1048576 | tf_op jit(solution)/shard_map/all_to_all | solution.py:134
  59.3 0.7 slice_bitcast_fusion.2
  60.0 24.9 %shard_map.114 = bf16[2,32,2048]{2,1,0:T(8,128)(2,1)} custom-call(bf16[2,32,2048]{2,1,0:T(8,128)(2,1)} %get-tuple-element.56.src_ref), custom_call_target="tpu_custom_call" | custom-call | bytes 524288 | tf_op jit(solution)/shard_map/pallas_call | solution.py:36
  85.0 1.8 pad_maximum_fusion.9
  86.9 13.8 %all-gather.5.cloned.1.call-done = bf16[2,16,32,2048]{3,2,0,1:T(8,128)(2,1)} async-done(((bf16[2,2,32,2048]{3,2,0,1:T(8,128)(2,1)}), bf16[2,16,32,2048]{3,2,0,1:T(8,128)(2,1)}) %all-gather.5.cloned.1.call-update) | async-done | bytes 4194320 | tf_op jit(solution)/shard_map/all_gather | solution.py:70
  100.7 2.7 fusion.108
  107.1 0.8 fusion.60.src_ref
  107.9 23.9 %shard_map.111 = bf16[3,8,32,256]{3,2,1,0:T(8,128)(2,1)} custom-call(bf16[3,8,32,256]{3,2,1,0:T(8,128)(2,1)} %fusion.60.src_ref), custom_call_target="tpu_custom_call" | custom-call | bytes 786432 | tf_op jit(solution)/shard_map/pallas_call | solution.py:36
  131.8 1.1 fusion.49
  133.1 0.8 pad_maximum_fusion.10.src_ref
  133.9 25.3 %shard_map.112 = bf16[3,256,256]{2,1,0:T(8,128)(2,1)} custom-call(bf16[3,256,256]{2,1,0:T(8,128)(2,1)} %pad_maximum_fusion.10.src_ref), custom_call_target="tpu_custom_call" | custom-call | bytes 786432 | tf_op jit(solution)/shard_map/pallas_call | solution.py:36
  159.4 1.1 pad_maximum_fusion.4
  160.5 1.0 fusion.111
  161.5 0.7 convolution_convert_fusion.1
  162.7 0.7 fusion.40
  163.9 0.7 add_convert_fusion.1
  164.7 2.3 pad_maximum_fusion
  167.3 2.7 fusion.109
  173.0 0.8 fusion.61.src_ref
  173.8 20.0 %shard_map.115 = bf16[3,8,32,256]{3,2,1,0:T(8,128)(2,1)} custom-call(bf16[3,8,32,256]{3,2,1,0:T(8,128)(2,1)} %fusion.61.src_ref), custom_call_target="tpu_custom_call" | custom-call | bytes 786432 | tf_op jit(solution)/shard_map/pallas_call | solution.py:36
  193.8 1.1 fusion.48
  195.1 0.8 pad_maximum_fusion.11.src_ref
  195.9 19.0 %shard_map.116 = bf16[3,256,256]{2,1,0:T(8,128)(2,1)} custom-call(bf16[3,256,256]{2,1,0:T(8,128)(2,1)} %pad_maximum_fusion.11.src_ref), custom_call_target="tpu_custom_call" | custom-call | bytes 786432 | tf_op jit(solution)/shard_map/pallas_call | solution.py:36
  215.1 1.1 pad_maximum_fusion.5
  216.5 0.7 convolution_convert_fusion
  219.7 2.4 pad_maximum_fusion.1
  223.7 0.7 convolution_bitcast_fusion.5
  225.4 0.9 copy-done.11
  227.0 0.9 copy-done.17
  228.7 0.9 copy-done.15
  230.3 0.7 convolution_bitcast_fusion.2
  231.1 0.9 maximum_add_fusion
  232.0 4.2 %reduce-scatter.3.cloned.1.call-done = bf16[2,1,2,32,2048]{4,3,0,2,1:T(8,128)(2,1)} async-done(((bf16[2,8,2,32,2048]{4,3,0,2,1:T(8,128)(2,1)}), bf16[2,1,2,32,2048]{4,3,0,2,1:T(8,128)(2,1)}) %reduce-scatter.3.cloned.1.call-update) | async-done | bytes 524304 | tf_op jit(solution)/shard_map/reduce_scatter | solution.py:107
  236.2 1.8 slice_bitcast_fusion.3
  238.0 6.7 %shard_map.113 = bf16[2,32,2048]{2,1,0:T(8,128)(2,1)} custom-call(bf16[2,32,2048]{2,1,0:T(8,128)(2,1)} %get-tuple-element.45.src_ref), custom_call_target="tpu_custom_call" | custom-call | bytes 524288 | tf_op jit(solution)/shard_map/pallas_call | solution.py:36
  244.7 1.3 fusion.55
  246.0 1.3 copy.69
  247.4 5.9 %all-to-all-start.1 = ((bf16[2,32,4096]{2,0,1:T(2,128)(2,1)}), bf16[2,32,4096]{2,0,1:T(2,128)(2,1)}, u32[]{:S(2)}, u32[]{:S(2)}) async-start(bf16[2,32,4096]{2,0,1:T(2,128)(2,1)} %copy.69), calls=%async_computation.2 | async-start | bytes 1048576 | tf_op jit(solution)/shard_map/all_to_all | solution.py:144
  253.3 42.8 %reduce-scatter.5.cloned.1.call-done = bf16[2,1,2,32,2048]{4,3,0,2,1:T(8,128)(2,1)} async-done(((bf16[2,8,2,32,2048]{4,3,0,2,1:T(8,128)(2,1)}), bf16[2,1,2,32,2048]{4,3,0,2,1:T(8,128)(2,1)}) %reduce-scatter.5.cloned.1.call-update) | async-done | bytes 524304 | tf_op jit(solution)/shard_map/reduce_scatter | solution.py:107
  296.1 1.8 slice_bitcast_fusion.6
  297.9 6.7 %shard_map.117 = bf16[2,32,2048]{2,1,0:T(8,128)(2,1)} custom-call(bf16[2,32,2048]{2,1,0:T(8,128)(2,1)} %get-tuple-element.47.src_ref), custom_call_target="tpu_custom_call" | custom-call | bytes 524288 | tf_op jit(solution)/shard_map/pallas_call | solution.py:36
  304.6 1.3 fusion.51
  306.0 1.3 copy.88
  307.3 7.1 %all-to-all-start.3 = ((bf16[2,32,4096]{2,0,1:T(2,128)(2,1)}), bf16[2,32,4096]{2,0,1:T(2,128)(2,1)}, u32[]{:S(2)}, u32[]{:S(2)}) async-start(bf16[2,32,4096]{2,0,1:T(2,128)(2,1)} %copy.88), calls=%async_computation.5 | async-start | bytes 1048576 | tf_op jit(solution)/shard_map/all_to_all | solution.py:144
  314.4 1.7 fusion.110
  316.1 9.1 %all-to-all-done.3 = bf16[2,32,4096]{2,0,1:T(2,128)(2,1)} async-done(((bf16[2,32,4096]{2,0,1:T(2,128)(2,1)}), bf16[2,32,4096]{2,0,1:T(2,128)(2,1)}, u32[]{:S(2)}, u32[]{:S(2)}) %all-to-all-start.3) | async-done | bytes 524320 | tf_op jit(solution)/shard_map/all_to_all | solution.py:144
  325.3 2.3 maximum_convert_fusion
  327.6 4.0 %slice_reduce_fusion = (f32[16,4,4096]{2,1,0:T(4,128)S(1)}, f32[1,16,4,4096]{3,0,2,1:T(1,128)S(1)}) fusion(f32[2,16,4,4096]{3,0,2,1:T(2,128)S(1)} %maximum_convert_fusion), kind=kLoop, calls=%fused_computation.39 | loop fusion | bytes 4194304 | tf_op jit(solution)/shard_map/slice | solution.py:149
  331.6 0.8 bitcast_multiply_fusion
  332.4 1.3 reshape.771
  333.7 3.1 scatter_custom_fusion
  336.8 1.1 convert_element_type.227
  337.9 1.3 reshape.779
  339.3 3.2 scatter_custom_fusion.1
  342.4 1.1 convert_element_type.228
  (106 shorter events, 21.0 us)
Async XLA Ops:
  7.2 99.0 %copy-start = (bf16[1,2048,256]{2,1,0:T(8,128)(2,1)S(1)}, bf16[1,2048,256]{2,1,0:T(8,128)(2,1)}, u32[]{:S(2)}) copy-start(bf16[1,2048,256]{2,1,0:T(8,128)(2,1)} %param.14) | copy-start | bytes 3145732
  7.2 4.3 %copy-start.3 = (bf16[128,4096]{1,0:T(8,128)(2,1)S(1)}, bf16[128,4096]{1,0:T(8,128)(2,1)}, u32[]{:S(2)}) copy-start(bf16[128,4096]{1,0:T(8,128)(2,1)} %param.9) | copy-start | bytes 3145732
  13.7 18.6 %all-to-all-start = ((bf16[2,32,4096]{2,0,1:T(2,128)(2,1)}), bf16[2,32,4096]{2,0,1:T(2,128)(2,1)S(1)}, u32[]{:S(2)}, u32[]{:S(2)}) async-start(bf16[2,32,4096]{2,0,1:T(2,128)(2,1)} %copy.60), calls=%async_computation | async-start | bytes 1048576 | tf_op jit(solution)/shard_map/all_to_all | solution.py:134
  20.8 79.9 %all-gather.5.cloned.1.call-start = ((), (), s32[]{:S(2)}) async-start(), calls=%async_computation.8 | async-start | bytes 4718592 | tf_op jit(solution)/shard_map/all_gather | solution.py:70
  32.6 10.2 %copy-start.2 = (bf16[128,4096]{1,0:T(8,128)(2,1)S(1)}, bf16[128,4096]{1,0:T(8,128)(2,1)}, u32[]{:S(2)}) copy-start(bf16[128,4096]{1,0:T(8,128)(2,1)} %param.15) | copy-start | bytes 3145732
  42.6 124.7 %all-gather.7.cloned.1.call-start = ((), (), s32[]{:S(2)}) async-start(), calls=%async_computation.9 | async-start | bytes 4718592 | tf_op jit(solution)/shard_map/all_gather | solution.py:70
  86.8 16.6 %copy-start.4 = (bf16[1,2048,256]{2,1,0:T(8,128)(2,1)S(1)}, bf16[1,2048,256]{2,1,0:T(8,128)(2,1)}, u32[]{:S(2)}) copy-start(bf16[1,2048,256]{2,1,0:T(8,128)(2,1)} %param.12) | copy-start | bytes 3145732
  86.8 149.4 %reduce-scatter.3.cloned.1.call-start = ((), (), s32[]{:S(2)}) async-start(), calls=%async_computation.6 | async-start | bytes 4718592 | tf_op jit(solution)/shard_map/reduce_scatter | solution.py:107
  103.4 1.4 copy-start.12
  103.4 2.8 copy-start.10
  103.4 2.0 copy-start.7
  161.5 1.2 copy-start.5
  162.7 1.2 copy-start.8
  167.1 129.1 %reduce-scatter.5.cloned.1.call-start = ((), (), s32[]{:S(2)}) async-start(), calls=%async_computation.7 | async-start | bytes 4718592 | tf_op jit(solution)/shard_map/reduce_scatter | solution.py:107
  170.0 1.3 copy-start.14
  170.1 2.0 copy-start.16
  216.4 1.2 copy-start.6
  217.7 1.2 copy-start.9
  222.1 0.7 copy-start.21
  222.1 0.8 copy-start.22
  222.1 1.7 copy-start.13
  222.1 1.7 copy-start.20
  223.7 1.0 copy-start.19
  224.7 1.6 copy-start.11
  224.7 1.6 copy-start.18
  226.3 1.6 copy-start.17
  227.9 1.6 copy-start.15
  247.4 59.9 %all-to-all-start.1 = ((bf16[2,32,4096]{2,0,1:T(2,128)(2,1)}), bf16[2,32,4096]{2,0,1:T(2,128)(2,1)}, u32[]{:S(2)}, u32[]{:S(2)}) async-start(bf16[2,32,4096]{2,0,1:T(2,128)(2,1)} %copy.69), calls=%async_computation.2 | async-start | bytes 1048576 | tf_op jit(solution)/shard_map/all_to_all | solution.py:144
  307.3 18.0 %all-to-all-start.3 = ((bf16[2,32,4096]{2,0,1:T(2,128)(2,1)}), bf16[2,32,4096]{2,0,1:T(2,128)(2,1)}, u32[]{:S(2)}, u32[]{:S(2)}) async-start(bf16[2,32,4096]{2,0,1:T(2,128)(2,1)} %copy.88), calls=%async_computation.5 | async-start | bytes 1048576 | tf_op jit(solution)/shard_map/all_to_all | solution.py:144
  339.3 4.3 %copy-start.1 = (bf16[1,2048,256]{2,1,0:T(8,128)(2,1)S(1)}, bf16[1,2048,256]{2,1,0:T(8,128)(2,1)}, u32[]{:S(2)}) copy-start(bf16[1,2048,256]{2,1,0:T(8,128)(2,1)} %param.14) | copy-start | bytes 3145732
Sparse Core Ops, SparseCore 0:
  42.7 57.9 all-gather.4
  103.1 58.4 all-gather.6
  167.2 68.9 reduce-scatter.2
  238.6 57.4 reduce-scatter.4

commit v12 on v11

--- a/solution.py
+++ b/solution.py
@@ -51,6 +51,13 @@
     return (split[:, :, 0] + traded.astype(jnp.float32)).reshape(streams, -1, k)
 
 
+def all_batches(partial, collective_id):
+    streams, rows, k = partial.shape
+    split = partial.reshape(streams, SPLIT, 2, -1, k)
+    traded = swap_with_partner(split.astype(jnp.bfloat16), collective_id)
+    return (split + traded[:, :, ::-1].astype(jnp.float32)).reshape(streams, -1, k)
+
+
 def both_batches(values, collective_id):
     traded = swap_with_partner(values, collective_id)
     streams, rows, k = values.shape
@@ -76,14 +83,13 @@
             jnp.dot(cot_rows, wd, preferred_element_type=jnp.float32),
         ]
     )
-    gate_pre, up_pre, hidden_grad = own_batch(partials, first_id + 1)
+    gate_pre, up_pre, hidden_grad = all_batches(partials, first_id + 1)
     gate_sigma = jax.nn.sigmoid(gate_pre)
-    hidden = (gate_pre * gate_sigma * up_pre).astype(jnp.bfloat16)
-    gate_rows = (hidden_grad * up_pre * gate_sigma * (1.0 + gate_pre * (1.0 - gate_sigma))).astype(
+    hidden_all = (gate_pre * gate_sigma * up_pre).astype(jnp.bfloat16)
+    gate_all = (hidden_grad * up_pre * gate_sigma * (1.0 + gate_pre * (1.0 - gate_sigma))).astype(
         jnp.bfloat16
     )
-    up_rows = (hidden_grad * gate_pre * gate_sigma).astype(jnp.bfloat16)
-    hidden_all, gate_all, up_all = both_batches(jnp.stack([hidden, gate_rows, up_rows]), first_id + 2)
+    up_all = (hidden_grad * gate_pre * gate_sigma).astype(jnp.bfloat16)
     partial_value = lax.dot_general(
         hidden_all, wd, CONTRACT_LAST, preferred_element_type=jnp.float32
     ).astype(jnp.bfloat16)

time: 355 us -> 353 us (level)
    pallas_call x8 -> x6, Pallas kernels: 134 us -> 134 us  [swap_with_partner(): pl.pallas_call(swap_kernel, out_shape=jax.ShapeDtypeStruct(x.shape, x.dty...]
    unnamed x46 -> x64, local copies, waits for them, and re-layouts: 7.95 us -> 7.79 us
  transfers between devices with their start and end apart: 7 -> 7, of which waited for: 5 -> 5; matrix products, arithmetic and copies ran while one was open for 15% -> 13% of each run, Pallas kernels for 36% -> 36%
where the time goes in v12:
time: 353 us; the launch traced here: 349 us
  Pallas kernels  134 us (38%)
  waiting for transfers between devices  82.7 us (23%)
  local copies, waits for them, and re-layouts  37.9 us (11%)
  other arithmetic  31.5 us (9%)
  starting transfers between devices  21.9 us (6%)
  between operations  14.5 us (4%)
  blocking collectives  13.5 us (4%)
  matrix products  13.3 us (4%)
    pallas_call x6, Pallas kernels, swap_with_partner(): pl.pallas_call(swap_kernel, out_shape=jax.ShapeDtypeStruct(x.shape, x.dty...  134 us
    reduce_scatter x2, waiting for transfers between devices, bring_back(): lax.psum_scatter(partial_rows.reshape(2, SPLIT, 2, -1, half), 'col', scat...  48 us
    all_to_all x2, starting transfers between devices, shards(): back = lax.all_to_all(rows, 'yx', split_axis=1, concat_axis=1, tiled=True)  14.5 us
    all_gather x2, waiting for transfers between devices, expert_chunk(): shared = lax.all_gather(arrived, 'col', axis=1, tiled=False)  13.8 us
    all_to_all x1, blocking collectives, shards(): lax.all_to_all(chunk, 'yx', split_axis=1, concat_axis=1, tiled=True)  13.5 us
    all_to_all x1, waiting for transfers between devices, shards(): lax.all_to_all(chunk, 'yx', split_axis=1, concat_axis=1, tiled=True)  11.5 us
    all_to_all x2, waiting for transfers between devices, shards(): back = lax.all_to_all(rows, 'yx', split_axis=1, concat_axis=1, tiled=True)  9.38 us
    unnamed x64, local copies, waits for them, and re-layouts  7.79 us
  transfers between devices with their start and end apart: 7, of which 5 were waited for; matrix products, arithmetic and copies ran while one was open for 13% of the time, Pallas kernels for 36%

profile of v12, /device:TPU:32, one launch (start us, length us, event | category | flops | bytes accessed | tf_op | source)
XLA Modules:
  0.0 349.3 jit_solution(15527571317506688659)
XLA Ops:
  7.2 0.9 compare_select_fusion.2
  8.2 0.8 fusion.39
  9.2 2.3 gather_fusion.1
  12.4 1.3 copy.28
  13.7 7.0 %all-to-all-start = ((bf16[2,32,4096]{2,0,1:T(2,128)(2,1)}), bf16[2,32,4096]{2,0,1:T(2,128)(2,1)S(1)}, u32[]{:S(2)}, u32[]{:S(2)}) async-start(bf16[2,32,4096]{2,0,1:T(2,128)(2,1)} %copy.28), calls=%async_computation | async-start | bytes 1048576 | tf_op jit(solution)/shard_map/all_to_all | solution.py:140
  20.8 11.5 %all-to-all-done = bf16[2,32,4096]{2,0,1:T(2,128)(2,1)S(1)} async-done(((bf16[2,32,4096]{2,0,1:T(2,128)(2,1)}), bf16[2,32,4096]{2,0,1:T(2,128)(2,1)S(1)}, u32[]{:S(2)}, u32[]{:S(2)}) %all-to-all-start) | async-done | bytes 524320 | tf_op jit(solution)/shard_map/all_to_all | solution.py:140
  32.9 0.7 slice_bitcast_fusion.3
  33.7 7.1 %shard_map.110 = bf16[2,32,2048]{2,1,0:T(8,128)(2,1)} custom-call(bf16[2,32,2048]{2,1,0:T(8,128)(2,1)} %get-tuple-element.34.src_ref), custom_call_target="tpu_custom_call" | custom-call | bytes 524288 | tf_op jit(solution)/shard_map/pallas_call | solution.py:36
  40.7 1.8 pad_maximum_fusion.5
  45.1 13.5 %all_to_all.20 = bf16[2,32,4096]{2,0,1:T(2,128)(2,1)S(1)} all-to-all(bf16[2,32,4096]{2,0,1:T(2,128)(2,1)S(1)} %copy.34), channel_id=1, replica_groups=mesh['dp'=2,'yx'=16,'col'=8] {'yx'}, dimensions={1} | all-to-all | bytes 1048576 | tf_op jit(solution)/shard_map/all_to_all | solution.py:140
  59.3 0.7 slice_bitcast_fusion
  60.0 24.9 %shard_map.113 = bf16[2,32,2048]{2,1,0:T(8,128)(2,1)} custom-call(bf16[2,32,2048]{2,1,0:T(8,128)(2,1)} %get-tuple-element.32.src_ref), custom_call_target="tpu_custom_call" | custom-call | bytes 524288 | tf_op jit(solution)/shard_map/pallas_call | solution.py:36
  85.0 1.8 pad_maximum_fusion.7
  86.9 13.8 %all-gather.5.cloned.1.call-done = bf16[2,16,32,2048]{3,2,0,1:T(8,128)(2,1)} async-done(((bf16[2,2,32,2048]{3,2,0,1:T(8,128)(2,1)}), bf16[2,16,32,2048]{3,2,0,1:T(8,128)(2,1)}) %all-gather.5.cloned.1.call-update) | async-done | bytes 4194320 | tf_op jit(solution)/shard_map/all_gather | solution.py:77
  100.7 2.7 fusion.36
  104.2 1.3 copy-done.4
  107.0 0.8 copy-done.10
  107.8 1.0 fusion.1.src_ref
  108.8 51.0 %shard_map.111 = bf16[3,8,2,32,256]{4,3,2,1,0:T(8,128)(2,1)} custom-call(bf16[3,8,2,32,256]{4,3,2,1,0:T(8,128)(2,1)} %fusion.1.src_ref), custom_call_target="tpu_custom_call" | custom-call | bytes 1572864 | tf_op jit(solution)/shard_map/pallas_call | solution.py:36
  159.8 1.9 convert_add_fusion.1
  162.0 0.7 convolution_convert_fusion.1
  162.8 0.7 fusion.12
  163.6 0.8 add_convert_fusion.1
  164.3 2.3 pad_maximum_fusion
  166.9 2.7 fusion.37
  172.4 0.8 copy-done.11
  173.2 1.0 fusion.src_ref
  174.2 34.0 %shard_map.114 = bf16[3,8,2,32,256]{4,3,2,1,0:T(8,128)(2,1)} custom-call(bf16[3,8,2,32,256]{4,3,2,1,0:T(8,128)(2,1)} %fusion.src_ref), custom_call_target="tpu_custom_call" | custom-call | bytes 1572864 | tf_op jit(solution)/shard_map/pallas_call | solution.py:36
  208.2 1.9 convert_add_fusion
  210.5 0.7 convolution_convert_fusion
  211.2 0.7 fusion.14
  212.0 0.8 add_convert_fusion
  212.8 2.4 pad_maximum_fusion.1
  216.8 0.7 convolution_bitcast_fusion.5
  218.5 0.9 copy-done.13
  219.4 0.7 convolution_bitcast_fusion.3
  220.2 0.9 copy-done.19
  221.1 0.7 convolution_bitcast_fusion
  221.8 0.8 copy-done.17
  222.7 0.7 convolution_bitcast_fusion.1
  223.6 0.7 convolution_bitcast_fusion.2
  225.1 7.3 %reduce-scatter.3.cloned.1.call-done = bf16[2,1,2,32,2048]{4,3,0,2,1:T(8,128)(2,1)} async-done(((bf16[2,8,2,32,2048]{4,3,0,2,1:T(8,128)(2,1)}), bf16[2,1,2,32,2048]{4,3,0,2,1:T(8,128)(2,1)}) %reduce-scatter.3.cloned.1.call-update) | async-done | bytes 524304 | tf_op jit(solution)/shard_map/reduce_scatter | solution.py:113
  232.3 1.8 slice_bitcast_fusion.1
  234.1 9.8 %shard_map.112 = bf16[2,32,2048]{2,1,0:T(8,128)(2,1)} custom-call(bf16[2,32,2048]{2,1,0:T(8,128)(2,1)} %get-tuple-element.27.src_ref), custom_call_target="tpu_custom_call" | custom-call | bytes 524288 | tf_op jit(solution)/shard_map/pallas_call | solution.py:36
  243.9 1.3 fusion.25
  245.2 1.3 copy.31
  246.6 7.5 %all-to-all-start.1 = ((bf16[2,32,4096]{2,0,1:T(2,128)(2,1)}), bf16[2,32,4096]{2,0,1:T(2,128)(2,1)}, u32[]{:S(2)}, u32[]{:S(2)}) async-start(bf16[2,32,4096]{2,0,1:T(2,128)(2,1)} %copy.31), calls=%async_computation.2 | async-start | bytes 1048576 | tf_op jit(solution)/shard_map/all_to_all | solution.py:150
  254.1 40.7 %reduce-scatter.5.cloned.1.call-done = bf16[2,1,2,32,2048]{4,3,0,2,1:T(8,128)(2,1)} async-done(((bf16[2,8,2,32,2048]{4,3,0,2,1:T(8,128)(2,1)}), bf16[2,1,2,32,2048]{4,3,0,2,1:T(8,128)(2,1)}) %reduce-scatter.5.cloned.1.call-update) | async-done | bytes 524304 | tf_op jit(solution)/shard_map/reduce_scatter | solution.py:113
  294.8 1.8 slice_bitcast_fusion.4
  296.6 7.0 %shard_map.115 = bf16[2,32,2048]{2,1,0:T(8,128)(2,1)} custom-call(bf16[2,32,2048]{2,1,0:T(8,128)(2,1)} %get-tuple-element.29.src_ref), custom_call_target="tpu_custom_call" | custom-call | bytes 524288 | tf_op jit(solution)/shard_map/pallas_call | solution.py:36
  303.6 1.3 fusion.21
  305.0 1.3 copy.37
  306.3 7.1 %all-to-all-start.3 = ((bf16[2,32,4096]{2,0,1:T(2,128)(2,1)}), bf16[2,32,4096]{2,0,1:T(2,128)(2,1)}, u32[]{:S(2)}, u32[]{:S(2)}) async-start(bf16[2,32,4096]{2,0,1:T(2,128)(2,1)} %copy.37), calls=%async_computation.5 | async-start | bytes 1048576 | tf_op jit(solution)/shard_map/all_to_all | solution.py:150
  313.4 1.7 fusion.38
  315.1 9.4 %all-to-all-done.3 = bf16[2,32,4096]{2,0,1:T(2,128)(2,1)} async-done(((bf16[2,32,4096]{2,0,1:T(2,128)(2,1)}), bf16[2,32,4096]{2,0,1:T(2,128)(2,1)}, u32[]{:S(2)}, u32[]{:S(2)}) %all-to-all-start.3) | async-done | bytes 524320 | tf_op jit(solution)/shard_map/all_to_all | solution.py:150
  324.5 2.3 maximum_convert_fusion
  326.8 4.0 %slice_reduce_fusion = (f32[16,4,4096]{2,1,0:T(4,128)S(1)}, f32[1,16,4,4096]{3,0,2,1:T(1,128)S(1)}) fusion(f32[2,16,4,4096]{3,0,2,1:T(2,128)S(1)} %maximum_convert_fusion), kind=kLoop, calls=%fused_computation.31 | loop fusion | bytes 4194304 | tf_op jit(solution)/shard_map/slice | solution.py:155
  330.8 0.8 bitcast_multiply_fusion
  331.6 1.3 reshape.303
  332.9 3.1 scatter_custom_fusion
  336.0 1.1 convert_element_type.155
  337.1 1.3 reshape.311
  338.5 3.2 scatter_custom_fusion.1
  341.6 1.1 convert_element_type.156
  (104 shorter events, 14.3 us)
Async XLA Ops:
  7.2 99.1 %copy-start = (bf16[1,2048,256]{2,1,0:T(8,128)(2,1)S(1)}, bf16[1,2048,256]{2,1,0:T(8,128)(2,1)}, u32[]{:S(2)}) copy-start(bf16[1,2048,256]{2,1,0:T(8,128)(2,1)} %param.14) | copy-start | bytes 3145732
  7.2 4.3 %copy-start.3 = (bf16[128,4096]{1,0:T(8,128)(2,1)S(1)}, bf16[128,4096]{1,0:T(8,128)(2,1)}, u32[]{:S(2)}) copy-start(bf16[128,4096]{1,0:T(8,128)(2,1)} %param.9) | copy-start | bytes 3145732
  13.7 18.6 %all-to-all-start = ((bf16[2,32,4096]{2,0,1:T(2,128)(2,1)}), bf16[2,32,4096]{2,0,1:T(2,128)(2,1)S(1)}, u32[]{:S(2)}, u32[]{:S(2)}) async-start(bf16[2,32,4096]{2,0,1:T(2,128)(2,1)} %copy.28), calls=%async_computation | async-start | bytes 1048576 | tf_op jit(solution)/shard_map/all_to_all | solution.py:140
  20.8 79.9 %all-gather.5.cloned.1.call-start = ((), (), s32[]{:S(2)}) async-start(), calls=%async_computation.8 | async-start | bytes 4718592 | tf_op jit(solution)/shard_map/all_gather | solution.py:77
  32.6 10.2 %copy-start.2 = (bf16[128,4096]{1,0:T(8,128)(2,1)S(1)}, bf16[128,4096]{1,0:T(8,128)(2,1)}, u32[]{:S(2)}) copy-start(bf16[128,4096]{1,0:T(8,128)(2,1)} %param.15) | copy-start | bytes 3145732
  42.6 124.4 %all-gather.7.cloned.1.call-start = ((), (), s32[]{:S(2)}) async-start(), calls=%async_computation.9 | async-start | bytes 4718592 | tf_op jit(solution)/shard_map/all_gather | solution.py:77
  86.8 16.6 %copy-start.5 = (bf16[1,2048,256]{2,1,0:T(8,128)(2,1)S(1)}, bf16[1,2048,256]{2,1,0:T(8,128)(2,1)}, u32[]{:S(2)}) copy-start(bf16[1,2048,256]{2,1,0:T(8,128)(2,1)} %param.13) | copy-start | bytes 3145732
  86.8 145.5 %reduce-scatter.3.cloned.1.call-start = ((), (), s32[]{:S(2)}) async-start(), calls=%async_computation.6 | async-start | bytes 4718592 | tf_op jit(solution)/shard_map/reduce_scatter | solution.py:113
  103.4 2.8 copy-start.14
  103.4 2.8 copy-start.12
  103.4 2.0 copy-start.4
  105.5 1.5 copy-start.6
  106.2 0.8 copy-start.7
  107.0 0.8 copy-start.10
  162.0 1.5 copy-start.22
  162.0 1.5 copy-start.26
  166.7 128.1 %reduce-scatter.5.cloned.1.call-start = ((), (), s32[]{:S(2)}) async-start(), calls=%async_computation.7 | async-start | bytes 4718592 | tf_op jit(solution)/shard_map/reduce_scatter | solution.py:113
  169.7 1.5 copy-start.16
  169.7 1.9 copy-start.18
  170.4 1.9 copy-start.8
  171.2 1.2 copy-start.9
  172.4 0.8 copy-start.11
  210.4 1.5 copy-start.20
  210.4 1.5 copy-start.24
  210.5 1.5 copy-start.28
  215.1 0.7 copy-start.30
  215.1 0.8 copy-start.31
  215.2 1.7 copy-start.15
  215.2 1.7 copy-start.23
  216.8 1.0 copy-start.27
  217.8 1.6 copy-start.13
  219.4 1.6 copy-start.19
  219.4 1.6 copy-start.21
  221.1 1.6 copy-start.17
  221.1 1.6 copy-start.29
  222.7 1.0 copy-start.25
  246.6 59.7 %all-to-all-start.1 = ((bf16[2,32,4096]{2,0,1:T(2,128)(2,1)}), bf16[2,32,4096]{2,0,1:T(2,128)(2,1)}, u32[]{:S(2)}, u32[]{:S(2)}) async-start(bf16[2,32,4096]{2,0,1:T(2,128)(2,1)} %copy.31), calls=%async_computation.2 | async-start | bytes 1048576 | tf_op jit(solution)/shard_map/all_to_all | solution.py:150
  306.3 18.2 %all-to-all-start.3 = ((bf16[2,32,4096]{2,0,1:T(2,128)(2,1)}), bf16[2,32,4096]{2,0,1:T(2,128)(2,1)}, u32[]{:S(2)}, u32[]{:S(2)}) async-start(bf16[2,32,4096]{2,0,1:T(2,128)(2,1)} %copy.37), calls=%async_computation.5 | async-start | bytes 1048576 | tf_op jit(solution)/shard_map/all_to_all | solution.py:150
  338.5 4.3 %copy-start.1 = (bf16[1,2048,256]{2,1,0:T(8,128)(2,1)S(1)}, bf16[1,2048,256]{2,1,0:T(8,128)(2,1)}, u32[]{:S(2)}) copy-start(bf16[1,2048,256]{2,1,0:T(8,128)(2,1)} %param.14) | copy-start | bytes 3145732
Sparse Core Ops, SparseCore 0:
  42.7 57.9 all-gather.4
  103.1 58.7 all-gather.6
  166.8 65.4 reduce-scatter.2
  234.7 59.9 reduce-scatter.4

commit v13 on v12

--- a/solution.py
+++ b/solution.py
@@ -19,16 +19,22 @@
     barrier = pltpu.get_barrier_semaphore()
     pl.semaphore_signal(barrier, 1, device_id={"dp": other}, device_id_type=MESH_ID)
     pl.semaphore_wait(barrier, 1)
-    copy = pltpu.make_async_remote_copy(
-        src_ref=src_ref,
-        dst_ref=dst_ref,
-        send_sem=sems.at[0],
-        recv_sem=sems.at[1],
-        device_id={"dp": other},
-        device_id_type=MESH_ID,
-    )
-    copy.start()
-    copy.wait()
+    lead = src_ref.shape[0]
+    cut = lead // 2
+    copies = []
+    for i, (start, size) in enumerate(((0, cut), (cut, lead - cut))):
+        copy = pltpu.make_async_remote_copy(
+            src_ref=src_ref.at[pl.ds(start, size)],
+            dst_ref=dst_ref.at[pl.ds(start, size)],
+            send_sem=sems.at[2 * i],
+            recv_sem=sems.at[2 * i + 1],
+            device_id={"dp": other},
+            device_id_type=MESH_ID,
+        )
+        copy.start()
+        copies.append(copy)
+    for copy in copies:
+        copy.wait()
 
 
 def swap_with_partner(x, collective_id):
@@ -38,7 +44,7 @@
         out_shape=jax.ShapeDtypeStruct(x.shape, x.dtype),
         in_specs=[pl.BlockSpec(memory_space=pl.ANY)],
         out_specs=pl.BlockSpec(memory_space=pl.ANY),
-        scratch_shapes=[pltpu.SemaphoreType.DMA((2,))],
+        scratch_shapes=[pltpu.SemaphoreType.DMA((4,))],
         compiler_params=pltpu.CompilerParams(collective_id=collective_id, has_side_effects=True),
         cost_estimate=pl.CostEstimate(flops=0, bytes_accessed=2 * size, transcendentals=0),
     )(x)

time: 353 us -> 353 us (level)
  no operation moved by 1% of the time
where the time goes in v13:
time: 353 us; the launch traced here: 349 us
  Pallas kernels  134 us (38%)
  waiting for transfers between devices  82.6 us (23%)
  local copies, waits for them, and re-layouts  37.9 us (11%)
  other arithmetic  31.5 us (9%)
  starting transfers between devices  22.2 us (6%)
  between operations  14.5 us (4%)
  blocking collectives  13.5 us (4%)
  matrix products  13.3 us (4%)
    pallas_call x6, Pallas kernels, swap_with_partner(): pl.pallas_call(swap_kernel, out_shape=jax.ShapeDtypeStruct(x.shape, x.dty...  134 us
    reduce_scatter x2, waiting for transfers between devices, bring_back(): lax.psum_scatter(partial_rows.reshape(2, SPLIT, 2, -1, half), 'col', scat...  48.2 us
    all_to_all x2, starting transfers between devices, shards(): back = lax.all_to_all(rows, 'yx', split_axis=1, concat_axis=1, tiled=True)  14.9 us
    all_gather x2, waiting for transfers between devices, expert_chunk(): shared = lax.all_gather(arrived, 'col', axis=1, tiled=False)  13.8 us
    all_to_all x1, blocking collectives, shards(): lax.all_to_all(chunk, 'yx', split_axis=1, concat_axis=1, tiled=True)  13.5 us
    all_to_all x1, waiting for transfers between devices, shards(): lax.all_to_all(chunk, 'yx', split_axis=1, concat_axis=1, tiled=True)  11.5 us
    all_to_all x2, waiting for transfers between devices, shards(): back = lax.all_to_all(rows, 'yx', split_axis=1, concat_axis=1, tiled=True)  9.04 us
    unnamed x64, local copies, waits for them, and re-layouts  7.77 us
  transfers between devices with their start and end apart: 7, of which 5 were waited for; matrix products, arithmetic and copies ran while one was open for 13% of the time, Pallas kernels for 36%

profile of v13, /device:TPU:32, one launch (start us, length us, event | category | flops | bytes accessed | tf_op | source)
XLA Modules:
  0.0 349.2 jit_solution(4052845018106356956)
XLA Ops:
  7.2 0.9 compare_select_fusion.2
  8.2 0.8 fusion.39
  9.2 2.3 gather_fusion.1
  12.4 1.3 copy.28
  13.7 7.0 %all-to-all-start = ((bf16[2,32,4096]{2,0,1:T(2,128)(2,1)}), bf16[2,32,4096]{2,0,1:T(2,128)(2,1)S(1)}, u32[]{:S(2)}, u32[]{:S(2)}) async-start(bf16[2,32,4096]{2,0,1:T(2,128)(2,1)} %copy.28), calls=%async_computation | async-start | bytes 1048576 | tf_op jit(solution)/shard_map/all_to_all | solution.py:146
  20.8 11.5 %all-to-all-done = bf16[2,32,4096]{2,0,1:T(2,128)(2,1)S(1)} async-done(((bf16[2,32,4096]{2,0,1:T(2,128)(2,1)}), bf16[2,32,4096]{2,0,1:T(2,128)(2,1)S(1)}, u32[]{:S(2)}, u32[]{:S(2)}) %all-to-all-start) | async-done | bytes 524320 | tf_op jit(solution)/shard_map/all_to_all | solution.py:146
  32.9 0.7 slice_bitcast_fusion.3
  33.7 7.1 %shard_map.110 = bf16[2,32,2048]{2,1,0:T(8,128)(2,1)} custom-call(bf16[2,32,2048]{2,1,0:T(8,128)(2,1)} %get-tuple-element.34.src_ref), custom_call_target="tpu_custom_call" | custom-call | bytes 524288 | tf_op jit(solution)/shard_map/pallas_call | solution.py:42
  40.8 1.8 pad_maximum_fusion.5
  45.2 13.5 %all_to_all.20 = bf16[2,32,4096]{2,0,1:T(2,128)(2,1)S(1)} all-to-all(bf16[2,32,4096]{2,0,1:T(2,128)(2,1)S(1)} %copy.34), channel_id=1, replica_groups=mesh['dp'=2,'yx'=16,'col'=8] {'yx'}, dimensions={1} | all-to-all | bytes 1048576 | tf_op jit(solution)/shard_map/all_to_all | solution.py:146
  59.3 0.7 slice_bitcast_fusion
  60.0 25.0 %shard_map.113 = bf16[2,32,2048]{2,1,0:T(8,128)(2,1)} custom-call(bf16[2,32,2048]{2,1,0:T(8,128)(2,1)} %get-tuple-element.32.src_ref), custom_call_target="tpu_custom_call" | custom-call | bytes 524288 | tf_op jit(solution)/shard_map/pallas_call | solution.py:42
  85.0 1.8 pad_maximum_fusion.7
  86.9 13.8 %all-gather.5.cloned.1.call-done = bf16[2,16,32,2048]{3,2,0,1:T(8,128)(2,1)} async-done(((bf16[2,2,32,2048]{3,2,0,1:T(8,128)(2,1)}), bf16[2,16,32,2048]{3,2,0,1:T(8,128)(2,1)}) %all-gather.5.cloned.1.call-update) | async-done | bytes 4194320 | tf_op jit(solution)/shard_map/all_gather | solution.py:83
  100.7 2.7 fusion.36
  104.2 1.3 copy-done.4
  107.0 0.8 copy-done.10
  107.8 1.0 fusion.1.src_ref
  108.8 51.0 %shard_map.111 = bf16[3,8,2,32,256]{4,3,2,1,0:T(8,128)(2,1)} custom-call(bf16[3,8,2,32,256]{4,3,2,1,0:T(8,128)(2,1)} %fusion.1.src_ref), custom_call_target="tpu_custom_call" | custom-call | bytes 1572864 | tf_op jit(solution)/shard_map/pallas_call | solution.py:42
  159.9 1.9 convert_add_fusion.1
  162.1 0.7 convolution_convert_fusion.1
  162.8 0.7 fusion.12
  163.6 0.8 add_convert_fusion.1
  164.4 2.3 pad_maximum_fusion
  167.0 2.7 fusion.37
  172.4 0.8 copy-done.11
  173.2 1.0 fusion.src_ref
  174.2 34.1 %shard_map.114 = bf16[3,8,2,32,256]{4,3,2,1,0:T(8,128)(2,1)} custom-call(bf16[3,8,2,32,256]{4,3,2,1,0:T(8,128)(2,1)} %fusion.src_ref), custom_call_target="tpu_custom_call" | custom-call | bytes 1572864 | tf_op jit(solution)/shard_map/pallas_call | solution.py:42
  208.3 1.9 convert_add_fusion
  210.5 0.7 convolution_convert_fusion
  211.3 0.7 fusion.14
  212.1 0.8 add_convert_fusion
  212.8 2.4 pad_maximum_fusion.1
  216.9 0.7 convolution_bitcast_fusion.5
  217.8 0.7 convolution_bitcast_fusion.4
  218.6 0.9 copy-done.13
  219.5 0.7 convolution_bitcast_fusion.3
  220.2 0.9 copy-done.19
  221.9 0.8 copy-done.17
  222.7 0.7 convolution_bitcast_fusion.1
  223.7 0.7 convolution_bitcast_fusion.2
  225.1 7.2 %reduce-scatter.3.cloned.1.call-done = bf16[2,1,2,32,2048]{4,3,0,2,1:T(8,128)(2,1)} async-done(((bf16[2,8,2,32,2048]{4,3,0,2,1:T(8,128)(2,1)}), bf16[2,1,2,32,2048]{4,3,0,2,1:T(8,128)(2,1)}) %reduce-scatter.3.cloned.1.call-update) | async-done | bytes 524304 | tf_op jit(solution)/shard_map/reduce_scatter | solution.py:119
  232.3 1.8 slice_bitcast_fusion.1
  234.1 9.8 %shard_map.112 = bf16[2,32,2048]{2,1,0:T(8,128)(2,1)} custom-call(bf16[2,32,2048]{2,1,0:T(8,128)(2,1)} %get-tuple-element.27.src_ref), custom_call_target="tpu_custom_call" | custom-call | bytes 524288 | tf_op jit(solution)/shard_map/pallas_call | solution.py:42
  243.9 1.3 fusion.25
  245.2 1.3 copy.31
  246.5 7.5 %all-to-all-start.1 = ((bf16[2,32,4096]{2,0,1:T(2,128)(2,1)}), bf16[2,32,4096]{2,0,1:T(2,128)(2,1)}, u32[]{:S(2)}, u32[]{:S(2)}) async-start(bf16[2,32,4096]{2,0,1:T(2,128)(2,1)} %copy.31), calls=%async_computation.2 | async-start | bytes 1048576 | tf_op jit(solution)/shard_map/all_to_all | solution.py:156
  254.1 41.1 %reduce-scatter.5.cloned.1.call-done = bf16[2,1,2,32,2048]{4,3,0,2,1:T(8,128)(2,1)} async-done(((bf16[2,8,2,32,2048]{4,3,0,2,1:T(8,128)(2,1)}), bf16[2,1,2,32,2048]{4,3,0,2,1:T(8,128)(2,1)}) %reduce-scatter.5.cloned.1.call-update) | async-done | bytes 524304 | tf_op jit(solution)/shard_map/reduce_scatter | solution.py:119
  295.1 1.8 slice_bitcast_fusion.4
  296.9 6.7 %shard_map.115 = bf16[2,32,2048]{2,1,0:T(8,128)(2,1)} custom-call(bf16[2,32,2048]{2,1,0:T(8,128)(2,1)} %get-tuple-element.29.src_ref), custom_call_target="tpu_custom_call" | custom-call | bytes 524288 | tf_op jit(solution)/shard_map/pallas_call | solution.py:42
  303.6 1.3 fusion.21
  305.0 1.3 copy.37
  306.3 7.3 %all-to-all-start.3 = ((bf16[2,32,4096]{2,0,1:T(2,128)(2,1)}), bf16[2,32,4096]{2,0,1:T(2,128)(2,1)}, u32[]{:S(2)}, u32[]{:S(2)}) async-start(bf16[2,32,4096]{2,0,1:T(2,128)(2,1)} %copy.37), calls=%async_computation.5 | async-start | bytes 1048576 | tf_op jit(solution)/shard_map/all_to_all | solution.py:156
  313.6 1.7 fusion.38
  315.4 9.0 %all-to-all-done.3 = bf16[2,32,4096]{2,0,1:T(2,128)(2,1)} async-done(((bf16[2,32,4096]{2,0,1:T(2,128)(2,1)}), bf16[2,32,4096]{2,0,1:T(2,128)(2,1)}, u32[]{:S(2)}, u32[]{:S(2)}) %all-to-all-start.3) | async-done | bytes 524320 | tf_op jit(solution)/shard_map/all_to_all | solution.py:156
  324.4 2.3 maximum_convert_fusion
  326.7 4.0 %slice_reduce_fusion = (f32[16,4,4096]{2,1,0:T(4,128)S(1)}, f32[1,16,4,4096]{3,0,2,1:T(1,128)S(1)}) fusion(f32[2,16,4,4096]{3,0,2,1:T(2,128)S(1)} %maximum_convert_fusion), kind=kLoop, calls=%fused_computation.31 | loop fusion | bytes 4194304 | tf_op jit(solution)/shard_map/slice | solution.py:161
  330.7 0.8 bitcast_multiply_fusion
  331.5 1.3 reshape.303
  332.9 3.1 scatter_custom_fusion
  336.0 1.1 convert_element_type.155
  337.1 1.3 reshape.311
  338.4 3.2 scatter_custom_fusion.1
  341.6 1.1 convert_element_type.156
  (104 shorter events, 14.3 us)
Async XLA Ops:
  7.2 99.1 %copy-start = (bf16[1,2048,256]{2,1,0:T(8,128)(2,1)S(1)}, bf16[1,2048,256]{2,1,0:T(8,128)(2,1)}, u32[]{:S(2)}) copy-start(bf16[1,2048,256]{2,1,0:T(8,128)(2,1)} %param.14) | copy-start | bytes 3145732
  7.2 4.3 %copy-start.3 = (bf16[128,4096]{1,0:T(8,128)(2,1)S(1)}, bf16[128,4096]{1,0:T(8,128)(2,1)}, u32[]{:S(2)}) copy-start(bf16[128,4096]{1,0:T(8,128)(2,1)} %param.9) | copy-start | bytes 3145732
  13.7 18.6 %all-to-all-start = ((bf16[2,32,4096]{2,0,1:T(2,128)(2,1)}), bf16[2,32,4096]{2,0,1:T(2,128)(2,1)S(1)}, u32[]{:S(2)}, u32[]{:S(2)}) async-start(bf16[2,32,4096]{2,0,1:T(2,128)(2,1)} %copy.28), calls=%async_computation | async-start | bytes 1048576 | tf_op jit(solution)/shard_map/all_to_all | solution.py:146
  20.8 79.9 %all-gather.5.cloned.1.call-start = ((), (), s32[]{:S(2)}) async-start(), calls=%async_computation.8 | async-start | bytes 4718592 | tf_op jit(solution)/shard_map/all_gather | solution.py:83
  32.6 10.2 %copy-start.2 = (bf16[128,4096]{1,0:T(8,128)(2,1)S(1)}, bf16[128,4096]{1,0:T(8,128)(2,1)}, u32[]{:S(2)}) copy-start(bf16[128,4096]{1,0:T(8,128)(2,1)} %param.15) | copy-start | bytes 3145732
  42.6 124.4 %all-gather.7.cloned.1.call-start = ((), (), s32[]{:S(2)}) async-start(), calls=%async_computation.9 | async-start | bytes 4718592 | tf_op jit(solution)/shard_map/all_gather | solution.py:83
  86.8 16.6 %copy-start.5 = (bf16[1,2048,256]{2,1,0:T(8,128)(2,1)S(1)}, bf16[1,2048,256]{2,1,0:T(8,128)(2,1)}, u32[]{:S(2)}) copy-start(bf16[1,2048,256]{2,1,0:T(8,128)(2,1)} %param.13) | copy-start | bytes 3145732
  86.8 145.4 %reduce-scatter.3.cloned.1.call-start = ((), (), s32[]{:S(2)}) async-start(), calls=%async_computation.6 | async-start | bytes 4718592 | tf_op jit(solution)/shard_map/reduce_scatter | solution.py:119
  103.4 2.8 copy-start.14
  103.4 2.8 copy-start.12
  103.4 2.0 copy-start.4
  105.5 1.5 copy-start.6
  106.2 0.8 copy-start.7
  107.0 0.8 copy-start.10
  162.1 1.5 copy-start.22
  162.1 1.5 copy-start.26
  166.7 128.4 %reduce-scatter.5.cloned.1.call-start = ((), (), s32[]{:S(2)}) async-start(), calls=%async_computation.7 | async-start | bytes 4718592 | tf_op jit(solution)/shard_map/reduce_scatter | solution.py:119
  169.7 1.5 copy-start.16
  169.7 1.9 copy-start.18
  170.5 1.9 copy-start.8
  171.2 1.2 copy-start.9
  172.4 0.8 copy-start.11
  210.5 1.5 copy-start.20
  210.5 1.5 copy-start.24
  210.5 1.5 copy-start.28
  215.2 0.7 copy-start.30
  215.2 0.8 copy-start.31
  215.2 1.7 copy-start.15
  215.2 1.7 copy-start.23
  216.9 1.0 copy-start.27
  217.8 1.6 copy-start.13
  219.5 1.6 copy-start.19
  219.5 1.6 copy-start.21
  221.1 1.6 copy-start.17
  221.1 1.6 copy-start.29
  222.7 1.0 copy-start.25
  246.5 59.8 %all-to-all-start.1 = ((bf16[2,32,4096]{2,0,1:T(2,128)(2,1)}), bf16[2,32,4096]{2,0,1:T(2,128)(2,1)}, u32[]{:S(2)}, u32[]{:S(2)}) async-start(bf16[2,32,4096]{2,0,1:T(2,128)(2,1)} %copy.31), calls=%async_computation.2 | async-start | bytes 1048576 | tf_op jit(solution)/shard_map/all_to_all | solution.py:156
  306.3 18.1 %all-to-all-start.3 = ((bf16[2,32,4096]{2,0,1:T(2,128)(2,1)}), bf16[2,32,4096]{2,0,1:T(2,128)(2,1)}, u32[]{:S(2)}, u32[]{:S(2)}) async-start(bf16[2,32,4096]{2,0,1:T(2,128)(2,1)} %copy.37), calls=%async_computation.5 | async-start | bytes 1048576 | tf_op jit(solution)/shard_map/all_to_all | solution.py:156
  338.4 4.3 %copy-start.1 = (bf16[1,2048,256]{2,1,0:T(8,128)(2,1)S(1)}, bf16[1,2048,256]{2,1,0:T(8,128)(2,1)}, u32[]{:S(2)}) copy-start(bf16[1,2048,256]{2,1,0:T(8,128)(2,1)} %param.14) | copy-start | bytes 3145732
Sparse Core Ops, SparseCore 0:
  42.7 57.9 all-gather.4
  103.1 58.7 all-gather.6
  166.8 65.4 reduce-scatter.2
  234.7 60.3 reduce-scatter.4
